TPU v7x, 32 devices: a whole 2x2x4 slice. The times are simulated.
32 devices in a mesh: slab: 8 (over z, y), row: 4 (over x, core).
Axes of the slice: x: 2, y: 2, z: 4, core: 2. Of those that a mesh axis runs over, the one named last changes fastest.
Arguments:
- queries: bfloat16 [8192, 32, 128], P('slab', 'row'), may hold values from -72 to 72, as said below
- keys: bfloat16 [8192, 32, 128], P('slab', 'row'), may hold values from -4 to 4
- values: bfloat16 [8192, 32, 128], P('slab', 'row'), may hold values from -6 to 6
- out_grad: bfloat16 [8192, 32, 128], P(('slab', 'row')), may hold values from -6 to 6
- col_start: int32 [64], replicated, may hold values from 0 to 2, as said below
- valid_tiles: int32 [8], replicated, may hold values from 4 to 8, as said below
Outputs:
- query_grad: bfloat16 [8192, 32, 128], P(('slab', 'row'))
- key_grad: bfloat16 [8192, 32, 128], P(('slab', 'row'))
- value_grad: bfloat16 [8192, 32, 128], P(('slab', 'row'))
Inputs may be any that keep to these rules, and one draw needn't show every extreme that they name: `queries`: of order one in most rows. For query tile a with tile column w = (a % 8) % 4, col_start[a] is w - 1 or w, kept within 0 to 2. The tiles of a slab with index below valid_tiles hold real keys, the others padding; the values 4 and 8 occur in every draw.
All inputs are finite; a program needn't handle non-finite values.
Results may differ from a plain program's by a relative error of at most 0.0095.
Values may be sent and summed in bfloat16 or wider, within the bound.
No kernel may reach another device: no remote copies, remote signals or barrier semaphores. Data moves between devices by JAX's collectives and lax.ppermute only.
A program may use at most 256 MiB of HBM per device.

v0:
```python
import math

import jax
import jax.numpy as jnp
from jax import lax
from jax.experimental import pallas as pl
from jax.experimental.pallas import tpu as pltpu
from jax.sharding import PartitionSpec as P


TILE = 128
GH = 2
GW = 4
WIN_COLS = 2
TPS = GH * GW
SPAN = WIN_COLS * TILE
NEG = -1e30


def attention_kernel(
    scalars,
    q_keep,
    q_recv,
    do_ref,
    kv_low,
    kv_keep,
    kv_recv,
    kv_high,
    dq_keep,
    dq_recv,
    own_keep,
    own_recv,
    half_low,
    half_high,
    q_buf,
    do_buf,
    k_buf,
    v_buf,
    kt_buf,
    dk_acc,
    dv_acc,
    p_buf,
    dp_buf,
):
    tok, head_dim = q_keep.shape
    scale = head_dim ** (-0.5)
    parity = scalars[2 * TPS + 4]

    q_buf[pl.ds(0, tok), :] = q_keep[...]
    q_buf[pl.ds(tok, tok), :] = q_recv[...]
    senders, _, part, _ = do_ref.shape
    for sender in range(senders):
        do_buf[pl.ds(sender * part, part), :] = do_ref[sender, 0]
    for slot, ref in enumerate((kv_low, kv_keep, kv_recv, kv_high)):
        k_buf[pl.ds(slot * tok, tok), :] = ref[0]
        v_buf[pl.ds(slot * tok, tok), :] = ref[1]
        kt_buf[:, pl.ds(slot * tok, tok)] = ref[0].T
    dk_acc[...] = jnp.zeros_like(dk_acc)
    dv_acc[...] = jnp.zeros_like(dv_acc)

    def unit(side, col, q_starts):
        width = TILE * len(q_starts)
        turn = ((side + parity) % 2 - side) * tok

        def rows_of(buf, shift):
            parts = [
                buf[pl.ds(pl.multiple_of(start + shift, TILE), TILE), :] for start in q_starts
            ]
            return parts[0] if len(parts) == 1 else jnp.concatenate(parts, axis=0)

        q = rows_of(q_buf, 0)
        do = rows_of(do_buf, turn)
        blocks = 3 * GH
        offsets = []
        limits = []
        for block in range(blocks):
            step, grid_row = block // GH, block % GH
            offset = (side + step) * tok + grid_row * GW * TILE + col * TILE
            offsets.append(pl.multiple_of(offset, TILE))
            count = scalars[2 * TPS + side + step]
            limits.append((count - grid_row * GW - col) * TILE)
        key_row = lax.broadcasted_iota(jnp.int32, (SPAN, width), 0)
        top = jnp.full((8, width), NEG, jnp.float32)
        for block in range(blocks):
            scores = lax.dot_general(
                k_buf[pl.ds(offsets[block], SPAN), :],
                q,
                (((1,), (1,)), ((), ())),
                preferred_element_type=jnp.float32,
            )
            scores = jnp.where(key_row < limits[block], scores, NEG)
            p_buf[pl.ds(block * SPAN, SPAN), pl.ds(0, width)] = scores
            top = jnp.maximum(top, jnp.max(scores.reshape(SPAN // 8, 8, width), axis=0))
        top = jnp.max(top, axis=0, keepdims=True)
        total = jnp.zeros((8, width), jnp.float32)
        delta = jnp.zeros((8, width), jnp.float32)
        for block in range(blocks):
            here = pl.ds(block * SPAN, SPAN), pl.ds(0, width)
            expo = jnp.exp2((p_buf[here] - top) * (scale * math.log2(math.e)))
            grad = lax.dot_general(
                v_buf[pl.ds(offsets[block], SPAN), :],
                do,
                (((1,), (1,)), ((), ())),
                preferred_element_type=jnp.float32,
            )
            p_buf[here] = expo
            dp_buf[here] = grad
            total += jnp.sum(expo.reshape(SPAN // 8, 8, width), axis=0)
            delta += jnp.sum((expo * grad).reshape(SPAN // 8, 8, width), axis=0)
        inverse = 1.0 / jnp.sum(total, axis=0, keepdims=True)
        delta = jnp.sum(delta, axis=0, keepdims=True) * inverse
        dq_t = jnp.zeros((head_dim, width), jnp.float32)
        for block in range(blocks):
            here = pl.ds(block * SPAN, SPAN), pl.ds(0, width)
            keys_here = pl.ds(offsets[block], SPAN)
            attend = p_buf[here] * inverse
            grad_scores = (attend * (dp_buf[here] - delta)).astype(jnp.bfloat16)
            attend_b = attend.astype(jnp.bfloat16)
            dv_acc[keys_here, :] += jnp.dot(attend_b, do, preferred_element_type=jnp.float32)
            dk_acc[keys_here, :] += jnp.dot(grad_scores, q, preferred_element_type=jnp.float32)
            dq_t += jnp.dot(kt_buf[:, keys_here], grad_scores, preferred_element_type=jnp.float32)
        dq = (dq_t * scale).T.astype(jnp.bfloat16)
        for place, start in enumerate(q_starts):
            q_buf[pl.ds(start, TILE), :] = dq[place * TILE : (place + 1) * TILE]

    def step(index, carry):
        side = index // GW
        column = index % GW
        first = scalars[side * TPS + column]
        second = scalars[side * TPS + GW + column]
        start0 = pl.multiple_of(side * tok + column * TILE, TILE)
        start1 = pl.multiple_of(side * tok + (GW + column) * TILE, TILE)

        @pl.when(first == second)
        def _():
            unit(side, first, [start0, start1])

        @pl.when(first != second)
        def _():
            def single(which, inner):
                start = pl.multiple_of(start0 + which * (GW * TILE), TILE)
                unit(side, jnp.where(which == 0, first, second), [start])
                return inner

            lax.fori_loop(0, GH, single, 0)

        return carry

    lax.fori_loop(0, 2 * GW, step, 0)
    dq_keep[...] = q_buf[pl.ds(0, tok), :]
    dq_recv[...] = q_buf[pl.ds(tok, tok), :]
    for place, (acc, factor) in enumerate(((dk_acc, scale), (dv_acc, None))):
        for slot, ref in enumerate((half_low, own_keep, own_recv, half_high)):
            part_sum = acc[pl.ds(slot * tok, tok), :]
            if factor is not None:
                part_sum = part_sum * factor
            ref[place] = part_sum.astype(ref.dtype)


def attention_call(scalars, chunk, q_keep, q_recv, do_all, kv_low, kv_keep, kv_recv, kv_high):
    tok, head_dim = q_keep.shape
    senders, _, part, _ = do_all.shape
    whole = pl.BlockSpec((tok, head_dim), lambda i: (0, 0))
    pair = pl.BlockSpec((2, tok, head_dim), lambda i: (0, 0, 0))
    do_spec = pl.BlockSpec((senders, 1, part, head_dim), lambda i: (0, chunk, 0, 0))
    keys_all = 4 * tok
    window = 3 * GH * SPAN
    pairs = 2 * TPS * TILE * window
    return pl.pallas_call(
        attention_kernel,
        grid=(1,),
        out_shape=(jax.ShapeDtypeStruct((tok, head_dim), jnp.bfloat16),) * 2
        + (jax.ShapeDtypeStruct((2, tok, head_dim), jnp.float32),) * 2
        + (jax.ShapeDtypeStruct((2, tok, head_dim), jnp.bfloat16),) * 2,
        in_specs=[pl.BlockSpec(memory_space=pltpu.SMEM), whole, whole, do_spec] + [pair] * 4,
        out_specs=(whole,) * 2 + (pair,) * 4,
        scratch_shapes=[
            pltpu.VMEM((2 * tok, head_dim), jnp.bfloat16),
            pltpu.VMEM((2 * tok, head_dim), jnp.bfloat16),
            pltpu.VMEM((keys_all, head_dim), jnp.bfloat16),
            pltpu.VMEM((keys_all, head_dim), jnp.bfloat16),
            pltpu.VMEM((head_dim, keys_all), jnp.bfloat16),
            pltpu.VMEM((keys_all, head_dim), jnp.float32),
            pltpu.VMEM((keys_all, head_dim), jnp.float32),
            pltpu.VMEM((window, GH * TILE), jnp.float32),
            pltpu.VMEM((window, GH * TILE), jnp.float32),
        ],
        cost_estimate=pl.CostEstimate(
            flops=10 * pairs * head_dim, transcendentals=pairs, bytes_accessed=16 * tok * head_dim * 2
        ),
        name="window_grads",
    )(scalars, q_keep, q_recv, do_all, kv_low, kv_keep, kv_recv, kv_high)


def split_kernel(scalars, *refs):
    (first, second), outs, held = refs[:2], refs[2:-1], refs[-1]
    chunks = len(outs) // 2
    side = scalars[0]
    for place, ref in enumerate((first, second)):
        held[...] = jnp.swapaxes(ref[...], 0, 1)
        for chunk in range(chunks):
            outs[chunk][place] = held[(1 - side) * chunks + chunk]
            outs[chunks + chunk][place] = held[side * chunks + chunk]


def split_pair(scalars, first, second):
    tok, heads_here, head_dim = first.shape
    steps = TPS
    block = tok // steps
    chunks = heads_here // 2
    spec = pl.BlockSpec((block, heads_here, head_dim), lambda i: (i, 0, 0))
    out_spec = pl.BlockSpec((2, block, head_dim), lambda i: (0, i, 0))
    outs = pl.pallas_call(
        split_kernel,
        grid=(steps,),
        out_shape=(jax.ShapeDtypeStruct((2, tok, head_dim), first.dtype),) * (2 * chunks),
        in_specs=[pl.BlockSpec(memory_space=pltpu.SMEM), spec, spec],
        out_specs=(out_spec,) * (2 * chunks),
        scratch_shapes=[pltpu.VMEM((heads_here, block, head_dim), first.dtype)],
        name="split_pair",
    )(scalars, first, second)
    return outs[:chunks], outs[chunks:]


def spread_kernel(scalars, queries, out_grad, *refs):
    outs, do_out, held_q, held_do = refs[:-3], refs[-3], refs[-2], refs[-1]
    side = scalars[0]
    heads_here = held_q.shape[0]
    chunks = heads_here // 2
    row_count = held_do.shape[0] // heads_here
    held_q[...] = jnp.swapaxes(queries[...], 0, 1)
    for chunk in range(chunks):
        outs[chunk][...] = held_q[(1 - side) * chunks + chunk]
        outs[chunks + chunk][...] = held_q[side * chunks + chunk]
    held_do[...] = jnp.swapaxes(out_grad[...], 0, 1)
    for group in range(2):
        for row in range(row_count):
            head = row * heads_here + group * chunks
            do_out[group * row_count + row] = held_do[head : head + chunks]


def spread(scalars, queries, out_grad):
    tok, heads_here, head_dim = queries.shape
    part, heads, _ = out_grad.shape
    steps = min(TPS, part // 16)
    chunks = heads_here // 2
    targets = 2 * heads // heads_here
    outs = pl.pallas_call(
        spread_kernel,
        grid=(steps,),
        out_shape=(jax.ShapeDtypeStruct((tok, head_dim), queries.dtype),) * (2 * chunks)
        + (jax.ShapeDtypeStruct((targets, chunks, part, head_dim), queries.dtype),),
        in_specs=[
            pl.BlockSpec(memory_space=pltpu.SMEM),
            pl.BlockSpec((tok // steps, heads_here, head_dim), lambda i: (i, 0, 0)),
            pl.BlockSpec((part // steps, heads, head_dim), lambda i: (i, 0, 0)),
        ],
        out_specs=(pl.BlockSpec((tok // steps, head_dim), lambda i: (i, 0)),) * (2 * chunks)
        + (pl.BlockSpec((targets, chunks, part // steps, head_dim), lambda i: (0, 0, i, 0)),),
        scratch_shapes=[
            pltpu.VMEM((heads_here, tok // steps, head_dim), queries.dtype),
            pltpu.VMEM((heads, part // steps, head_dim), queries.dtype),
        ],
        name="spread",
    )(scalars, queries, out_grad)
    return outs[:chunks], outs[chunks : 2 * chunks], outs[-1]


def merge_kernel(scalars, dq_keep, dq_recv, own_keep, own_recv, add_keep, add_recv, out):
    targets, _, part, _ = out.shape
    row_count = targets // 2
    side = scalars[0]
    groups = ((dq_keep, own_keep, add_keep, side), (dq_recv, own_recv, add_recv, 1 - side))
    for grad, own, add, place in groups:
        for row in range(row_count):
            rows = pl.ds(row * part, part)
            target = place * row_count + row
            out[target, 0] = grad[rows, :]
            for which in range(2):
                total = own[which, rows, :] + add[which, rows, :].astype(jnp.float32)
                out[target, 1 + which] = total.astype(out.dtype)


def merge(scalars, row_count, dq_keep, dq_recv, own_keep, own_recv, add_keep, add_recv):
    tok, head_dim = dq_keep.shape
    vmem = pl.BlockSpec(memory_space=pltpu.VMEM)
    return pl.pallas_call(
        merge_kernel,
        out_shape=jax.ShapeDtypeStruct((2 * row_count, 3, tok // row_count, head_dim), jnp.bfloat16),
        in_specs=[pl.BlockSpec(memory_space=pltpu.SMEM)] + [vmem] * 6,
        out_specs=vmem,
        name="merge",
    )(scalars, dq_keep, dq_recv, own_keep, own_recv, add_keep, add_recv)


def assemble_kernel(*refs):
    chunks = len(refs) - 4
    pieces, outs, held = refs[:chunks], refs[chunks:-1], refs[-1]
    senders = pieces[0].shape[0]
    for plane in range(3):
        for chunk in range(chunks):
            for group in range(2):
                for row in range(senders // 2):
                    head = row * 2 * chunks + group * chunks + chunk
                    held[head] = pieces[chunk][group * (senders // 2) + row, plane]
        outs[plane][...] = jnp.swapaxes(held[...], 0, 1)


def assemble(pieces):
    chunks = len(pieces)
    senders, _, part, head_dim = pieces[0].shape
    heads = chunks * senders
    steps = min(TPS, part // 16)
    block = part // steps
    return pl.pallas_call(
        assemble_kernel,
        grid=(steps,),
        out_shape=(jax.ShapeDtypeStruct((part, heads, head_dim), jnp.bfloat16),) * 3,
        in_specs=[pl.BlockSpec((senders, 3, block, head_dim), lambda i: (0, 0, i, 0))] * chunks,
        out_specs=(pl.BlockSpec((block, heads, head_dim), lambda i: (i, 0, 0)),) * 3,
        scratch_shapes=[pltpu.VMEM((heads, block, head_dim), jnp.bfloat16)],
        name="assemble",
    )(*pieces)


def on_device(mesh_shape, queries, keys, values, out_grad, col_start, valid_tiles):
    _, heads_here, _ = queries.shape
    row_count = mesh_shape["row"]
    slab_total = mesh_shape["slab"]
    chunks = heads_here // 2
    slab_pos = lax.axis_index("slab")
    parity = slab_pos % 2
    partner = slab_pos + 1 - 2 * parity

    swap = [(s, s ^ 1) for s in range(slab_total)]
    out_high = [(s, s - 2 if s % 2 == 0 else s + 2) for s in range(slab_total)]
    out_high = [(s, t) for s, t in out_high if 0 <= t < slab_total]
    out_low = [(s, s + 2 if s % 2 == 0 else s - 2) for s in range(slab_total)]
    out_low = [(s, t) for s, t in out_low if 0 <= t < slab_total]

    def turned(pairs):
        return [(t, s) for s, t in pairs]

    def over_slab(array, pairs):
        return lax.ppermute(array, "slab", pairs)

    groups = [
        list(range(first, first + 2 * row_count))
        for first in range(0, slab_total * row_count, 2 * row_count)
    ]

    def to_all(array):
        return lax.all_to_all(
            array, ("slab", "row"), 0, 0, axis_index_groups=groups, tiled=True
        )

    slab_ids = jnp.stack(
        [
            jnp.where(parity == 0, slab_pos - 1, slab_pos + 1),
            slab_pos,
            partner,
            jnp.where(parity == 0, slab_pos + 2, slab_pos - 2),
        ]
    )
    inside = (slab_ids >= 0) & (slab_ids < slab_total)
    counts = jnp.where(inside, valid_tiles[jnp.clip(slab_ids, 0, slab_total - 1)], 0)
    places = parity.reshape(1)
    scalars = jnp.concatenate(
        [
            lax.dynamic_slice_in_dim(col_start, slab_pos * TPS, TPS, 0),
            lax.dynamic_slice_in_dim(col_start, partner * TPS, TPS, 0),
            counts.astype(jnp.int32),
            places,
        ]
    )

    kv_sent, kv_keep = split_pair(places, keys, values)
    q_sent, q_keep, do_sent = spread(places, queries, out_grad)
    do_all = to_all(do_sent)
    inputs = []
    for chunk in range(chunks):
        kv_recv = over_slab(kv_sent[chunk], swap)
        kv_high = over_slab(kv_keep[chunk], out_high)
        kv_low = over_slab(kv_recv, out_low)
        q_recv = over_slab(q_sent[chunk], swap)
        inputs.append((q_keep[chunk], q_recv, do_all, kv_low, kv_keep[chunk], kv_recv, kv_high))

    pieces = []
    for chunk in range(chunks):
        dq_keep, dq_recv, own_keep, own_recv, half_low, half_high = attention_call(
            scalars, chunk, *inputs[chunk]
        )
        add_keep = over_slab(half_high, turned(out_high))
        add_recv = over_slab(half_low, turned(out_low))
        merged = merge(places, row_count, dq_keep, dq_recv, own_keep, own_recv, add_keep, add_recv)
        pieces.append(to_all(merged))
    return tuple(assemble(pieces))


def solution(mesh):
    placed = (
        P("slab", "row", None),
        P("slab", "row", None),
        P("slab", "row", None),
        P(("slab", "row"), None, None),
        P(),
        P(),
    )

    def body(*operands):
        return on_device(dict(mesh.shape), *operands)

    return jax.shard_map(
        body,
        mesh=mesh,
        in_specs=placed,
        out_specs=(P(("slab", "row"), None, None),) * 3,
        check_vma=False,
    )
```

profile of v0, /device:TPU:24, one launch (start us, length us, event | category | flops | bytes accessed | tf_op | source)
XLA Modules:
  0.0 357.9 jit_solution(6449620486597765908)
XLA Ops:
  0.7 6.7 %spread.1 = (bf16[1024,128]{1,0:T(8,128)(2,1)}, bf16[1024,128]{1,0:T(8,128)(2,1)}, bf16[1024,128]{1,0:T(8,128)(2,1)}, bf16[1024,128]{1,0:T(8,128)(2,1)}, bf16[10...) custom-call(s32[1]{0:T(128)} %bitcast.scalars, ...), custom_call_target="tpu_custom_call" | custom-call | tf_op jit(solution)/shard_map/spread/pallas_call | solution.py:248
  7.4 3.7 %all-to-all-start = ((bf16[8,4,256,128]{3,2,1,0:T(8,128)(2,1)}), bf16[8,4,256,128]{3,2,1,0:T(8,128)(2,1)S(1)}, u32[]{:S(2)}, u32[]{:S(2)}) async-start(bf16[8,4,256,128]{3,2,1,0:T(8,128)(2,1)} %get-tuple-element.46), calls=%async_computation | async-start | bytes 4194304 | tf_op jit(solution)/shard_map/all_to_all | solution.py:353
  11.1 7.0 %split_pair.1 = (bf16[2,1024,128]{2,1,0:T(8,128)(2,1)}, bf16[2,1024,128]{2,1,0:T(8,128)(2,1)}, bf16[2,1024,128]{2,1,0:T(8,128)(2,1)}, bf16[2,1024,128]{2,1,0:T(8...) custom-call(s32[1]{0:T(128)} %bitcast.scalars, ...), custom_call_target="tpu_custom_call" | custom-call | tf_op jit(solution)/shard_map/split_pair/pallas_call | solution.py:213
  20.2 3.2 collective-permute-start.21
  25.5 23.1 %collective-permute-done.19.kv_recv = bf16[2,1024,128]{2,1,0:T(8,128)(2,1)S(1)} collective-permute-done((bf16[2,1024,128]{2,1,0:T(8,128)(2,1)}, bf16[2,1024,128]{2,1,0:T(8,128)(2,1)S(1)}, u32[]{:S(2)}, u32[]{:S(2)}) %collective-permute-start.19) | collective-permute-done | bytes 524320 | tf_op jit(solution)/shard_map/ppermute | solution.py:345
  54.2 9.2 %collective-permute-done.20.kv_low = bf16[2,1024,128]{2,1,0:T(8,128)(2,1)} collective-permute-done((bf16[2,1024,128]{2,1,0:T(8,128)(2,1)S(1)}, bf16[2,1024,128]{2,1,0:T(8,128)(2,1)}, u32[]{:S(2)}, u32[]{:S(2)}) %collective-permute-start.20) | collective-permute-done | bytes 524320 | tf_op jit(solution)/shard_map/ppermute | solution.py:345
  64.7 19.2 %window_grads.7 = (bf16[1024,128]{1,0:T(8,128)(2,1)}, bf16[1024,128]{1,0:T(8,128)(2,1)}, f32[2,1024,128]{2,1,0:T(8,128)}, f32[2,1024,128]{2,1,0:T(8,128)}, bf16[...) custom-call(s32[21]{0:T(128)} %pad_add_fusion.scalars, bf16[1024,128]{1,0:T(8,128)(2,1)} %get-tuple-element.75.q_keep, ...), custom_call_target="tpu_custom_call" | custom-call | flops 4026531840 | bytes 4194304 | tf_op jit(solution)/shard_map/window_grads/pallas_call | solution.py:169
  85.2 4.6 %collective-permute-start.23 = (bf16[2,1024,128]{2,1,0:T(8,128)(2,1)}, bf16[2,1024,128]{2,1,0:T(8,128)(2,1)S(1)}, u32[]{:S(2)}, u32[]{:S(2)}) collective-permute-start(bf16[2,1024,128]{2,1,0:T(8,128)(2,1)} %get-tuple-element.84), channel_id=1, source_target_pairs={{8,0},{16,8},{4,12},{24,16},{12,20},{20,28},{9,1},{17,9},{5,13},{2... | collective-permute-start | bytes 1572872 | tf_op jit(solution)/shard_map/ppermute | solution.py:345
  93.0 7.8 %collective-permute-done.22.add_keep = bf16[2,1024,128]{2,1,0:T(8,128)(2,1)S(1)} collective-permute-done((bf16[2,1024,128]{2,1,0:T(8,128)(2,1)}, bf16[2,1024,128]{2,1,0:T(8,128)(2,1)S(1)}, u32[]{:S(2)}, u32[]{:S(2)}) %collective-permute-start.22) | collective-permute-done | bytes 524320 | tf_op jit(solution)/shard_map/ppermute | solution.py:345
  103.1 3.3 merge.7
  106.5 3.7 %all-to-all-start.4 = ((bf16[8,3,256,128]{3,2,1,0:T(8,128)(2,1)}), bf16[8,3,256,128]{3,2,1,0:T(8,128)(2,1)S(1)}, u32[]{:S(2)}, u32[]{:S(2)}) async-start(bf16[8,3,256,128]{3,2,1,0:T(8,128)(2,1)} %merge.7), calls=%async_computation.4 | async-start | bytes 3145728 | tf_op jit(solution)/shard_map/all_to_all | solution.py:353
  112.3 24.0 %collective-permute-done.12.q_recv = bf16[1024,128]{1,0:T(8,128)(2,1)S(1)} collective-permute-done((bf16[1024,128]{1,0:T(8,128)(2,1)S(1)}, bf16[1024,128]{1,0:T(8,128)(2,1)S(1)}, u32[]{:S(2)}, u32[]{:S(2)}) %collective-permute-start.12) | collective-permute-done | bytes 262176 | tf_op jit(solution)/shard_map/ppermute | solution.py:345
  137.8 19.3 %window_grads.6 = (bf16[1024,128]{1,0:T(8,128)(2,1)}, bf16[1024,128]{1,0:T(8,128)(2,1)}, f32[2,1024,128]{2,1,0:T(8,128)}, f32[2,1024,128]{2,1,0:T(8,128)}, bf16[...) custom-call(s32[21]{0:T(128)} %pad_add_fusion.scalars, bf16[1024,128]{1,0:T(8,128)(2,1)} %get-tuple-element.65.q_keep, ...), custom_call_target="tpu_custom_call" | custom-call | flops 4026531840 | bytes 4194304 | tf_op jit(solution)/shard_map/window_grads/pallas_call | solution.py:169
  158.4 4.6 %collective-permute-start.17 = (bf16[2,1024,128]{2,1,0:T(8,128)(2,1)}, bf16[2,1024,128]{2,1,0:T(8,128)(2,1)S(1)}, u32[]{:S(2)}, u32[]{:S(2)}) collective-permute-start(bf16[2,1024,128]{2,1,0:T(8,128)(2,1)} %get-tuple-element.74), channel_id=1, source_target_pairs={{8,0},{16,8},{4,12},{24,16},{12,20},{20,28},{9,1},{17,9},{5,13},{2... | collective-permute-start | bytes 1572872 | tf_op jit(solution)/shard_map/ppermute | solution.py:345
  163.0 4.5 %collective-permute-start.9 = (bf16[2,1024,128]{2,1,0:T(8,128)(2,1)}, bf16[2,1024,128]{2,1,0:T(8,128)(2,1)}, u32[]{:S(2)}, u32[]{:S(2)}) collective-permute-start(bf16[2,1024,128]{2,1,0:T(8,128)(2,1)} %get-tuple-element.58.kv_keep), channel_id=1, source_target_pairs={{4,12},{8,0},{12,20},{16,8},{20,28},{24,16},{5,13},{9,1},{13,21},{... | collective-permute-start | bytes 1572872 | tf_op jit(solution)/shard_map/ppermute | solution.py:345
  168.7 5.0 %collective-permute-done.16.add_keep = bf16[2,1024,128]{2,1,0:T(8,128)(2,1)S(1)} collective-permute-done((bf16[2,1024,128]{2,1,0:T(8,128)(2,1)}, bf16[2,1024,128]{2,1,0:T(8,128)(2,1)S(1)}, u32[]{:S(2)}, u32[]{:S(2)}) %collective-permute-start.16) | collective-permute-done | bytes 524320 | tf_op jit(solution)/shard_map/ppermute | solution.py:345
  176.3 3.3 merge.6
  179.7 4.3 %all-to-all-start.3 = ((bf16[8,3,256,128]{3,2,1,0:T(8,128)(2,1)}), bf16[8,3,256,128]{3,2,1,0:T(8,128)(2,1)S(1)}, u32[]{:S(2)}, u32[]{:S(2)}) async-start(bf16[8,3,256,128]{3,2,1,0:T(8,128)(2,1)} %merge.6), calls=%async_computation.3 | async-start | bytes 3145728 | tf_op jit(solution)/shard_map/all_to_all | solution.py:353
  186.1 24.1 %collective-permute-done.6.q_recv = bf16[1024,128]{1,0:T(8,128)(2,1)S(1)} collective-permute-done((bf16[1024,128]{1,0:T(8,128)(2,1)S(1)}, bf16[1024,128]{1,0:T(8,128)(2,1)S(1)}, u32[]{:S(2)}, u32[]{:S(2)}) %collective-permute-start.6) | collective-permute-done | bytes 262176 | tf_op jit(solution)/shard_map/ppermute | solution.py:345
  210.9 19.2 %window_grads.5 = (bf16[1024,128]{1,0:T(8,128)(2,1)}, bf16[1024,128]{1,0:T(8,128)(2,1)}, f32[2,1024,128]{2,1,0:T(8,128)}, f32[2,1024,128]{2,1,0:T(8,128)}, bf16[...) custom-call(s32[21]{0:T(128)} %pad_add_fusion.scalars, bf16[1024,128]{1,0:T(8,128)(2,1)} %get-tuple-element.55.q_keep, ...), custom_call_target="tpu_custom_call" | custom-call | flops 4026531840 | bytes 4194304 | tf_op jit(solution)/shard_map/window_grads/pallas_call | solution.py:169
  231.4 4.6 %collective-permute-start.11 = (bf16[2,1024,128]{2,1,0:T(8,128)(2,1)}, bf16[2,1024,128]{2,1,0:T(8,128)(2,1)S(1)}, u32[]{:S(2)}, u32[]{:S(2)}) collective-permute-start(bf16[2,1024,128]{2,1,0:T(8,128)(2,1)} %get-tuple-element.64), channel_id=1, source_target_pairs={{8,0},{16,8},{4,12},{24,16},{12,20},{20,28},{9,1},{17,9},{5,13},{2... | collective-permute-start | bytes 1572872 | tf_op jit(solution)/shard_map/ppermute | solution.py:345
  236.0 4.1 %collective-permute-start.3 = (bf16[2,1024,128]{2,1,0:T(8,128)(2,1)}, bf16[2,1024,128]{2,1,0:T(8,128)(2,1)}, u32[]{:S(2)}, u32[]{:S(2)}) collective-permute-start(bf16[2,1024,128]{2,1,0:T(8,128)(2,1)} %get-tuple-element.48.kv_keep), channel_id=1, source_target_pairs={{4,12},{8,0},{12,20},{16,8},{20,28},{24,16},{5,13},{9,1},{13,21},{... | collective-permute-start | bytes 1572872 | tf_op jit(solution)/shard_map/ppermute | solution.py:345
  241.4 5.3 %collective-permute-done.10.add_keep = bf16[2,1024,128]{2,1,0:T(8,128)(2,1)S(1)} collective-permute-done((bf16[2,1024,128]{2,1,0:T(8,128)(2,1)}, bf16[2,1024,128]{2,1,0:T(8,128)(2,1)S(1)}, u32[]{:S(2)}, u32[]{:S(2)}) %collective-permute-start.10) | collective-permute-done | bytes 524320 | tf_op jit(solution)/shard_map/ppermute | solution.py:345
  249.3 3.3 merge.5
  252.7 4.0 %all-to-all-start.2 = ((bf16[8,3,256,128]{3,2,1,0:T(8,128)(2,1)}), bf16[8,3,256,128]{3,2,1,0:T(8,128)(2,1)S(1)}, u32[]{:S(2)}, u32[]{:S(2)}) async-start(bf16[8,3,256,128]{3,2,1,0:T(8,128)(2,1)} %merge.5), calls=%async_computation.2 | async-start | bytes 3145728 | tf_op jit(solution)/shard_map/all_to_all | solution.py:353
  258.7 23.6 %collective-permute-done.q_recv = bf16[1024,128]{1,0:T(8,128)(2,1)S(1)} collective-permute-done((bf16[1024,128]{1,0:T(8,128)(2,1)S(1)}, bf16[1024,128]{1,0:T(8,128)(2,1)S(1)}, u32[]{:S(2)}, u32[]{:S(2)}) %collective-permute-start) | collective-permute-done | bytes 262176 | tf_op jit(solution)/shard_map/ppermute | solution.py:345
  283.0 19.2 %window_grads.4 = (bf16[1024,128]{1,0:T(8,128)(2,1)}, bf16[1024,128]{1,0:T(8,128)(2,1)}, f32[2,1024,128]{2,1,0:T(8,128)}, f32[2,1024,128]{2,1,0:T(8,128)}, bf16[...) custom-call(s32[21]{0:T(128)} %pad_add_fusion.scalars, bf16[1024,128]{1,0:T(8,128)(2,1)} %get-tuple-element.44.q_keep, ...), custom_call_target="tpu_custom_call" | custom-call | flops 4026531840 | bytes 4194304 | tf_op jit(solution)/shard_map/window_grads/pallas_call | solution.py:169
  303.5 4.6 %collective-permute-start.5 = (bf16[2,1024,128]{2,1,0:T(8,128)(2,1)}, bf16[2,1024,128]{2,1,0:T(8,128)(2,1)S(1)}, u32[]{:S(2)}, u32[]{:S(2)}) collective-permute-start(bf16[2,1024,128]{2,1,0:T(8,128)(2,1)} %get-tuple-element.54), channel_id=1, source_target_pairs={{8,0},{16,8},{4,12},{24,16},{12,20},{20,28},{9,1},{17,9},{5,13},{2... | collective-permute-start | bytes 1572872 | tf_op jit(solution)/shard_map/ppermute | solution.py:345
  308.1 9.6 %collective-permute-done.4.add_keep = bf16[2,1024,128]{2,1,0:T(8,128)(2,1)S(1)} collective-permute-done((bf16[2,1024,128]{2,1,0:T(8,128)(2,1)}, bf16[2,1024,128]{2,1,0:T(8,128)(2,1)S(1)}, u32[]{:S(2)}, u32[]{:S(2)}) %collective-permute-start.4) | collective-permute-done | bytes 524320 | tf_op jit(solution)/shard_map/ppermute | solution.py:345
  319.7 3.3 merge.4
  323.1 26.2 %all_to_all.25.refs_0_ = bf16[8,3,256,128]{3,2,1,0:T(8,128)(2,1)} all-to-all(bf16[8,3,256,128]{3,2,1,0:T(8,128)(2,1)} %merge.4), channel_id=1, replica_groups={{0,1,2,3,4,5,6,7},{8,9,10,11,12,13,14,15},{16,17,18,19,20,21,22,23},{24..., dimensions={0} | all-to-all | bytes 3145728 | tf_op jit(solution)/shard_map/all_to_all | solution.py:353
  349.3 8.6 %assemble.1 = (bf16[256,32,128]{2,1,0:T(8,128)(2,1)}, bf16[256,32,128]{2,1,0:T(8,128)(2,1)}, bf16[256,32,128]{2,1,0:T(8,128)(2,1)}) custom-call(bf16[8,3,256,128]{3,2,1,0:T(8,128)(2,1)} %all_to_all.25.refs_0_, bf16[8,3,256,128]{3,2,1,0:T(8,128)(2,1)} %copy-done.3, bf16[8,3,256,128]{3,2,1,0:T(8,128)(2,1)} %copy-done.2, bf16[8,3,256,128]{3,2,1,0:T(8,128)(2,1)} %copy-done.1), custom_call_target="tpu_custom_call" | custom-call | tf_op jit(solution)/shard_map/assemble/pallas_call | solution.py:315
  (94 shorter events, 40.7 us)
Async XLA Ops:
  0.6 49.2 %copy-start = (s32[8]{0:T(128)S(1)}, s32[8]{0:T(128)}, u32[]{:S(2)}) copy-start(s32[8]{0:T(128)} %param.11) | copy-start | bytes 100
  7.4 56.0 %all-to-all-start = ((bf16[8,4,256,128]{3,2,1,0:T(8,128)(2,1)}), bf16[8,4,256,128]{3,2,1,0:T(8,128)(2,1)S(1)}, u32[]{:S(2)}, u32[]{:S(2)}) async-start(bf16[8,4,256,128]{3,2,1,0:T(8,128)(2,1)} %get-tuple-element.46), calls=%async_computation | async-start | bytes 4194304 | tf_op jit(solution)/shard_map/all_to_all | solution.py:353
  11.1 39.5 %copy-start.13 = (s32[64]{0:T(128)S(1)}, s32[64]{0:T(128)}, u32[]{:S(2)}) copy-start(s32[64]{0:T(128)} %param.10) | copy-start | bytes 772
  18.1 30.4 %collective-permute-start.19 = (bf16[2,1024,128]{2,1,0:T(8,128)(2,1)}, bf16[2,1024,128]{2,1,0:T(8,128)(2,1)S(1)}, u32[]{:S(2)}, u32[]{:S(2)}) collective-permute-start(bf16[2,1024,128]{2,1,0:T(8,128)(2,1)} %get-tuple-element.77), channel_id=1, source_target_pairs={{0,4},{4,0},{8,12},{12,8},{16,20},{20,16},{24,28},{28,24},{1,5},{5... | collective-permute-start | bytes 1572872 | tf_op jit(solution)/shard_map/ppermute | solution.py:345
  20.2 34.0 %collective-permute-start.21 = (bf16[2,1024,128]{2,1,0:T(8,128)(2,1)}, bf16[2,1024,128]{2,1,0:T(8,128)(2,1)}, u32[]{:S(2)}, u32[]{:S(2)}) collective-permute-start(bf16[2,1024,128]{2,1,0:T(8,128)(2,1)} %get-tuple-element.78.kv_keep), channel_id=1, source_target_pairs={{4,12},{8,0},{12,20},{16,8},{20,28},{24,16},{5,13},{9,1},{13,21},{... | collective-permute-start | bytes 1572872 | tf_op jit(solution)/shard_map/ppermute | solution.py:345
  23.3 30.8 %collective-permute-start.18 = (bf16[1024,128]{1,0:T(8,128)(2,1)S(1)}, bf16[1024,128]{1,0:T(8,128)(2,1)S(1)}, u32[]{:S(2)}, u32[]{:S(2)}) collective-permute-start(bf16[1024,128]{1,0:T(8,128)(2,1)S(1)} %copy-done.21), channel_id=1, source_target_pairs={{0,4},{4,0},{8,12},{12,8},{16,20},{20,16},{24,28},{28,24},{1,5},{5... | collective-permute-start | bytes 786440 | tf_op jit(solution)/shard_map/ppermute | solution.py:345
  23.4 68.3 %collective-permute-start.13 = (bf16[2,1024,128]{2,1,0:T(8,128)(2,1)}, bf16[2,1024,128]{2,1,0:T(8,128)(2,1)}, u32[]{:S(2)}, u32[]{:S(2)}) collective-permute-start(bf16[2,1024,128]{2,1,0:T(8,128)(2,1)} %get-tuple-element.67), channel_id=1, source_target_pairs={{0,4},{4,0},{8,12},{12,8},{16,20},{20,16},{24,28},{28,24},{1,5},{5... | collective-permute-start | bytes 1572872 | tf_op jit(solution)/shard_map/ppermute | solution.py:345
  48.6 14.8 %collective-permute-start.20 = (bf16[2,1024,128]{2,1,0:T(8,128)(2,1)S(1)}, bf16[2,1024,128]{2,1,0:T(8,128)(2,1)}, u32[]{:S(2)}, u32[]{:S(2)}) collective-permute-start(bf16[2,1024,128]{2,1,0:T(8,128)(2,1)S(1)} %collective-permute-done.19.kv_recv), channel_id=1, source_target_pairs={{0,8},{8,16},{12,4},{16,24},{20,12},{28,20},{1,9},{9,17},{13,5},{1... | collective-permute-start | bytes 1572872 | tf_op jit(solution)/shard_map/ppermute | solution.py:345
  83.9 16.9 %collective-permute-start.22 = (bf16[2,1024,128]{2,1,0:T(8,128)(2,1)}, bf16[2,1024,128]{2,1,0:T(8,128)(2,1)S(1)}, u32[]{:S(2)}, u32[]{:S(2)}) collective-permute-start(bf16[2,1024,128]{2,1,0:T(8,128)(2,1)} %get-tuple-element.83), channel_id=1, source_target_pairs={{12,4},{0,8},{20,12},{8,16},{28,20},{16,24},{13,5},{1,9},{21,13},{... | collective-permute-start | bytes 1572872 | tf_op jit(solution)/shard_map/ppermute | solution.py:345
  85.2 17.2 %collective-permute-start.23 = (bf16[2,1024,128]{2,1,0:T(8,128)(2,1)}, bf16[2,1024,128]{2,1,0:T(8,128)(2,1)S(1)}, u32[]{:S(2)}, u32[]{:S(2)}) collective-permute-start(bf16[2,1024,128]{2,1,0:T(8,128)(2,1)} %get-tuple-element.84), channel_id=1, source_target_pairs={{8,0},{16,8},{4,12},{24,16},{12,20},{20,28},{9,1},{17,9},{5,13},{2... | collective-permute-start | bytes 1572872 | tf_op jit(solution)/shard_map/ppermute | solution.py:345
  89.8 46.6 %collective-permute-start.15 = (bf16[2,1024,128]{2,1,0:T(8,128)(2,1)S(1)}, bf16[2,1024,128]{2,1,0:T(8,128)(2,1)S(1)}, u32[]{:S(2)}, u32[]{:S(2)}) collective-permute-start(bf16[2,1024,128]{2,1,0:T(8,128)(2,1)S(1)} %copy-done.15), channel_id=1, source_target_pairs={{4,12},{8,0},{12,20},{16,8},{20,28},{24,16},{5,13},{9,1},{13,21},{... | collective-permute-start | bytes 1572872 | tf_op jit(solution)/shard_map/ppermute | solution.py:345
  91.7 45.3 %collective-permute-start.14 = (bf16[2,1024,128]{2,1,0:T(8,128)(2,1)}, bf16[2,1024,128]{2,1,0:T(8,128)(2,1)}, u32[]{:S(2)}, u32[]{:S(2)}) collective-permute-start(bf16[2,1024,128]{2,1,0:T(8,128)(2,1)} %collective-permute-done.13.kv_recv), channel_id=1, source_target_pairs={{0,8},{8,16},{12,4},{16,24},{20,12},{28,20},{1,9},{9,17},{13,5},{1... | collective-permute-start | bytes 1572872 | tf_op jit(solution)/shard_map/ppermute | solution.py:345
  106.5 73.2 %all-to-all-start.4 = ((bf16[8,3,256,128]{3,2,1,0:T(8,128)(2,1)}), bf16[8,3,256,128]{3,2,1,0:T(8,128)(2,1)S(1)}, u32[]{:S(2)}, u32[]{:S(2)}) async-start(bf16[8,3,256,128]{3,2,1,0:T(8,128)(2,1)} %merge.7), calls=%async_computation.4 | async-start | bytes 3145728 | tf_op jit(solution)/shard_map/all_to_all | solution.py:353
  110.2 26.1 %collective-permute-start.12 = (bf16[1024,128]{1,0:T(8,128)(2,1)S(1)}, bf16[1024,128]{1,0:T(8,128)(2,1)S(1)}, u32[]{:S(2)}, u32[]{:S(2)}) collective-permute-start(bf16[1024,128]{1,0:T(8,128)(2,1)S(1)} %copy-done.20), channel_id=1, source_target_pairs={{0,4},{4,0},{8,12},{12,8},{16,20},{20,16},{24,28},{28,24},{1,5},{5... | collective-permute-start | bytes 786440 | tf_op jit(solution)/shard_map/ppermute | solution.py:345
  112.1 55.3 %collective-permute-start.7 = (bf16[2,1024,128]{2,1,0:T(8,128)(2,1)S(1)}, bf16[2,1024,128]{2,1,0:T(8,128)(2,1)}, u32[]{:S(2)}, u32[]{:S(2)}) collective-permute-start(bf16[2,1024,128]{2,1,0:T(8,128)(2,1)S(1)} %copy-done.14), channel_id=1, source_target_pairs={{0,4},{4,0},{8,12},{12,8},{16,20},{20,16},{24,28},{28,24},{1,5},{5... | collective-permute-start | bytes 1572872 | tf_op jit(solution)/shard_map/ppermute | solution.py:345
  157.1 16.7 %collective-permute-start.16 = (bf16[2,1024,128]{2,1,0:T(8,128)(2,1)}, bf16[2,1024,128]{2,1,0:T(8,128)(2,1)S(1)}, u32[]{:S(2)}, u32[]{:S(2)}) collective-permute-start(bf16[2,1024,128]{2,1,0:T(8,128)(2,1)} %get-tuple-element.73), channel_id=1, source_target_pairs={{12,4},{0,8},{20,12},{8,16},{28,20},{16,24},{13,5},{1,9},{21,13},{... | collective-permute-start | bytes 1572872 | tf_op jit(solution)/shard_map/ppermute | solution.py:345
  158.4 17.2 %collective-permute-start.17 = (bf16[2,1024,128]{2,1,0:T(8,128)(2,1)}, bf16[2,1024,128]{2,1,0:T(8,128)(2,1)S(1)}, u32[]{:S(2)}, u32[]{:S(2)}) collective-permute-start(bf16[2,1024,128]{2,1,0:T(8,128)(2,1)} %get-tuple-element.74), channel_id=1, source_target_pairs={{8,0},{16,8},{4,12},{24,16},{12,20},{20,28},{9,1},{17,9},{5,13},{2... | collective-permute-start | bytes 1572872 | tf_op jit(solution)/shard_map/ppermute | solution.py:345
  163.0 48.0 %collective-permute-start.9 = (bf16[2,1024,128]{2,1,0:T(8,128)(2,1)}, bf16[2,1024,128]{2,1,0:T(8,128)(2,1)}, u32[]{:S(2)}, u32[]{:S(2)}) collective-permute-start(bf16[2,1024,128]{2,1,0:T(8,128)(2,1)} %get-tuple-element.58.kv_keep), channel_id=1, source_target_pairs={{4,12},{8,0},{12,20},{16,8},{20,28},{24,16},{5,13},{9,1},{13,21},{... | collective-permute-start | bytes 1572872 | tf_op jit(solution)/shard_map/ppermute | solution.py:345
  167.4 43.5 %collective-permute-start.8 = (bf16[2,1024,128]{2,1,0:T(8,128)(2,1)}, bf16[2,1024,128]{2,1,0:T(8,128)(2,1)}, u32[]{:S(2)}, u32[]{:S(2)}) collective-permute-start(bf16[2,1024,128]{2,1,0:T(8,128)(2,1)} %collective-permute-done.7.kv_recv), channel_id=1, source_target_pairs={{0,8},{8,16},{12,4},{16,24},{20,12},{28,20},{1,9},{9,17},{13,5},{1... | collective-permute-start | bytes 1572872 | tf_op jit(solution)/shard_map/ppermute | solution.py:345
  179.7 50.5 %copy-start.1 = (bf16[8,3,256,128]{3,2,1,0:T(8,128)(2,1)}, bf16[8,3,256,128]{3,2,1,0:T(8,128)(2,1)S(1)}, u32[]{:S(2)}) copy-start(bf16[8,3,256,128]{3,2,1,0:T(8,128)(2,1)S(1)} %all-to-all-done.4.refs_3_) | copy-start | bytes 4718596
  179.7 73.0 %all-to-all-start.3 = ((bf16[8,3,256,128]{3,2,1,0:T(8,128)(2,1)}), bf16[8,3,256,128]{3,2,1,0:T(8,128)(2,1)S(1)}, u32[]{:S(2)}, u32[]{:S(2)}) async-start(bf16[8,3,256,128]{3,2,1,0:T(8,128)(2,1)} %merge.6), calls=%async_computation.3 | async-start | bytes 3145728 | tf_op jit(solution)/shard_map/all_to_all | solution.py:353
  184.0 26.2 %collective-permute-start.6 = (bf16[1024,128]{1,0:T(8,128)(2,1)S(1)}, bf16[1024,128]{1,0:T(8,128)(2,1)S(1)}, u32[]{:S(2)}, u32[]{:S(2)}) collective-permute-start(bf16[1024,128]{1,0:T(8,128)(2,1)S(1)} %copy-done.19), channel_id=1, source_target_pairs={{0,4},{4,0},{8,12},{12,8},{16,20},{20,16},{24,28},{28,24},{1,5},{5... | collective-permute-start | bytes 786440 | tf_op jit(solution)/shard_map/ppermute | solution.py:345
  186.0 54.1 %collective-permute-start.1 = (bf16[2,1024,128]{2,1,0:T(8,128)(2,1)}, bf16[2,1024,128]{2,1,0:T(8,128)(2,1)}, u32[]{:S(2)}, u32[]{:S(2)}) collective-permute-start(bf16[2,1024,128]{2,1,0:T(8,128)(2,1)} %get-tuple-element.47), channel_id=1, source_target_pairs={{0,4},{4,0},{8,12},{12,8},{16,20},{20,16},{24,28},{28,24},{1,5},{5... | collective-permute-start | bytes 1572872 | tf_op jit(solution)/shard_map/ppermute | solution.py:345
  230.1 16.6 %collective-permute-start.10 = (bf16[2,1024,128]{2,1,0:T(8,128)(2,1)}, bf16[2,1024,128]{2,1,0:T(8,128)(2,1)S(1)}, u32[]{:S(2)}, u32[]{:S(2)}) collective-permute-start(bf16[2,1024,128]{2,1,0:T(8,128)(2,1)} %get-tuple-element.63), channel_id=1, source_target_pairs={{12,4},{0,8},{20,12},{8,16},{28,20},{16,24},{13,5},{1,9},{21,13},{... | collective-permute-start | bytes 1572872 | tf_op jit(solution)/shard_map/ppermute | solution.py:345
  231.4 17.2 %collective-permute-start.11 = (bf16[2,1024,128]{2,1,0:T(8,128)(2,1)}, bf16[2,1024,128]{2,1,0:T(8,128)(2,1)S(1)}, u32[]{:S(2)}, u32[]{:S(2)}) collective-permute-start(bf16[2,1024,128]{2,1,0:T(8,128)(2,1)} %get-tuple-element.64), channel_id=1, source_target_pairs={{8,0},{16,8},{4,12},{24,16},{12,20},{20,28},{9,1},{17,9},{5,13},{2... | collective-permute-start | bytes 1572872 | tf_op jit(solution)/shard_map/ppermute | solution.py:345
  236.0 47.0 %collective-permute-start.3 = (bf16[2,1024,128]{2,1,0:T(8,128)(2,1)}, bf16[2,1024,128]{2,1,0:T(8,128)(2,1)}, u32[]{:S(2)}, u32[]{:S(2)}) collective-permute-start(bf16[2,1024,128]{2,1,0:T(8,128)(2,1)} %get-tuple-element.48.kv_keep), channel_id=1, source_target_pairs={{4,12},{8,0},{12,20},{16,8},{20,28},{24,16},{5,13},{9,1},{13,21},{... | collective-permute-start | bytes 1572872 | tf_op jit(solution)/shard_map/ppermute | solution.py:345
  240.1 42.9 %collective-permute-start.2 = (bf16[2,1024,128]{2,1,0:T(8,128)(2,1)}, bf16[2,1024,128]{2,1,0:T(8,128)(2,1)}, u32[]{:S(2)}, u32[]{:S(2)}) collective-permute-start(bf16[2,1024,128]{2,1,0:T(8,128)(2,1)} %collective-permute-done.1.kv_recv), channel_id=1, source_target_pairs={{0,8},{8,16},{12,4},{16,24},{20,12},{28,20},{1,9},{9,17},{13,5},{1... | collective-permute-start | bytes 1572872 | tf_op jit(solution)/shard_map/ppermute | solution.py:345
  252.7 49.5 %copy-start.2 = (bf16[8,3,256,128]{3,2,1,0:T(8,128)(2,1)}, bf16[8,3,256,128]{3,2,1,0:T(8,128)(2,1)S(1)}, u32[]{:S(2)}) copy-start(bf16[8,3,256,128]{3,2,1,0:T(8,128)(2,1)S(1)} %all-to-all-done.3.refs_2_) | copy-start | bytes 4718596
  252.7 70.4 %all-to-all-start.2 = ((bf16[8,3,256,128]{3,2,1,0:T(8,128)(2,1)}), bf16[8,3,256,128]{3,2,1,0:T(8,128)(2,1)S(1)}, u32[]{:S(2)}, u32[]{:S(2)}) async-start(bf16[8,3,256,128]{3,2,1,0:T(8,128)(2,1)} %merge.5), calls=%async_computation.2 | async-start | bytes 3145728 | tf_op jit(solution)/shard_map/all_to_all | solution.py:353
  256.6 25.7 %collective-permute-start = (bf16[1024,128]{1,0:T(8,128)(2,1)S(1)}, bf16[1024,128]{1,0:T(8,128)(2,1)S(1)}, u32[]{:S(2)}, u32[]{:S(2)}) collective-permute-start(bf16[1024,128]{1,0:T(8,128)(2,1)S(1)} %copy-done.18), channel_id=1, source_target_pairs={{0,4},{4,0},{8,12},{12,8},{16,20},{20,16},{24,28},{28,24},{1,5},{5... | collective-permute-start | bytes 786440 | tf_op jit(solution)/shard_map/ppermute | solution.py:345
  302.2 15.5 %collective-permute-start.4 = (bf16[2,1024,128]{2,1,0:T(8,128)(2,1)}, bf16[2,1024,128]{2,1,0:T(8,128)(2,1)S(1)}, u32[]{:S(2)}, u32[]{:S(2)}) collective-permute-start(bf16[2,1024,128]{2,1,0:T(8,128)(2,1)} %get-tuple-element.53), channel_id=1, source_target_pairs={{12,4},{0,8},{20,12},{8,16},{28,20},{16,24},{13,5},{1,9},{21,13},{... | collective-permute-start | bytes 1572872 | tf_op jit(solution)/shard_map/ppermute | solution.py:345
  303.5 15.5 %collective-permute-start.5 = (bf16[2,1024,128]{2,1,0:T(8,128)(2,1)}, bf16[2,1024,128]{2,1,0:T(8,128)(2,1)S(1)}, u32[]{:S(2)}, u32[]{:S(2)}) collective-permute-start(bf16[2,1024,128]{2,1,0:T(8,128)(2,1)} %get-tuple-element.54), channel_id=1, source_target_pairs={{8,0},{16,8},{4,12},{24,16},{12,20},{20,28},{9,1},{17,9},{5,13},{2... | collective-permute-start | bytes 1572872 | tf_op jit(solution)/shard_map/ppermute | solution.py:345
  (22 other events, 119.1 us)
where the time goes:
time: 364 us; the launch traced here: 358 us
  waiting for transfers between devices  141 us (39%)
  Pallas kernels  112 us (31%)
  starting transfers between devices  68.3 us (19%)
  blocking collectives  26.2 us (7%)
  local copies, waits for them, and re-layouts  8.17 us (2%)
    ppermute x24, waiting for transfers between devices, over_slab(): return lax.ppermute(array, 'slab', pairs)  141 us
    pallas_call x4, Pallas kernels, attention_call(): pl.pallas_call(attention_kernel, grid=(1,), out_shape=(jax.ShapeDtypeStru...  76.8 us
    ppermute x24, starting transfers between devices, over_slab(): return lax.ppermute(array, 'slab', pairs)  52.5 us
    all_to_all x1, blocking collectives, to_all(): lax.all_to_all(array, ('slab', 'row'), 0, 0, axis_index_groups=groups, ti...  26.2 us
    all_to_all x4, starting transfers between devices, to_all(): lax.all_to_all(array, ('slab', 'row'), 0, 0, axis_index_groups=groups, ti...  15.7 us
    pallas_call x4, Pallas kernels, merge(): pl.pallas_call(merge_kernel, out_shape=jax.ShapeDtypeStruct((2 * row_coun...  13.3 us
    pallas_call x1, Pallas kernels, assemble(): pl.pallas_call(assemble_kernel, grid=(steps,), out_shape=(jax.ShapeDtypeS...  8.59 us
    unnamed x52, local copies, waits for them, and re-layouts  7.45 us
  transfers between devices with their start and end apart: 28, of which 14 were waited for; matrix products, arithmetic and copies ran while one was open for 0% of the time, Pallas kernels for 27%

commit v1 on v0

--- a/solution.py
+++ b/solution.py
@@ -1,3 +1,4 @@
+import functools
 import math
 
 import jax
@@ -18,6 +19,7 @@
 
 
 def attention_kernel(
+    place_in_group,
     scalars,
     q_keep,
     q_recv,
@@ -36,27 +38,42 @@
     do_buf,
     k_buf,
     v_buf,
-    kt_buf,
+    low_buf,
+    high_buf,
     dk_acc,
     dv_acc,
     p_buf,
     dp_buf,
+    sems,
 ):
     tok, head_dim = q_keep.shape
     scale = head_dim ** (-0.5)
     parity = scalars[2 * TPS + 4]
-
-    q_buf[pl.ds(0, tok), :] = q_keep[...]
-    q_buf[pl.ds(tok, tok), :] = q_recv[...]
     senders, _, part, _ = do_ref.shape
-    for sender in range(senders):
-        do_buf[pl.ds(sender * part, part), :] = do_ref[sender, 0]
+    count = 0
+
+    def begin(source, target):
+        nonlocal count
+        copy = pltpu.make_async_copy(source, target, sems.at[count])
+        count += 1
+        copy.start()
+        return copy
+
+    loads = []
     for slot, ref in enumerate((kv_low, kv_keep, kv_recv, kv_high)):
-        k_buf[pl.ds(slot * tok, tok), :] = ref[0]
-        v_buf[pl.ds(slot * tok, tok), :] = ref[1]
-        kt_buf[:, pl.ds(slot * tok, tok)] = ref[0].T
+        rows = pl.ds(slot * tok, tok)
+        if slot == 1:
+            loads += [begin(q_keep, q_buf.at[pl.ds(0, tok), :])]
+            for sender in range(senders):
+                rows_do = pl.ds(sender * part, part)
+                loads += [begin(do_ref.at[sender, place_in_group], do_buf.at[rows_do, :])]
+        late = [begin(ref.at[0], k_buf.at[rows, :]), begin(ref.at[1], v_buf.at[rows, :])]
+        loads += late if slot < 3 else []
+    late += [begin(q_recv, q_buf.at[pl.ds(tok, tok), :])]
     dk_acc[...] = jnp.zeros_like(dk_acc)
     dv_acc[...] = jnp.zeros_like(dv_acc)
+    for copy in loads:
+        copy.wait()
 
     def unit(side, col, q_starts):
         width = TILE * len(q_starts)
@@ -88,7 +105,8 @@
                 (((1,), (1,)), ((), ())),
                 preferred_element_type=jnp.float32,
             )
-            scores = jnp.where(key_row < limits[block], scores, NEG)
+            if block != GH:
+                scores = jnp.where(key_row < limits[block], scores, NEG)
             p_buf[pl.ds(block * SPAN, SPAN), pl.ds(0, width)] = scores
             top = jnp.maximum(top, jnp.max(scores.reshape(SPAN // 8, 8, width), axis=0))
         top = jnp.max(top, axis=0, keepdims=True)
@@ -109,7 +127,7 @@
             delta += jnp.sum((expo * grad).reshape(SPAN // 8, 8, width), axis=0)
         inverse = 1.0 / jnp.sum(total, axis=0, keepdims=True)
         delta = jnp.sum(delta, axis=0, keepdims=True) * inverse
-        dq_t = jnp.zeros((head_dim, width), jnp.float32)
+        dq = jnp.zeros((width, head_dim), jnp.float32)
         for block in range(blocks):
             here = pl.ds(block * SPAN, SPAN), pl.ds(0, width)
             keys_here = pl.ds(offsets[block], SPAN)
@@ -118,8 +136,13 @@
             attend_b = attend.astype(jnp.bfloat16)
             dv_acc[keys_here, :] += jnp.dot(attend_b, do, preferred_element_type=jnp.float32)
             dk_acc[keys_here, :] += jnp.dot(grad_scores, q, preferred_element_type=jnp.float32)
-            dq_t += jnp.dot(kt_buf[:, keys_here], grad_scores, preferred_element_type=jnp.float32)
-        dq = (dq_t * scale).T.astype(jnp.bfloat16)
+            dq += lax.dot_general(
+                grad_scores,
+                k_buf[keys_here, :],
+                (((0,), (0,)), ((), ())),
+                preferred_element_type=jnp.float32,
+            )
+        dq = (dq * scale).astype(jnp.bfloat16)
         for place, start in enumerate(q_starts):
             q_buf[pl.ds(start, TILE), :] = dq[place * TILE : (place + 1) * TILE]
 
@@ -146,44 +169,51 @@
 
         return carry
 
-    lax.fori_loop(0, 2 * GW, step, 0)
-    dq_keep[...] = q_buf[pl.ds(0, tok), :]
-    dq_recv[...] = q_buf[pl.ds(tok, tok), :]
-    for place, (acc, factor) in enumerate(((dk_acc, scale), (dv_acc, None))):
-        for slot, ref in enumerate((half_low, own_keep, own_recv, half_high)):
-            part_sum = acc[pl.ds(slot * tok, tok), :]
-            if factor is not None:
-                part_sum = part_sum * factor
-            ref[place] = part_sum.astype(ref.dtype)
-
-
-def attention_call(scalars, chunk, q_keep, q_recv, do_all, kv_low, kv_keep, kv_recv, kv_high):
+    lax.fori_loop(0, GW, step, 0)
+    for copy in late:
+        copy.wait()
+    stores = [begin(q_buf.at[pl.ds(0, tok), :], dq_keep)]
+    low_buf[0] = (dk_acc[pl.ds(0, tok), :] * scale).astype(low_buf.dtype)
+    low_buf[1] = dv_acc[pl.ds(0, tok), :].astype(low_buf.dtype)
+    stores += [begin(low_buf, half_low)]
+    lax.fori_loop(GW, 2 * GW, step, 0)
+    stores += [begin(q_buf.at[pl.ds(tok, tok), :], dq_recv)]
+    for slot, ref in ((1, own_keep), (2, own_recv)):
+        rows = pl.ds(slot * tok, tok)
+        stores += [begin(dk_acc.at[rows, :], ref.at[0]), begin(dv_acc.at[rows, :], ref.at[1])]
+    high_buf[0] = (dk_acc[pl.ds(3 * tok, tok), :] * scale).astype(high_buf.dtype)
+    high_buf[1] = dv_acc[pl.ds(3 * tok, tok), :].astype(high_buf.dtype)
+    stores += [begin(high_buf, half_high)]
+    for copy in stores:
+        copy.wait()
+
+
+def attention_call(scalars, place_in_group, q_keep, q_recv, do_all, kv_low, kv_keep, kv_recv, kv_high):
     tok, head_dim = q_keep.shape
-    senders, _, part, _ = do_all.shape
-    whole = pl.BlockSpec((tok, head_dim), lambda i: (0, 0))
-    pair = pl.BlockSpec((2, tok, head_dim), lambda i: (0, 0, 0))
-    do_spec = pl.BlockSpec((senders, 1, part, head_dim), lambda i: (0, chunk, 0, 0))
+    senders, _, _, _ = do_all.shape
+    place = pl.BlockSpec(memory_space=pl.ANY)
     keys_all = 4 * tok
     window = 3 * GH * SPAN
     pairs = 2 * TPS * TILE * window
     return pl.pallas_call(
-        attention_kernel,
-        grid=(1,),
+        functools.partial(attention_kernel, place_in_group),
         out_shape=(jax.ShapeDtypeStruct((tok, head_dim), jnp.bfloat16),) * 2
         + (jax.ShapeDtypeStruct((2, tok, head_dim), jnp.float32),) * 2
         + (jax.ShapeDtypeStruct((2, tok, head_dim), jnp.bfloat16),) * 2,
-        in_specs=[pl.BlockSpec(memory_space=pltpu.SMEM), whole, whole, do_spec] + [pair] * 4,
-        out_specs=(whole,) * 2 + (pair,) * 4,
+        in_specs=[pl.BlockSpec(memory_space=pltpu.SMEM)] + [place] * 7,
+        out_specs=(place,) * 6,
         scratch_shapes=[
             pltpu.VMEM((2 * tok, head_dim), jnp.bfloat16),
             pltpu.VMEM((2 * tok, head_dim), jnp.bfloat16),
             pltpu.VMEM((keys_all, head_dim), jnp.bfloat16),
             pltpu.VMEM((keys_all, head_dim), jnp.bfloat16),
-            pltpu.VMEM((head_dim, keys_all), jnp.bfloat16),
+            pltpu.VMEM((2, tok, head_dim), jnp.bfloat16),
+            pltpu.VMEM((2, tok, head_dim), jnp.bfloat16),
             pltpu.VMEM((keys_all, head_dim), jnp.float32),
             pltpu.VMEM((keys_all, head_dim), jnp.float32),
             pltpu.VMEM((window, GH * TILE), jnp.float32),
             pltpu.VMEM((window, GH * TILE), jnp.float32),
+            pltpu.SemaphoreType.DMA((18 + senders,)),
         ],
         cost_estimate=pl.CostEstimate(
             flops=10 * pairs * head_dim, transcendentals=pairs, bytes_accessed=16 * tok * head_dim * 2
@@ -205,7 +235,7 @@
 
 def split_pair(scalars, first, second):
     tok, heads_here, head_dim = first.shape
-    steps = TPS
+    steps = TPS // 2
     block = tok // steps
     chunks = heads_here // 2
     spec = pl.BlockSpec((block, heads_here, head_dim), lambda i: (i, 0, 0))
@@ -222,8 +252,13 @@
     return outs[:chunks], outs[chunks:]
 
 
+def chunk_groups(chunks):
+    first = max(1, chunks // 2)
+    return [range(first)] + ([range(first, chunks)] if first < chunks else [])
+
+
 def spread_kernel(scalars, queries, out_grad, *refs):
-    outs, do_out, held_q, held_do = refs[:-3], refs[-3], refs[-2], refs[-1]
+    outs, held_q, held_do = refs[:-2], refs[-2], refs[-1]
     side = scalars[0]
     heads_here = held_q.shape[0]
     chunks = heads_here // 2
@@ -233,90 +268,110 @@
         outs[chunk][...] = held_q[(1 - side) * chunks + chunk]
         outs[chunks + chunk][...] = held_q[side * chunks + chunk]
     held_do[...] = jnp.swapaxes(out_grad[...], 0, 1)
-    for group in range(2):
-        for row in range(row_count):
-            head = row * heads_here + group * chunks
-            do_out[group * row_count + row] = held_do[head : head + chunks]
+    for out, members in zip(outs[2 * chunks :], chunk_groups(chunks)):
+        for group in range(2):
+            for row in range(row_count):
+                head = row * heads_here + group * chunks + members[0]
+                out[group * row_count + row] = held_do[head : head + len(members)]
 
 
 def spread(scalars, queries, out_grad):
     tok, heads_here, head_dim = queries.shape
     part, heads, _ = out_grad.shape
-    steps = min(TPS, part // 16)
+    steps = min(TPS // 2, part // 16)
     chunks = heads_here // 2
     targets = 2 * heads // heads_here
+    sizes = [len(members) for members in chunk_groups(chunks)]
     outs = pl.pallas_call(
         spread_kernel,
         grid=(steps,),
         out_shape=(jax.ShapeDtypeStruct((tok, head_dim), queries.dtype),) * (2 * chunks)
-        + (jax.ShapeDtypeStruct((targets, chunks, part, head_dim), queries.dtype),),
+        + tuple(
+            jax.ShapeDtypeStruct((targets, size, part, head_dim), queries.dtype) for size in sizes
+        ),
         in_specs=[
             pl.BlockSpec(memory_space=pltpu.SMEM),
             pl.BlockSpec((tok // steps, heads_here, head_dim), lambda i: (i, 0, 0)),
             pl.BlockSpec((part // steps, heads, head_dim), lambda i: (i, 0, 0)),
         ],
         out_specs=(pl.BlockSpec((tok // steps, head_dim), lambda i: (i, 0)),) * (2 * chunks)
-        + (pl.BlockSpec((targets, chunks, part // steps, head_dim), lambda i: (0, 0, i, 0)),),
+        + tuple(
+            pl.BlockSpec((targets, size, part // steps, head_dim), lambda i: (0, 0, i, 0))
+            for size in sizes
+        ),
         scratch_shapes=[
             pltpu.VMEM((heads_here, tok // steps, head_dim), queries.dtype),
             pltpu.VMEM((heads, part // steps, head_dim), queries.dtype),
         ],
         name="spread",
     )(scalars, queries, out_grad)
-    return outs[:chunks], outs[chunks : 2 * chunks], outs[-1]
-
-
-def merge_kernel(scalars, dq_keep, dq_recv, own_keep, own_recv, add_keep, add_recv, out):
-    targets, _, part, _ = out.shape
+    return outs[:chunks], outs[chunks : 2 * chunks], outs[2 * chunks :]
+
+
+def merge_kernel(scalars, own_keep, own_recv, add_keep, add_recv, *refs):
+    query_grads, out = refs[:-1], refs[-1]
+    targets, _, part, head_dim = out.shape
     row_count = targets // 2
     side = scalars[0]
-    groups = ((dq_keep, own_keep, add_keep, side), (dq_recv, own_recv, add_recv, 1 - side))
-    for grad, own, add, place in groups:
+    factors = (head_dim ** (-0.5), 1.0)
+    sums = ((own_keep, add_keep, side), (own_recv, add_recv, 1 - side))
+    for which, (own, add, place) in enumerate(sums):
         for row in range(row_count):
             rows = pl.ds(row * part, part)
             target = place * row_count + row
-            out[target, 0] = grad[rows, :]
-            for which in range(2):
-                total = own[which, rows, :] + add[which, rows, :].astype(jnp.float32)
-                out[target, 1 + which] = total.astype(out.dtype)
-
-
-def merge(scalars, row_count, dq_keep, dq_recv, own_keep, own_recv, add_keep, add_recv):
-    tok, head_dim = dq_keep.shape
+            for plane, factor in enumerate(factors):
+                total = own[plane, rows, :] * factor + add[plane, rows, :].astype(jnp.float32)
+                out[target, plane] = total.astype(out.dtype)
+            for plane, grad in enumerate(query_grads[which::2]):
+                out[target, 2 + plane] = grad[rows, :]
+
+
+def merge(scalars, row_count, own_keep, own_recv, add_keep, add_recv, query_grads):
+    _, tok, head_dim = own_keep.shape
     vmem = pl.BlockSpec(memory_space=pltpu.VMEM)
+    flat = [grad for pair in query_grads for grad in pair]
+    shape = (2 * row_count, 2 + len(query_grads), tok // row_count, head_dim)
     return pl.pallas_call(
         merge_kernel,
-        out_shape=jax.ShapeDtypeStruct((2 * row_count, 3, tok // row_count, head_dim), jnp.bfloat16),
-        in_specs=[pl.BlockSpec(memory_space=pltpu.SMEM)] + [vmem] * 6,
+        out_shape=jax.ShapeDtypeStruct(shape, jnp.bfloat16),
+        in_specs=[pl.BlockSpec(memory_space=pltpu.SMEM)] + [vmem] * (4 + len(flat)),
         out_specs=vmem,
         name="merge",
-    )(scalars, dq_keep, dq_recv, own_keep, own_recv, add_keep, add_recv)
+    )(scalars, own_keep, own_recv, add_keep, add_recv, *flat)
+
+
+def query_place(chunk):
+    return (0, 2) if chunk == 0 else (chunk - 1, 3 if chunk == 1 else 2)
 
 
 def assemble_kernel(*refs):
     chunks = len(refs) - 4
     pieces, outs, held = refs[:chunks], refs[chunks:-1], refs[-1]
-    senders = pieces[0].shape[0]
-    for plane in range(3):
+    row_count = pieces[0].shape[0] // 2
+    for index, out in enumerate(outs):
         for chunk in range(chunks):
+            message, plane = query_place(chunk) if index == 0 else (chunk, index - 1)
             for group in range(2):
-                for row in range(senders // 2):
+                for row in range(row_count):
                     head = row * 2 * chunks + group * chunks + chunk
-                    held[head] = pieces[chunk][group * (senders // 2) + row, plane]
-        outs[plane][...] = jnp.swapaxes(held[...], 0, 1)
+                    held[head] = pieces[message][group * row_count + row, plane]
+        out[...] = jnp.swapaxes(held[...], 0, 1)
 
 
 def assemble(pieces):
     chunks = len(pieces)
     senders, _, part, head_dim = pieces[0].shape
     heads = chunks * senders
-    steps = min(TPS, part // 16)
+    steps = min(TPS // 2, part // 16)
     block = part // steps
     return pl.pallas_call(
         assemble_kernel,
         grid=(steps,),
         out_shape=(jax.ShapeDtypeStruct((part, heads, head_dim), jnp.bfloat16),) * 3,
-        in_specs=[pl.BlockSpec((senders, 3, block, head_dim), lambda i: (0, 0, i, 0))] * chunks,
+        in_specs=[
+            pl.BlockSpec((senders, piece.shape[1], block, head_dim), lambda i: (0, 0, i, 0))
+            for piece in pieces
+        ],
         out_specs=(pl.BlockSpec((block, heads, head_dim), lambda i: (i, 0, 0)),) * 3,
         scratch_shapes=[pltpu.VMEM((heads, block, head_dim), jnp.bfloat16)],
         name="assemble",
@@ -376,23 +431,36 @@
 
     kv_sent, kv_keep = split_pair(places, keys, values)
     q_sent, q_keep, do_sent = spread(places, queries, out_grad)
-    do_all = to_all(do_sent)
+    do_of = {}
+    for index, members in enumerate(chunk_groups(chunks)):
+        arrived = to_all(do_sent[index])
+        for place, chunk in enumerate(members):
+            do_of[chunk] = (place, arrived)
     inputs = []
     for chunk in range(chunks):
         kv_recv = over_slab(kv_sent[chunk], swap)
         kv_high = over_slab(kv_keep[chunk], out_high)
         kv_low = over_slab(kv_recv, out_low)
         q_recv = over_slab(q_sent[chunk], swap)
-        inputs.append((q_keep[chunk], q_recv, do_all, kv_low, kv_keep[chunk], kv_recv, kv_high))
-
-    pieces = []
+        place, do_all = do_of[chunk]
+        inputs.append(
+            (place, q_keep[chunk], q_recv, do_all, kv_low, kv_keep[chunk], kv_recv, kv_high)
+        )
+
+    query_grads = []
+    partial_sums = []
     for chunk in range(chunks):
         dq_keep, dq_recv, own_keep, own_recv, half_low, half_high = attention_call(
-            scalars, chunk, *inputs[chunk]
+            scalars, *inputs[chunk]
         )
         add_keep = over_slab(half_high, turned(out_high))
         add_recv = over_slab(half_low, turned(out_low))
-        merged = merge(places, row_count, dq_keep, dq_recv, own_keep, own_recv, add_keep, add_recv)
+        query_grads.append((dq_keep, dq_recv))
+        partial_sums.append((own_keep, own_recv, add_keep, add_recv))
+    pieces = []
+    for chunk in range(chunks):
+        own = [query_grads[other] for other in range(chunks) if query_place(other)[0] == chunk]
+        merged = merge(places, row_count, *partial_sums[chunk], own)
         pieces.append(to_all(merged))
     return tuple(assemble(pieces))
 

time: 364 us -> 316 us (0.87)
  the two profiles are of different devices: /device:TPU:24 before, /device:TPU:0 now
where the time goes in v1:
time: 316 us; the launch traced here: 314 us
  Pallas kernels  103 us (33%)
  waiting for transfers between devices  90.1 us (29%)
  starting transfers between devices  81.1 us (26%)
  blocking collectives  30.9 us (10%)
  local copies, waits for them, and re-layouts  7.12 us (2%)
    ppermute x24, waiting for transfers between devices, over_slab(): return lax.ppermute(array, 'slab', pairs)  85.4 us
    pallas_call x4, Pallas kernels, attention_call(): pl.pallas_call(functools.partial(attention_kernel, place_in_group), out_s...  73 us
    ppermute x24, starting transfers between devices, over_slab(): return lax.ppermute(array, 'slab', pairs)  61.6 us
    all_to_all x1, blocking collectives, to_all(): lax.all_to_all(array, ('slab', 'row'), 0, 0, axis_index_groups=groups, ti...  30.9 us
    all_to_all x5, starting transfers between devices, to_all(): lax.all_to_all(array, ('slab', 'row'), 0, 0, axis_index_groups=groups, ti...  19.6 us
    pallas_call x4, Pallas kernels, merge(): pl.pallas_call(merge_kernel, out_shape=jax.ShapeDtypeStruct(shape, jnp.bf...  13.4 us
    pallas_call x1, Pallas kernels, assemble(): pl.pallas_call(assemble_kernel, grid=(steps,), out_shape=(jax.ShapeDtypeS...  6.63 us
    unnamed x54, local copies, waits for them, and re-layouts  6.41 us
  transfers between devices with their start and end apart: 29, of which 13 were waited for; matrix products, arithmetic and copies ran while one was open for 0% of the time, Pallas kernels for 29%

profile of v1, /device:TPU:0, one launch (start us, length us, event | category | flops | bytes accessed | tf_op | source)
XLA Modules:
  0.0 314.3 jit_solution(14749013848133153019)
XLA Ops:
  0.7 5.2 %split_pair.1 = (bf16[2,1024,128]{2,1,0:T(8,128)(2,1)}, bf16[2,1024,128]{2,1,0:T(8,128)(2,1)}, bf16[2,1024,128]{2,1,0:T(8,128)(2,1)}, bf16[2,1024,128]{2,1,0:T(8...) custom-call(s32[1]{0:T(128)} %bitcast.scalars, ...), custom_call_target="tpu_custom_call" | custom-call | tf_op jit(solution)/shard_map/split_pair/pallas_call | solution.py:243
  8.9 5.1 %spread.1 = (bf16[1024,128]{1,0:T(8,128)(2,1)}, bf16[1024,128]{1,0:T(8,128)(2,1)}, bf16[1024,128]{1,0:T(8,128)(2,1)}, bf16[1024,128]{1,0:T(8,128)(2,1)}, bf16[10...) custom-call(s32[1]{0:T(128)} %bitcast.scalars, ...), custom_call_target="tpu_custom_call" | custom-call | tf_op jit(solution)/shard_map/spread/pallas_call | solution.py:285
  14.0 3.7 %all-to-all-start.2 = ((bf16[8,2,256,128]{3,2,1,0:T(8,128)(2,1)}), bf16[8,2,256,128]{3,2,1,0:T(8,128)(2,1)S(1)}, u32[]{:S(2)}, u32[]{:S(2)}) async-start(bf16[8,2,256,128]{3,2,1,0:T(8,128)(2,1)} %get-tuple-element.68), calls=%async_computation.2 | async-start | bytes 2097152 | tf_op jit(solution)/shard_map/all_to_all | solution.py:408
  19.1 4.9 %collective-permute-start.18 = (bf16[1024,128]{1,0:T(8,128)(2,1)S(1)}, bf16[1024,128]{1,0:T(8,128)(2,1)S(1)}, u32[]{:S(2)}, u32[]{:S(2)}) collective-permute-start(bf16[1024,128]{1,0:T(8,128)(2,1)S(1)} %copy-done.23), channel_id=1, source_target_pairs={{0,4},{4,0},{8,12},{12,8},{16,20},{20,16},{24,28},{28,24},{1,5},{5... | collective-permute-start | bytes 786440 | tf_op jit(solution)/shard_map/ppermute | solution.py:400
  24.1 3.6 %collective-permute-start.20 = (bf16[2,1024,128]{2,1,0:T(8,128)(2,1)}, bf16[2,1024,128]{2,1,0:T(8,128)(2,1)}, u32[]{:S(2)}, u32[]{:S(2)}) collective-permute-start(bf16[2,1024,128]{2,1,0:T(8,128)(2,1)} %collective-permute-done.19.kv_recv), channel_id=1, source_target_pairs={{0,8},{8,16},{12,4},{16,24},{20,12},{28,20},{1,9},{9,17},{13,5},{1... | collective-permute-start | bytes 1572872 | tf_op jit(solution)/shard_map/ppermute | solution.py:400
  28.5 4.7 %all-to-all-done.2.do_ref = bf16[8,2,256,128]{3,2,1,0:T(8,128)(2,1)S(1)} async-done(((bf16[8,2,256,128]{3,2,1,0:T(8,128)(2,1)}), bf16[8,2,256,128]{3,2,1,0:T(8,128)(2,1)S(1)}, u32[]{:S(2)}, u32[]{:S(2)}) %all-to-all-start.2) | async-done | bytes 1048608 | tf_op jit(solution)/shard_map/all_to_all | solution.py:408
  33.2 4.2 %all-to-all-start = ((bf16[8,2,256,128]{3,2,1,0:T(8,128)(2,1)}), bf16[8,2,256,128]{3,2,1,0:T(8,128)(2,1)S(1)}, u32[]{:S(2)}, u32[]{:S(2)}) async-start(bf16[8,2,256,128]{3,2,1,0:T(8,128)(2,1)} %get-tuple-element.47), calls=%async_computation | async-start | bytes 2097152 | tf_op jit(solution)/shard_map/all_to_all | solution.py:408
  39.0 18.3 %window_grads.7 = (bf16[1024,128]{1,0:T(8,128)(2,1)}, bf16[1024,128]{1,0:T(8,128)(2,1)}, f32[2,1024,128]{2,1,0:T(8,128)}, f32[2,1024,128]{2,1,0:T(8,128)}, bf16[...) custom-call(s32[21]{0:T(128)} %pad_add_fusion.scalars, bf16[1024,128]{1,0:T(8,128)(2,1)} %get-tuple-element.77.q_keep, ...), custom_call_target="tpu_custom_call" | custom-call | flops 4026531840 | bytes 4194304 | tf_op jit(solution)/shard_map/window_grads/pallas_call | solution.py:198
  57.3 4.2 %collective-permute-start.22 = (bf16[2,1024,128]{2,1,0:T(8,128)(2,1)}, bf16[2,1024,128]{2,1,0:T(8,128)(2,1)S(1)}, u32[]{:S(2)}, u32[]{:S(2)}) collective-permute-start(bf16[2,1024,128]{2,1,0:T(8,128)(2,1)} %get-tuple-element.85), channel_id=1, source_target_pairs={{12,4},{0,8},{20,12},{8,16},{28,20},{16,24},{13,5},{1,9},{21,13},{... | collective-permute-start | bytes 1572872 | tf_op jit(solution)/shard_map/ppermute | solution.py:400
  64.1 6.0 %collective-permute-start.14 = (bf16[2,1024,128]{2,1,0:T(8,128)(2,1)}, bf16[2,1024,128]{2,1,0:T(8,128)(2,1)}, u32[]{:S(2)}, u32[]{:S(2)}) collective-permute-start(bf16[2,1024,128]{2,1,0:T(8,128)(2,1)} %collective-permute-done.13.kv_recv), channel_id=1, source_target_pairs={{0,8},{8,16},{12,4},{16,24},{20,12},{28,20},{1,9},{9,17},{13,5},{1... | collective-permute-start | bytes 1572872 | tf_op jit(solution)/shard_map/ppermute | solution.py:400
  74.1 4.3 %collective-permute-done.23.add_recv = bf16[2,1024,128]{2,1,0:T(8,128)(2,1)S(1)} collective-permute-done((bf16[2,1024,128]{2,1,0:T(8,128)(2,1)}, bf16[2,1024,128]{2,1,0:T(8,128)(2,1)S(1)}, u32[]{:S(2)}, u32[]{:S(2)}) %collective-permute-start.23) | collective-permute-done | bytes 524320 | tf_op jit(solution)/shard_map/ppermute | solution.py:400
  82.3 3.9 %all-to-all-start.5 = ((bf16[8,2,256,128]{3,2,1,0:T(8,128)(2,1)}), bf16[8,2,256,128]{3,2,1,0:T(8,128)(2,1)S(1)}, u32[]{:S(2)}, u32[]{:S(2)}) async-start(bf16[8,2,256,128]{3,2,1,0:T(8,128)(2,1)} %merge.7), calls=%async_computation.5 | async-start | bytes 2097152 | tf_op jit(solution)/shard_map/all_to_all | solution.py:408
  88.4 18.4 %window_grads.6 = (bf16[1024,128]{1,0:T(8,128)(2,1)}, bf16[1024,128]{1,0:T(8,128)(2,1)}, f32[2,1024,128]{2,1,0:T(8,128)}, f32[2,1024,128]{2,1,0:T(8,128)}, bf16[...) custom-call(s32[21]{0:T(128)} %pad_add_fusion.scalars, bf16[1024,128]{1,0:T(8,128)(2,1)} %get-tuple-element.66.q_keep, ...), custom_call_target="tpu_custom_call" | custom-call | flops 4026531840 | bytes 4194304 | tf_op jit(solution)/shard_map/window_grads/pallas_call | solution.py:198
  106.8 3.8 %collective-permute-start.16 = (bf16[2,1024,128]{2,1,0:T(8,128)(2,1)}, bf16[2,1024,128]{2,1,0:T(8,128)(2,1)S(1)}, u32[]{:S(2)}, u32[]{:S(2)}) collective-permute-start(bf16[2,1024,128]{2,1,0:T(8,128)(2,1)} %get-tuple-element.75), channel_id=1, source_target_pairs={{12,4},{0,8},{20,12},{8,16},{28,20},{16,24},{13,5},{1,9},{21,13},{... | collective-permute-start | bytes 1572872 | tf_op jit(solution)/shard_map/ppermute | solution.py:400
  113.2 6.0 %collective-permute-start.8 = (bf16[2,1024,128]{2,1,0:T(8,128)(2,1)}, bf16[2,1024,128]{2,1,0:T(8,128)(2,1)}, u32[]{:S(2)}, u32[]{:S(2)}) collective-permute-start(bf16[2,1024,128]{2,1,0:T(8,128)(2,1)} %collective-permute-done.7.kv_recv), channel_id=1, source_target_pairs={{0,8},{8,16},{12,4},{16,24},{20,12},{28,20},{1,9},{9,17},{13,5},{1... | collective-permute-start | bytes 1572872 | tf_op jit(solution)/shard_map/ppermute | solution.py:400
  119.2 4.0 %collective-permute-done.16.add_keep = bf16[2,1024,128]{2,1,0:T(8,128)(2,1)S(1)} collective-permute-done((bf16[2,1024,128]{2,1,0:T(8,128)(2,1)}, bf16[2,1024,128]{2,1,0:T(8,128)(2,1)S(1)}, u32[]{:S(2)}, u32[]{:S(2)}) %collective-permute-start.16) | collective-permute-done | bytes 524320 | tf_op jit(solution)/shard_map/ppermute | solution.py:400
  123.2 4.3 %collective-permute-done.17.add_recv = bf16[2,1024,128]{2,1,0:T(8,128)(2,1)S(1)} collective-permute-done((bf16[2,1024,128]{2,1,0:T(8,128)(2,1)}, bf16[2,1024,128]{2,1,0:T(8,128)(2,1)S(1)}, u32[]{:S(2)}, u32[]{:S(2)}) %collective-permute-start.17) | collective-permute-done | bytes 524320 | tf_op jit(solution)/shard_map/ppermute | solution.py:400
  132.6 3.8 %all-to-all-start.4 = ((bf16[8,3,256,128]{3,2,1,0:T(8,128)(2,1)}), bf16[8,3,256,128]{3,2,1,0:T(8,128)(2,1)S(1)}, u32[]{:S(2)}, u32[]{:S(2)}) async-start(bf16[8,3,256,128]{3,2,1,0:T(8,128)(2,1)} %merge.6), calls=%async_computation.4 | async-start | bytes 3145728 | tf_op jit(solution)/shard_map/all_to_all | solution.py:408
  138.5 23.8 %collective-permute-done.6.q_recv = bf16[1024,128]{1,0:T(8,128)(2,1)S(1)} collective-permute-done((bf16[1024,128]{1,0:T(8,128)(2,1)S(1)}, bf16[1024,128]{1,0:T(8,128)(2,1)S(1)}, u32[]{:S(2)}, u32[]{:S(2)}) %collective-permute-start.6) | collective-permute-done | bytes 262176 | tf_op jit(solution)/shard_map/ppermute | solution.py:400
  163.1 18.2 %window_grads.5 = (bf16[1024,128]{1,0:T(8,128)(2,1)}, bf16[1024,128]{1,0:T(8,128)(2,1)}, f32[2,1024,128]{2,1,0:T(8,128)}, f32[2,1024,128]{2,1,0:T(8,128)}, bf16[...) custom-call(s32[21]{0:T(128)} %pad_add_fusion.scalars, bf16[1024,128]{1,0:T(8,128)(2,1)} %get-tuple-element.56.q_keep, ...), custom_call_target="tpu_custom_call" | custom-call | flops 4026531840 | bytes 4194304 | tf_op jit(solution)/shard_map/window_grads/pallas_call | solution.py:198
  181.3 3.6 %collective-permute-start.10 = (bf16[2,1024,128]{2,1,0:T(8,128)(2,1)}, bf16[2,1024,128]{2,1,0:T(8,128)(2,1)S(1)}, u32[]{:S(2)}, u32[]{:S(2)}) collective-permute-start(bf16[2,1024,128]{2,1,0:T(8,128)(2,1)} %get-tuple-element.64), channel_id=1, source_target_pairs={{12,4},{0,8},{20,12},{8,16},{28,20},{16,24},{13,5},{1,9},{21,13},{... | collective-permute-start | bytes 1572872 | tf_op jit(solution)/shard_map/ppermute | solution.py:400
  187.5 6.0 %collective-permute-start.2 = (bf16[2,1024,128]{2,1,0:T(8,128)(2,1)}, bf16[2,1024,128]{2,1,0:T(8,128)(2,1)}, u32[]{:S(2)}, u32[]{:S(2)}) collective-permute-start(bf16[2,1024,128]{2,1,0:T(8,128)(2,1)} %collective-permute-done.1.kv_recv), channel_id=1, source_target_pairs={{0,8},{8,16},{12,4},{16,24},{20,12},{28,20},{1,9},{9,17},{13,5},{1... | collective-permute-start | bytes 1572872 | tf_op jit(solution)/shard_map/ppermute | solution.py:400
  193.6 4.0 %collective-permute-done.10.add_keep = bf16[2,1024,128]{2,1,0:T(8,128)(2,1)S(1)} collective-permute-done((bf16[2,1024,128]{2,1,0:T(8,128)(2,1)}, bf16[2,1024,128]{2,1,0:T(8,128)(2,1)S(1)}, u32[]{:S(2)}, u32[]{:S(2)}) %collective-permute-start.10) | collective-permute-done | bytes 524320 | tf_op jit(solution)/shard_map/ppermute | solution.py:400
  197.5 4.3 %collective-permute-done.11.add_recv = bf16[2,1024,128]{2,1,0:T(8,128)(2,1)S(1)} collective-permute-done((bf16[2,1024,128]{2,1,0:T(8,128)(2,1)}, bf16[2,1024,128]{2,1,0:T(8,128)(2,1)S(1)}, u32[]{:S(2)}, u32[]{:S(2)}) %collective-permute-start.11) | collective-permute-done | bytes 524320 | tf_op jit(solution)/shard_map/ppermute | solution.py:400
  205.9 4.0 %all-to-all-start.3 = ((bf16[8,3,256,128]{3,2,1,0:T(8,128)(2,1)}), bf16[8,3,256,128]{3,2,1,0:T(8,128)(2,1)S(1)}, u32[]{:S(2)}, u32[]{:S(2)}) async-start(bf16[8,3,256,128]{3,2,1,0:T(8,128)(2,1)} %merge.5), calls=%async_computation.3 | async-start | bytes 3145728 | tf_op jit(solution)/shard_map/all_to_all | solution.py:408
  211.6 23.6 %collective-permute-done.q_recv = bf16[1024,128]{1,0:T(8,128)(2,1)S(1)} collective-permute-done((bf16[1024,128]{1,0:T(8,128)(2,1)S(1)}, bf16[1024,128]{1,0:T(8,128)(2,1)S(1)}, u32[]{:S(2)}, u32[]{:S(2)}) %collective-permute-start) | collective-permute-done | bytes 262176 | tf_op jit(solution)/shard_map/ppermute | solution.py:400
  236.0 18.1 %window_grads.4 = (bf16[1024,128]{1,0:T(8,128)(2,1)}, bf16[1024,128]{1,0:T(8,128)(2,1)}, f32[2,1024,128]{2,1,0:T(8,128)}, f32[2,1024,128]{2,1,0:T(8,128)}, bf16[...) custom-call(s32[21]{0:T(128)} %pad_add_fusion.scalars, bf16[1024,128]{1,0:T(8,128)(2,1)} %get-tuple-element.45.q_keep, ...), custom_call_target="tpu_custom_call" | custom-call | flops 4026531840 | bytes 4194304 | tf_op jit(solution)/shard_map/window_grads/pallas_call | solution.py:198
  258.4 9.8 %collective-permute-done.4.add_keep = bf16[2,1024,128]{2,1,0:T(8,128)(2,1)S(1)} collective-permute-done((bf16[2,1024,128]{2,1,0:T(8,128)(2,1)}, bf16[2,1024,128]{2,1,0:T(8,128)(2,1)S(1)}, u32[]{:S(2)}, u32[]{:S(2)}) %collective-permute-start.4) | collective-permute-done | bytes 524320 | tf_op jit(solution)/shard_map/ppermute | solution.py:400
  268.2 4.0 %collective-permute-done.5.add_recv = bf16[2,1024,128]{2,1,0:T(8,128)(2,1)S(1)} collective-permute-done((bf16[2,1024,128]{2,1,0:T(8,128)(2,1)}, bf16[2,1024,128]{2,1,0:T(8,128)(2,1)S(1)}, u32[]{:S(2)}, u32[]{:S(2)}) %collective-permute-start.5) | collective-permute-done | bytes 524320 | tf_op jit(solution)/shard_map/ppermute | solution.py:400
  273.1 3.7 %merge.4 = bf16[8,4,256,128]{3,2,1,0:T(8,128)(2,1)} custom-call(s32[1]{0:T(128)} %bitcast.scalars, f32[2,1024,128]{2,1,0:T(8,128)} %get-tuple-element.50.own_keep, f32[2,1024,128]{2,1,0:T(8,128)} %get-tuple-element.51.own_recv, bf16[2,1024,128]{2,1,0:T(8,128)(2,1)} %copy-done.8, bf16[2,1024,128]{2,1,0:T(8,128)(2,1)} %copy-done.9, ...), custom_call_target="tpu_custom_call" | custom-call | tf_op jit(solution)/shard_map/merge/pallas_call | solution.py:334
  276.8 30.9 %all_to_all.30.refs_0_ = bf16[8,4,256,128]{3,2,1,0:T(8,128)(2,1)} all-to-all(bf16[8,4,256,128]{3,2,1,0:T(8,128)(2,1)} %merge.4), channel_id=1, replica_groups={{0,1,2,3,4,5,6,7},{8,9,10,11,12,13,14,15},{16,17,18,19,20,21,22,23},{24..., dimensions={0} | all-to-all | bytes 4194304 | tf_op jit(solution)/shard_map/all_to_all | solution.py:408
  307.7 6.6 %assemble.1 = (bf16[256,32,128]{2,1,0:T(8,128)(2,1)}, bf16[256,32,128]{2,1,0:T(8,128)(2,1)}, bf16[256,32,128]{2,1,0:T(8,128)(2,1)}) custom-call(bf16[8,4,256,128]{3,2,1,0:T(8,128)(2,1)} %all_to_all.30.refs_0_, bf16[8,3,256,128]{3,2,1,0:T(8,128)(2,1)} %copy-done.2, bf16[8,3,256,128]{3,2,1,0:T(8,128)(2,1)} %copy-done.1, bf16[8,2,256,128]{3,2,1,0:T(8,128)(2,1)} %copy-done.3), custom_call_target="tpu_custom_call" | custom-call | tf_op jit(solution)/shard_map/assemble/pallas_call | solution.py:367
  (98 shorter events, 44.2 us)
Async XLA Ops:
  5.9 18.3 %collective-permute-start.19 = (bf16[2,1024,128]{2,1,0:T(8,128)(2,1)}, bf16[2,1024,128]{2,1,0:T(8,128)(2,1)}, u32[]{:S(2)}, u32[]{:S(2)}) collective-permute-start(bf16[2,1024,128]{2,1,0:T(8,128)(2,1)} %get-tuple-element.79), channel_id=1, source_target_pairs={{0,4},{4,0},{8,12},{12,8},{16,20},{20,16},{24,28},{28,24},{1,5},{5... | collective-permute-start | bytes 1572872 | tf_op jit(solution)/shard_map/ppermute | solution.py:400
  14.0 19.1 %all-to-all-start.2 = ((bf16[8,2,256,128]{3,2,1,0:T(8,128)(2,1)}), bf16[8,2,256,128]{3,2,1,0:T(8,128)(2,1)S(1)}, u32[]{:S(2)}, u32[]{:S(2)}) async-start(bf16[8,2,256,128]{3,2,1,0:T(8,128)(2,1)} %get-tuple-element.68), calls=%async_computation.2 | async-start | bytes 2097152 | tf_op jit(solution)/shard_map/all_to_all | solution.py:408
  17.7 20.5 %collective-permute-start.21 = (bf16[2,1024,128]{2,1,0:T(8,128)(2,1)}, bf16[2,1024,128]{2,1,0:T(8,128)(2,1)}, u32[]{:S(2)}, u32[]{:S(2)}) collective-permute-start(bf16[2,1024,128]{2,1,0:T(8,128)(2,1)} %get-tuple-element.80.kv_keep), channel_id=1, source_target_pairs={{4,12},{8,0},{12,20},{16,8},{20,28},{24,16},{5,13},{9,1},{13,21},{... | collective-permute-start | bytes 1572872 | tf_op jit(solution)/shard_map/ppermute | solution.py:400
  19.1 19.2 %collective-permute-start.18 = (bf16[1024,128]{1,0:T(8,128)(2,1)S(1)}, bf16[1024,128]{1,0:T(8,128)(2,1)S(1)}, u32[]{:S(2)}, u32[]{:S(2)}) collective-permute-start(bf16[1024,128]{1,0:T(8,128)(2,1)S(1)} %copy-done.23), channel_id=1, source_target_pairs={{0,4},{4,0},{8,12},{12,8},{16,20},{20,16},{24,28},{28,24},{1,5},{5... | collective-permute-start | bytes 786440 | tf_op jit(solution)/shard_map/ppermute | solution.py:400
  24.0 40.1 %collective-permute-start.13 = (bf16[2,1024,128]{2,1,0:T(8,128)(2,1)S(1)}, bf16[2,1024,128]{2,1,0:T(8,128)(2,1)}, u32[]{:S(2)}, u32[]{:S(2)}) collective-permute-start(bf16[2,1024,128]{2,1,0:T(8,128)(2,1)S(1)} %copy-done.19), channel_id=1, source_target_pairs={{0,4},{4,0},{8,12},{12,8},{16,20},{20,16},{24,28},{28,24},{1,5},{5... | collective-permute-start | bytes 1572872 | tf_op jit(solution)/shard_map/ppermute | solution.py:400
  24.1 14.2 %collective-permute-start.20 = (bf16[2,1024,128]{2,1,0:T(8,128)(2,1)}, bf16[2,1024,128]{2,1,0:T(8,128)(2,1)}, u32[]{:S(2)}, u32[]{:S(2)}) collective-permute-start(bf16[2,1024,128]{2,1,0:T(8,128)(2,1)} %collective-permute-done.19.kv_recv), channel_id=1, source_target_pairs={{0,8},{8,16},{12,4},{16,24},{20,12},{28,20},{1,9},{9,17},{13,5},{1... | collective-permute-start | bytes 1572872 | tf_op jit(solution)/shard_map/ppermute | solution.py:400
  33.2 49.1 %all-to-all-start = ((bf16[8,2,256,128]{3,2,1,0:T(8,128)(2,1)}), bf16[8,2,256,128]{3,2,1,0:T(8,128)(2,1)S(1)}, u32[]{:S(2)}, u32[]{:S(2)}) async-start(bf16[8,2,256,128]{3,2,1,0:T(8,128)(2,1)} %get-tuple-element.47), calls=%async_computation | async-start | bytes 2097152 | tf_op jit(solution)/shard_map/all_to_all | solution.py:408
  39.0 31.1 %copy-start.22 = (bf16[1024,128]{1,0:T(8,128)(2,1)S(1)}, bf16[1024,128]{1,0:T(8,128)(2,1)}, u32[]{:S(2)}) copy-start(bf16[1024,128]{1,0:T(8,128)(2,1)} %get-tuple-element.67) | copy-start | bytes 786436
  57.3 16.8 %collective-permute-start.22 = (bf16[2,1024,128]{2,1,0:T(8,128)(2,1)}, bf16[2,1024,128]{2,1,0:T(8,128)(2,1)S(1)}, u32[]{:S(2)}, u32[]{:S(2)}) collective-permute-start(bf16[2,1024,128]{2,1,0:T(8,128)(2,1)} %get-tuple-element.85), channel_id=1, source_target_pairs={{12,4},{0,8},{20,12},{8,16},{28,20},{16,24},{13,5},{1,9},{21,13},{... | collective-permute-start | bytes 1572872 | tf_op jit(solution)/shard_map/ppermute | solution.py:400
  61.5 16.9 %collective-permute-start.23 = (bf16[2,1024,128]{2,1,0:T(8,128)(2,1)}, bf16[2,1024,128]{2,1,0:T(8,128)(2,1)S(1)}, u32[]{:S(2)}, u32[]{:S(2)}) collective-permute-start(bf16[2,1024,128]{2,1,0:T(8,128)(2,1)} %get-tuple-element.86), channel_id=1, source_target_pairs={{8,0},{16,8},{4,12},{24,16},{12,20},{20,28},{9,1},{17,9},{5,13},{2... | collective-permute-start | bytes 1572872 | tf_op jit(solution)/shard_map/ppermute | solution.py:400
  62.8 25.6 %collective-permute-start.15 = (bf16[2,1024,128]{2,1,0:T(8,128)(2,1)S(1)}, bf16[2,1024,128]{2,1,0:T(8,128)(2,1)}, u32[]{:S(2)}, u32[]{:S(2)}) collective-permute-start(bf16[2,1024,128]{2,1,0:T(8,128)(2,1)S(1)} %copy-done.18), channel_id=1, source_target_pairs={{4,12},{8,0},{12,20},{16,8},{20,28},{24,16},{5,13},{9,1},{13,21},{... | collective-permute-start | bytes 1572872 | tf_op jit(solution)/shard_map/ppermute | solution.py:400
  64.1 24.3 %collective-permute-start.14 = (bf16[2,1024,128]{2,1,0:T(8,128)(2,1)}, bf16[2,1024,128]{2,1,0:T(8,128)(2,1)}, u32[]{:S(2)}, u32[]{:S(2)}) collective-permute-start(bf16[2,1024,128]{2,1,0:T(8,128)(2,1)} %collective-permute-done.13.kv_recv), channel_id=1, source_target_pairs={{0,8},{8,16},{12,4},{16,24},{20,12},{28,20},{1,9},{9,17},{13,5},{1... | collective-permute-start | bytes 1572872 | tf_op jit(solution)/shard_map/ppermute | solution.py:400
  70.1 17.8 %collective-permute-start.12 = (bf16[1024,128]{1,0:T(8,128)(2,1)S(1)}, bf16[1024,128]{1,0:T(8,128)(2,1)}, u32[]{:S(2)}, u32[]{:S(2)}) collective-permute-start(bf16[1024,128]{1,0:T(8,128)(2,1)S(1)} %copy-done.22), channel_id=1, source_target_pairs={{0,4},{4,0},{8,12},{12,8},{16,20},{20,16},{24,28},{28,24},{1,5},{5... | collective-permute-start | bytes 786440 | tf_op jit(solution)/shard_map/ppermute | solution.py:400
  82.3 49.3 %all-to-all-start.5 = ((bf16[8,2,256,128]{3,2,1,0:T(8,128)(2,1)}), bf16[8,2,256,128]{3,2,1,0:T(8,128)(2,1)S(1)}, u32[]{:S(2)}, u32[]{:S(2)}) async-start(bf16[8,2,256,128]{3,2,1,0:T(8,128)(2,1)} %merge.7), calls=%async_computation.5 | async-start | bytes 2097152 | tf_op jit(solution)/shard_map/all_to_all | solution.py:408
  86.2 27.0 %collective-permute-start.7 = (bf16[2,1024,128]{2,1,0:T(8,128)(2,1)S(1)}, bf16[2,1024,128]{2,1,0:T(8,128)(2,1)}, u32[]{:S(2)}, u32[]{:S(2)}) collective-permute-start(bf16[2,1024,128]{2,1,0:T(8,128)(2,1)S(1)} %copy-done.17), channel_id=1, source_target_pairs={{0,4},{4,0},{8,12},{12,8},{16,20},{20,16},{24,28},{28,24},{1,5},{5... | collective-permute-start | bytes 1572872 | tf_op jit(solution)/shard_map/ppermute | solution.py:400
  106.8 16.4 %collective-permute-start.16 = (bf16[2,1024,128]{2,1,0:T(8,128)(2,1)}, bf16[2,1024,128]{2,1,0:T(8,128)(2,1)S(1)}, u32[]{:S(2)}, u32[]{:S(2)}) collective-permute-start(bf16[2,1024,128]{2,1,0:T(8,128)(2,1)} %get-tuple-element.75), channel_id=1, source_target_pairs={{12,4},{0,8},{20,12},{8,16},{28,20},{16,24},{13,5},{1,9},{21,13},{... | collective-permute-start | bytes 1572872 | tf_op jit(solution)/shard_map/ppermute | solution.py:400
  110.6 16.9 %collective-permute-start.17 = (bf16[2,1024,128]{2,1,0:T(8,128)(2,1)}, bf16[2,1024,128]{2,1,0:T(8,128)(2,1)S(1)}, u32[]{:S(2)}, u32[]{:S(2)}) collective-permute-start(bf16[2,1024,128]{2,1,0:T(8,128)(2,1)} %get-tuple-element.76), channel_id=1, source_target_pairs={{8,0},{16,8},{4,12},{24,16},{12,20},{20,28},{9,1},{17,9},{5,13},{2... | collective-permute-start | bytes 1572872 | tf_op jit(solution)/shard_map/ppermute | solution.py:400
  111.9 50.5 %collective-permute-start.9 = (bf16[2,1024,128]{2,1,0:T(8,128)(2,1)S(1)}, bf16[2,1024,128]{2,1,0:T(8,128)(2,1)}, u32[]{:S(2)}, u32[]{:S(2)}) collective-permute-start(bf16[2,1024,128]{2,1,0:T(8,128)(2,1)S(1)} %copy-done.16), channel_id=1, source_target_pairs={{4,12},{8,0},{12,20},{16,8},{20,28},{24,16},{5,13},{9,1},{13,21},{... | collective-permute-start | bytes 1572872 | tf_op jit(solution)/shard_map/ppermute | solution.py:400
  113.2 49.2 %collective-permute-start.8 = (bf16[2,1024,128]{2,1,0:T(8,128)(2,1)}, bf16[2,1024,128]{2,1,0:T(8,128)(2,1)}, u32[]{:S(2)}, u32[]{:S(2)}) collective-permute-start(bf16[2,1024,128]{2,1,0:T(8,128)(2,1)} %collective-permute-done.7.kv_recv), channel_id=1, source_target_pairs={{0,8},{8,16},{12,4},{16,24},{20,12},{28,20},{1,9},{9,17},{13,5},{1... | collective-permute-start | bytes 1572872 | tf_op jit(solution)/shard_map/ppermute | solution.py:400
  132.6 73.3 %all-to-all-start.4 = ((bf16[8,3,256,128]{3,2,1,0:T(8,128)(2,1)}), bf16[8,3,256,128]{3,2,1,0:T(8,128)(2,1)S(1)}, u32[]{:S(2)}, u32[]{:S(2)}) async-start(bf16[8,3,256,128]{3,2,1,0:T(8,128)(2,1)} %merge.6), calls=%async_computation.4 | async-start | bytes 3145728 | tf_op jit(solution)/shard_map/all_to_all | solution.py:408
  136.4 25.9 %collective-permute-start.6 = (bf16[1024,128]{1,0:T(8,128)(2,1)S(1)}, bf16[1024,128]{1,0:T(8,128)(2,1)S(1)}, u32[]{:S(2)}, u32[]{:S(2)}) collective-permute-start(bf16[1024,128]{1,0:T(8,128)(2,1)S(1)} %copy-done.21), channel_id=1, source_target_pairs={{0,4},{4,0},{8,12},{12,8},{16,20},{20,16},{24,28},{28,24},{1,5},{5... | collective-permute-start | bytes 786440 | tf_op jit(solution)/shard_map/ppermute | solution.py:400
  138.2 49.4 %collective-permute-start.1 = (bf16[2,1024,128]{2,1,0:T(8,128)(2,1)S(1)}, bf16[2,1024,128]{2,1,0:T(8,128)(2,1)}, u32[]{:S(2)}, u32[]{:S(2)}) collective-permute-start(bf16[2,1024,128]{2,1,0:T(8,128)(2,1)S(1)} %copy-done.15), channel_id=1, source_target_pairs={{0,4},{4,0},{8,12},{12,8},{16,20},{20,16},{24,28},{28,24},{1,5},{5... | collective-permute-start | bytes 1572872 | tf_op jit(solution)/shard_map/ppermute | solution.py:400
  181.3 16.2 %collective-permute-start.10 = (bf16[2,1024,128]{2,1,0:T(8,128)(2,1)}, bf16[2,1024,128]{2,1,0:T(8,128)(2,1)S(1)}, u32[]{:S(2)}, u32[]{:S(2)}) collective-permute-start(bf16[2,1024,128]{2,1,0:T(8,128)(2,1)} %get-tuple-element.64), channel_id=1, source_target_pairs={{12,4},{0,8},{20,12},{8,16},{28,20},{16,24},{13,5},{1,9},{21,13},{... | collective-permute-start | bytes 1572872 | tf_op jit(solution)/shard_map/ppermute | solution.py:400
  184.9 16.9 %collective-permute-start.11 = (bf16[2,1024,128]{2,1,0:T(8,128)(2,1)}, bf16[2,1024,128]{2,1,0:T(8,128)(2,1)S(1)}, u32[]{:S(2)}, u32[]{:S(2)}) collective-permute-start(bf16[2,1024,128]{2,1,0:T(8,128)(2,1)} %get-tuple-element.65), channel_id=1, source_target_pairs={{8,0},{16,8},{4,12},{24,16},{12,20},{20,28},{9,1},{17,9},{5,13},{2... | collective-permute-start | bytes 1572872 | tf_op jit(solution)/shard_map/ppermute | solution.py:400
  186.2 49.8 %collective-permute-start.3 = (bf16[2,1024,128]{2,1,0:T(8,128)(2,1)}, bf16[2,1024,128]{2,1,0:T(8,128)(2,1)}, u32[]{:S(2)}, u32[]{:S(2)}) collective-permute-start(bf16[2,1024,128]{2,1,0:T(8,128)(2,1)} %get-tuple-element.49.kv_keep), channel_id=1, source_target_pairs={{4,12},{8,0},{12,20},{16,8},{20,28},{24,16},{5,13},{9,1},{13,21},{... | collective-permute-start | bytes 1572872 | tf_op jit(solution)/shard_map/ppermute | solution.py:400
  187.5 48.5 %collective-permute-start.2 = (bf16[2,1024,128]{2,1,0:T(8,128)(2,1)}, bf16[2,1024,128]{2,1,0:T(8,128)(2,1)}, u32[]{:S(2)}, u32[]{:S(2)}) collective-permute-start(bf16[2,1024,128]{2,1,0:T(8,128)(2,1)} %collective-permute-done.1.kv_recv), channel_id=1, source_target_pairs={{0,8},{8,16},{12,4},{16,24},{20,12},{28,20},{1,9},{9,17},{13,5},{1... | collective-permute-start | bytes 1572872 | tf_op jit(solution)/shard_map/ppermute | solution.py:400
  205.9 48.2 %copy-start.1 = (bf16[8,3,256,128]{3,2,1,0:T(8,128)(2,1)}, bf16[8,3,256,128]{3,2,1,0:T(8,128)(2,1)S(1)}, u32[]{:S(2)}) copy-start(bf16[8,3,256,128]{3,2,1,0:T(8,128)(2,1)S(1)} %all-to-all-done.4.refs_2_) | copy-start | bytes 4718596
  205.9 70.8 %all-to-all-start.3 = ((bf16[8,3,256,128]{3,2,1,0:T(8,128)(2,1)}), bf16[8,3,256,128]{3,2,1,0:T(8,128)(2,1)S(1)}, u32[]{:S(2)}, u32[]{:S(2)}) async-start(bf16[8,3,256,128]{3,2,1,0:T(8,128)(2,1)} %merge.5), calls=%async_computation.3 | async-start | bytes 3145728 | tf_op jit(solution)/shard_map/all_to_all | solution.py:408
  209.9 25.3 %collective-permute-start = (bf16[1024,128]{1,0:T(8,128)(2,1)S(1)}, bf16[1024,128]{1,0:T(8,128)(2,1)S(1)}, u32[]{:S(2)}, u32[]{:S(2)}) collective-permute-start(bf16[1024,128]{1,0:T(8,128)(2,1)S(1)} %copy-done.20), channel_id=1, source_target_pairs={{0,4},{4,0},{8,12},{12,8},{16,20},{20,16},{24,28},{28,24},{1,5},{5... | collective-permute-start | bytes 786440 | tf_op jit(solution)/shard_map/ppermute | solution.py:400
  254.2 14.1 %collective-permute-start.4 = (bf16[2,1024,128]{2,1,0:T(8,128)(2,1)}, bf16[2,1024,128]{2,1,0:T(8,128)(2,1)S(1)}, u32[]{:S(2)}, u32[]{:S(2)}) collective-permute-start(bf16[2,1024,128]{2,1,0:T(8,128)(2,1)} %get-tuple-element.52), channel_id=1, source_target_pairs={{12,4},{0,8},{20,12},{8,16},{28,20},{16,24},{13,5},{1,9},{21,13},{... | collective-permute-start | bytes 1572872 | tf_op jit(solution)/shard_map/ppermute | solution.py:400
  257.1 15.2 %collective-permute-start.5 = (bf16[2,1024,128]{2,1,0:T(8,128)(2,1)}, bf16[2,1024,128]{2,1,0:T(8,128)(2,1)S(1)}, u32[]{:S(2)}, u32[]{:S(2)}) collective-permute-start(bf16[2,1024,128]{2,1,0:T(8,128)(2,1)} %get-tuple-element.53), channel_id=1, source_target_pairs={{8,0},{16,8},{4,12},{24,16},{12,20},{20,28},{9,1},{17,9},{5,13},{2... | collective-permute-start | bytes 1572872 | tf_op jit(solution)/shard_map/ppermute | solution.py:400
  276.8 30.9 %copy-start.2 = (bf16[8,3,256,128]{3,2,1,0:T(8,128)(2,1)}, bf16[8,3,256,128]{3,2,1,0:T(8,128)(2,1)S(1)}, u32[]{:S(2)}) copy-start(bf16[8,3,256,128]{3,2,1,0:T(8,128)(2,1)S(1)} %all-to-all-done.3.refs_1_) | copy-start | bytes 4718596
  (24 other events, 176.7 us)

commit v2 on v1

--- a/solution.py
+++ b/solution.py
@@ -17,9 +17,33 @@
 SPAN = WIN_COLS * TILE
 NEG = -1e30
 
+ALL_VMEM = pltpu.CompilerParams(vmem_limit_bytes=67_043_328)
+
+
+def chunk_groups(chunks):
+    first = max(1, chunks // 2)
+    return [range(first)] + ([range(first, chunks)] if first < chunks else [])
+
+
+def lead_groups(chunks):
+    return [range(1)] + ([range(1, chunks)] if chunks > 1 else [])
+
+
+def query_groups(chunks):
+    bounds = [0, 1, 2, chunks]
+    return [range(a, min(b, chunks)) for a, b in zip(bounds, bounds[1:]) if a < min(b, chunks)]
+
+
+def group_of(groups, chunk):
+    return next(index for index, members in enumerate(groups) if chunk in members)
+
+
+def place_of(groups, chunk):
+    return groups[group_of(groups, chunk)].index(chunk)
+
 
 def attention_kernel(
-    place_in_group,
+    chunk,
     scalars,
     q_keep,
     q_recv,
@@ -46,10 +70,16 @@
     dp_buf,
     sems,
 ):
-    tok, head_dim = q_keep.shape
+    _, tok, head_dim = q_keep.shape
+    chunks = q_keep.shape[0]
     scale = head_dim ** (-0.5)
     parity = scalars[2 * TPS + 4]
     senders, _, part, _ = do_ref.shape
+    do_place = place_of(chunk_groups(chunks), chunk)
+    place = place_of(lead_groups(chunks), chunk)
+    kv_keep, kv_high = kv_keep.at[place], kv_high.at[place]
+    q_recv = q_recv.at[place_of(query_groups(chunks), chunk)]
+    q_keep = q_keep.at[chunk]
     count = 0
 
     def begin(source, target):
@@ -66,7 +96,7 @@
             loads += [begin(q_keep, q_buf.at[pl.ds(0, tok), :])]
             for sender in range(senders):
                 rows_do = pl.ds(sender * part, part)
-                loads += [begin(do_ref.at[sender, place_in_group], do_buf.at[rows_do, :])]
+                loads += [begin(do_ref.at[sender, do_place], do_buf.at[rows_do, :])]
         late = [begin(ref.at[0], k_buf.at[rows, :]), begin(ref.at[1], v_buf.at[rows, :])]
         loads += late if slot < 3 else []
     late += [begin(q_recv, q_buf.at[pl.ds(tok, tok), :])]
@@ -146,37 +176,40 @@
         for place, start in enumerate(q_starts):
             q_buf[pl.ds(start, TILE), :] = dq[place * TILE : (place + 1) * TILE]
 
-    def step(index, carry):
-        side = index // GW
-        column = index % GW
-        first = scalars[side * TPS + column]
-        second = scalars[side * TPS + GW + column]
-        start0 = pl.multiple_of(side * tok + column * TILE, TILE)
-        start1 = pl.multiple_of(side * tok + (GW + column) * TILE, TILE)
-
-        @pl.when(first == second)
-        def _():
-            unit(side, first, [start0, start1])
-
-        @pl.when(first != second)
-        def _():
-            def single(which, inner):
-                start = pl.multiple_of(start0 + which * (GW * TILE), TILE)
-                unit(side, jnp.where(which == 0, first, second), [start])
-                return inner
-
-            lax.fori_loop(0, GH, single, 0)
-
-        return carry
-
-    lax.fori_loop(0, GW, step, 0)
+    def run_side(side):
+        def tile_at(index):
+            column, which = index // GH, index % GH
+            first = scalars[side * TPS + column]
+            second = scalars[side * TPS + GW + column]
+            row = jnp.where(first <= second, which, GH - 1 - which)
+            start = side * tok + (row * GW + column) * TILE
+            return jnp.where(row == 0, first, second), pl.multiple_of(start, TILE)
+
+        def step(index):
+            col, start = tile_at(index)
+            next_col, next_start = tile_at(jnp.minimum(index + 1, TPS - 1))
+            double = (index + 1 < TPS) & (col == next_col)
+
+            @pl.when(double)
+            def _():
+                unit(side, col, [start, next_start])
+
+            @pl.when(jnp.logical_not(double))
+            def _():
+                unit(side, col, [start])
+
+            return index + 1 + double.astype(jnp.int32)
+
+        lax.while_loop(lambda index: index < TPS, step, jnp.int32(0))
+
+    run_side(0)
     for copy in late:
         copy.wait()
     stores = [begin(q_buf.at[pl.ds(0, tok), :], dq_keep)]
     low_buf[0] = (dk_acc[pl.ds(0, tok), :] * scale).astype(low_buf.dtype)
     low_buf[1] = dv_acc[pl.ds(0, tok), :].astype(low_buf.dtype)
     stores += [begin(low_buf, half_low)]
-    lax.fori_loop(GW, 2 * GW, step, 0)
+    run_side(1)
     stores += [begin(q_buf.at[pl.ds(tok, tok), :], dq_recv)]
     for slot, ref in ((1, own_keep), (2, own_recv)):
         rows = pl.ds(slot * tok, tok)
@@ -188,15 +221,15 @@
         copy.wait()
 
 
-def attention_call(scalars, place_in_group, q_keep, q_recv, do_all, kv_low, kv_keep, kv_recv, kv_high):
-    tok, head_dim = q_keep.shape
-    senders, _, _, _ = do_all.shape
+def attention_call(scalars, chunk, q_keep, q_recv, do_all, kv_low, kv_keep, kv_recv, kv_high):
+    _, tok, head_dim = q_keep.shape
+    senders = do_all.shape[0]
     place = pl.BlockSpec(memory_space=pl.ANY)
     keys_all = 4 * tok
     window = 3 * GH * SPAN
     pairs = 2 * TPS * TILE * window
     return pl.pallas_call(
-        functools.partial(attention_kernel, place_in_group),
+        functools.partial(attention_kernel, chunk),
         out_shape=(jax.ShapeDtypeStruct((tok, head_dim), jnp.bfloat16),) * 2
         + (jax.ShapeDtypeStruct((2, tok, head_dim), jnp.float32),) * 2
         + (jax.ShapeDtypeStruct((2, tok, head_dim), jnp.bfloat16),) * 2,
@@ -218,19 +251,22 @@
         cost_estimate=pl.CostEstimate(
             flops=10 * pairs * head_dim, transcendentals=pairs, bytes_accessed=16 * tok * head_dim * 2
         ),
+        compiler_params=ALL_VMEM,
         name="window_grads",
     )(scalars, q_keep, q_recv, do_all, kv_low, kv_keep, kv_recv, kv_high)
 
 
 def split_kernel(scalars, *refs):
     (first, second), outs, held = refs[:2], refs[2:-1], refs[-1]
-    chunks = len(outs) // 2
+    chunks = held.shape[0] // 2
+    groups = lead_groups(chunks)
     side = scalars[0]
     for place, ref in enumerate((first, second)):
         held[...] = jnp.swapaxes(ref[...], 0, 1)
         for chunk in range(chunks):
             outs[chunk][place] = held[(1 - side) * chunks + chunk]
-            outs[chunks + chunk][place] = held[side * chunks + chunk]
+            kept = outs[chunks + group_of(groups, chunk)]
+            kept[place_of(groups, chunk), place] = held[side * chunks + chunk]
 
 
 def split_pair(scalars, first, second):
@@ -238,23 +274,22 @@
     steps = TPS // 2
     block = tok // steps
     chunks = heads_here // 2
+    sizes = [len(members) for members in lead_groups(chunks)]
     spec = pl.BlockSpec((block, heads_here, head_dim), lambda i: (i, 0, 0))
     out_spec = pl.BlockSpec((2, block, head_dim), lambda i: (0, i, 0))
     outs = pl.pallas_call(
         split_kernel,
         grid=(steps,),
-        out_shape=(jax.ShapeDtypeStruct((2, tok, head_dim), first.dtype),) * (2 * chunks),
+        out_shape=(jax.ShapeDtypeStruct((2, tok, head_dim), first.dtype),) * chunks
+        + tuple(jax.ShapeDtypeStruct((size, 2, tok, head_dim), first.dtype) for size in sizes),
         in_specs=[pl.BlockSpec(memory_space=pltpu.SMEM), spec, spec],
-        out_specs=(out_spec,) * (2 * chunks),
+        out_specs=(out_spec,) * chunks
+        + tuple(pl.BlockSpec((size, 2, block, head_dim), lambda i: (0, 0, i, 0)) for size in sizes),
         scratch_shapes=[pltpu.VMEM((heads_here, block, head_dim), first.dtype)],
+        compiler_params=ALL_VMEM,
         name="split_pair",
     )(scalars, first, second)
     return outs[:chunks], outs[chunks:]
-
-
-def chunk_groups(chunks):
-    first = max(1, chunks // 2)
-    return [range(first)] + ([range(first, chunks)] if first < chunks else [])
 
 
 def spread_kernel(scalars, queries, out_grad, *refs):
@@ -263,12 +298,13 @@
     heads_here = held_q.shape[0]
     chunks = heads_here // 2
     row_count = held_do.shape[0] // heads_here
+    leads = query_groups(chunks)
     held_q[...] = jnp.swapaxes(queries[...], 0, 1)
-    for chunk in range(chunks):
-        outs[chunk][...] = held_q[(1 - side) * chunks + chunk]
-        outs[chunks + chunk][...] = held_q[side * chunks + chunk]
+    outs[0][...] = held_q[pl.ds(side * chunks, chunks)]
+    for index, members in enumerate(leads):
+        outs[1 + index][...] = held_q[pl.ds((1 - side) * chunks + members[0], len(members))]
     held_do[...] = jnp.swapaxes(out_grad[...], 0, 1)
-    for out, members in zip(outs[2 * chunks :], chunk_groups(chunks)):
+    for out, members in zip(outs[1 + len(leads) :], chunk_groups(chunks)):
         for group in range(2):
             for row in range(row_count):
                 head = row * heads_here + group * chunks + members[0]
@@ -281,31 +317,38 @@
     steps = min(TPS // 2, part // 16)
     chunks = heads_here // 2
     targets = 2 * heads // heads_here
-    sizes = [len(members) for members in chunk_groups(chunks)]
+    q_sizes = [chunks] + [len(members) for members in query_groups(chunks)]
+    do_sizes = [len(members) for members in chunk_groups(chunks)]
     outs = pl.pallas_call(
         spread_kernel,
         grid=(steps,),
-        out_shape=(jax.ShapeDtypeStruct((tok, head_dim), queries.dtype),) * (2 * chunks)
+        out_shape=tuple(
+            jax.ShapeDtypeStruct((size, tok, head_dim), queries.dtype) for size in q_sizes
+        )
         + tuple(
-            jax.ShapeDtypeStruct((targets, size, part, head_dim), queries.dtype) for size in sizes
+            jax.ShapeDtypeStruct((targets, size, part, head_dim), queries.dtype)
+            for size in do_sizes
         ),
         in_specs=[
             pl.BlockSpec(memory_space=pltpu.SMEM),
             pl.BlockSpec((tok // steps, heads_here, head_dim), lambda i: (i, 0, 0)),
             pl.BlockSpec((part // steps, heads, head_dim), lambda i: (i, 0, 0)),
         ],
-        out_specs=(pl.BlockSpec((tok // steps, head_dim), lambda i: (i, 0)),) * (2 * chunks)
+        out_specs=tuple(
+            pl.BlockSpec((size, tok // steps, head_dim), lambda i: (0, i, 0)) for size in q_sizes
+        )
         + tuple(
             pl.BlockSpec((targets, size, part // steps, head_dim), lambda i: (0, 0, i, 0))
-            for size in sizes
+            for size in do_sizes
         ),
         scratch_shapes=[
             pltpu.VMEM((heads_here, tok // steps, head_dim), queries.dtype),
             pltpu.VMEM((heads, part // steps, head_dim), queries.dtype),
         ],
+        compiler_params=ALL_VMEM,
         name="spread",
     )(scalars, queries, out_grad)
-    return outs[:chunks], outs[chunks : 2 * chunks], outs[2 * chunks :]
+    return outs[0], outs[1 : len(q_sizes)], outs[len(q_sizes) :]
 
 
 def merge_kernel(scalars, own_keep, own_recv, add_keep, add_recv, *refs):
@@ -336,6 +379,7 @@
         out_shape=jax.ShapeDtypeStruct(shape, jnp.bfloat16),
         in_specs=[pl.BlockSpec(memory_space=pltpu.SMEM)] + [vmem] * (4 + len(flat)),
         out_specs=vmem,
+        compiler_params=ALL_VMEM,
         name="merge",
     )(scalars, own_keep, own_recv, add_keep, add_recv, *flat)
 
@@ -344,13 +388,13 @@
     return (0, 2) if chunk == 0 else (chunk - 1, 3 if chunk == 1 else 2)
 
 
-def assemble_kernel(*refs):
-    chunks = len(refs) - 4
-    pieces, outs, held = refs[:chunks], refs[chunks:-1], refs[-1]
+def assemble_kernel(sources, *refs):
+    count = len(refs) - 1 - len(sources)
+    pieces, outs, held = refs[:count], refs[count:-1], refs[-1]
     row_count = pieces[0].shape[0] // 2
-    for index, out in enumerate(outs):
-        for chunk in range(chunks):
-            message, plane = query_place(chunk) if index == 0 else (chunk, index - 1)
+    for source, out in zip(sources, outs):
+        chunks = len(source)
+        for chunk, (message, plane) in enumerate(source):
             for group in range(2):
                 for row in range(row_count):
                     head = row * 2 * chunks + group * chunks + chunk
@@ -358,22 +402,22 @@
         out[...] = jnp.swapaxes(held[...], 0, 1)
 
 
-def assemble(pieces):
-    chunks = len(pieces)
+def assemble(pieces, sources):
     senders, _, part, head_dim = pieces[0].shape
-    heads = chunks * senders
+    heads = len(sources[0]) * senders
     steps = min(TPS // 2, part // 16)
     block = part // steps
     return pl.pallas_call(
-        assemble_kernel,
+        functools.partial(assemble_kernel, sources),
         grid=(steps,),
-        out_shape=(jax.ShapeDtypeStruct((part, heads, head_dim), jnp.bfloat16),) * 3,
+        out_shape=(jax.ShapeDtypeStruct((part, heads, head_dim), jnp.bfloat16),) * len(sources),
         in_specs=[
             pl.BlockSpec((senders, piece.shape[1], block, head_dim), lambda i: (0, 0, i, 0))
             for piece in pieces
         ],
-        out_specs=(pl.BlockSpec((block, heads, head_dim), lambda i: (i, 0, 0)),) * 3,
+        out_specs=(pl.BlockSpec((block, heads, head_dim), lambda i: (i, 0, 0)),) * len(sources),
         scratch_shapes=[pltpu.VMEM((heads, block, head_dim), jnp.bfloat16)],
+        compiler_params=ALL_VMEM,
         name="assemble",
     )(*pieces)
 
@@ -429,22 +473,20 @@
         ]
     )
 
+    leads, do_groups = lead_groups(chunks), chunk_groups(chunks)
     kv_sent, kv_keep = split_pair(places, keys, values)
-    q_sent, q_keep, do_sent = spread(places, queries, out_grad)
-    do_of = {}
-    for index, members in enumerate(chunk_groups(chunks)):
-        arrived = to_all(do_sent[index])
-        for place, chunk in enumerate(members):
-            do_of[chunk] = (place, arrived)
+    q_keep, q_sent, do_sent = spread(places, queries, out_grad)
+    do_recv = [to_all(sent) for sent in do_sent]
+    kv_high = [over_slab(kept, out_high) for kept in kv_keep]
+    q_recv = [over_slab(sent, swap) for sent in q_sent]
     inputs = []
     for chunk in range(chunks):
         kv_recv = over_slab(kv_sent[chunk], swap)
-        kv_high = over_slab(kv_keep[chunk], out_high)
         kv_low = over_slab(kv_recv, out_low)
-        q_recv = over_slab(q_sent[chunk], swap)
-        place, do_all = do_of[chunk]
+        lead, do_all = group_of(leads, chunk), do_recv[group_of(do_groups, chunk)]
+        q_other = q_recv[group_of(query_groups(chunks), chunk)]
         inputs.append(
-            (place, q_keep[chunk], q_recv, do_all, kv_low, kv_keep[chunk], kv_recv, kv_high)
+            (chunk, q_keep, q_other, do_all, kv_low, kv_keep[lead], kv_recv, kv_high[lead])
         )
 
     query_grads = []
@@ -462,7 +504,13 @@
         own = [query_grads[other] for other in range(chunks) if query_place(other)[0] == chunk]
         merged = merge(places, row_count, *partial_sums[chunk], own)
         pieces.append(to_all(merged))
-    return tuple(assemble(pieces))
+    query_sources = [query_place(chunk) for chunk in range(chunks)]
+    used = 1 + max(message for message, _ in query_sources)
+    (query_grad,) = assemble(pieces[:used], [query_sources])
+    key_grad, value_grad = assemble(
+        pieces, [[(chunk, plane) for chunk in range(chunks)] for plane in range(2)]
+    )
+    return query_grad, key_grad, value_grad
 
 
 def solution(mesh):

time: 316 us -> 291 us (0.921)
  the two profiles are of different devices: /device:TPU:0 before, /device:TPU:24 now
where the time goes in v2:
time: 291 us; the launch traced here: 287 us
  Pallas kernels  105 us (36%)
  waiting for transfers between devices  103 us (35%)
  starting transfers between devices  73.4 us (25%)
  local copies, waits for them, and re-layouts  3.17 us (1%)
    ppermute x21, waiting for transfers between devices, over_slab(): return lax.ppermute(array, 'slab', pairs)  81.7 us
    pallas_call x4, Pallas kernels, attention_call(): pl.pallas_call(functools.partial(attention_kernel, chunk), out_shape=(jax...  71 us
    ppermute x21, starting transfers between devices, over_slab(): return lax.ppermute(array, 'slab', pairs)  43 us
    all_to_all x6, starting transfers between devices, to_all(): lax.all_to_all(array, ('slab', 'row'), 0, 0, axis_index_groups=groups, ti...  30.4 us
    all_to_all x6, waiting for transfers between devices, to_all(): lax.all_to_all(array, ('slab', 'row'), 0, 0, axis_index_groups=groups, ti...  21.7 us
    pallas_call x4, Pallas kernels, merge(): pl.pallas_call(merge_kernel, out_shape=jax.ShapeDtypeStruct(shape, jnp.bf...  13.4 us
    pallas_call x2, Pallas kernels, assemble(): pl.pallas_call(functools.partial(assemble_kernel, sources), grid=(steps,)...  10.2 us
  transfers between devices with their start and end apart: 27, of which 11 were waited for; matrix products, arithmetic and copies ran while one was open for 1% of the time, Pallas kernels for 33%

profile of v2, /device:TPU:24, one launch (start us, length us, event | category | flops | bytes accessed | tf_op | source)
XLA Modules:
  0.0 286.9 jit_solution(10888323432528915522)
XLA Ops:
  0.6 5.2 %split_pair.1 = (bf16[2,1024,128]{2,1,0:T(8,128)(2,1)}, bf16[2,1024,128]{2,1,0:T(8,128)(2,1)}, bf16[2,1024,128]{2,1,0:T(8,128)(2,1)}, bf16[2,1024,128]{2,1,0:T(8...) custom-call(s32[1]{0:T(128)} %bitcast.scalars, bf16[1024,8,128]{2,1,0:T(8,128)(2,1)} %refs_0_.1, ...), custom_call_target="tpu_custom_call" | custom-call | tf_op jit(solution)/shard_map/split_pair/pallas_call | solution.py:280
  7.4 3.5 %collective-permute-start.9 = (bf16[3,2,1024,128]{3,2,1,0:T(8,128)(2,1)}, bf16[3,2,1024,128]{3,2,1,0:T(8,128)(2,1)}, u32[]{:S(2)}, u32[]{:S(2)}) collective-permute-start(bf16[3,2,1024,128]{3,2,1,0:T(8,128)(2,1)} %get-tuple-element.54.kv_keep), channel_id=1, source_target_pairs={{4,12},{8,0},{12,20},{16,8},{20,28},{24,16},{5,13},{9,1},{13,21},{... | collective-permute-start | bytes 4718600 | tf_op jit(solution)/shard_map/ppermute | solution.py:444
  10.9 5.5 %spread.1 = (bf16[4,1024,128]{2,1,0:T(8,128)(2,1)}, bf16[1,1024,128]{2,1,0:T(8,128)(2,1)}, bf16[1,1024,128]{2,1,0:T(8,128)(2,1)}, bf16[2,1024,128]{2,1,0:T(8,128...) custom-call(s32[1]{0:T(128)} %bitcast.scalars, bf16[1024,8,128]{2,1,0:T(8,128)(2,1)} %queries.1, ...), custom_call_target="tpu_custom_call" | custom-call | tf_op jit(solution)/shard_map/spread/pallas_call | solution.py:322
  16.4 4.4 %all-to-all-start = ((bf16[8,2,256,128]{3,2,1,0:T(8,128)(2,1)}), bf16[8,2,256,128]{3,2,1,0:T(8,128)(2,1)}, u32[]{:S(2)}, u32[]{:S(2)}) async-start(bf16[8,2,256,128]{3,2,1,0:T(8,128)(2,1)} %get-tuple-element.43), calls=%async_computation | async-start | bytes 2097152 | tf_op jit(solution)/shard_map/all_to_all | solution.py:452
  20.8 1.9 collective-permute-start.7
  26.5 9.8 %all-to-all-done.do_ref = bf16[8,2,256,128]{3,2,1,0:T(8,128)(2,1)} async-done(((bf16[8,2,256,128]{3,2,1,0:T(8,128)(2,1)}), bf16[8,2,256,128]{3,2,1,0:T(8,128)(2,1)}, u32[]{:S(2)}, u32[]{:S(2)}) %all-to-all-start) | async-done | bytes 1048608 | tf_op jit(solution)/shard_map/all_to_all | solution.py:452
  36.3 4.2 %all-to-all-start.2 = ((bf16[8,2,256,128]{3,2,1,0:T(8,128)(2,1)}), bf16[8,2,256,128]{3,2,1,0:T(8,128)(2,1)}, u32[]{:S(2)}, u32[]{:S(2)}) async-start(bf16[8,2,256,128]{3,2,1,0:T(8,128)(2,1)} %get-tuple-element.62), calls=%async_computation.2 | async-start | bytes 2097152 | tf_op jit(solution)/shard_map/all_to_all | solution.py:452
  41.2 17.0 %collective-permute-done.q_recv = bf16[1,1024,128]{2,1,0:T(8,128)(2,1)S(1)} collective-permute-done((bf16[1,1024,128]{2,1,0:T(8,128)(2,1)S(1)}, bf16[1,1024,128]{2,1,0:T(8,128)(2,1)S(1)}, u32[]{:S(2)}, u32[]{:S(2)}) %collective-permute-start) | collective-permute-done | bytes 262176 | tf_op jit(solution)/shard_map/ppermute | solution.py:444
  61.1 17.7 %window_grads.4 = (bf16[1024,128]{1,0:T(8,128)(2,1)}, bf16[1024,128]{1,0:T(8,128)(2,1)}, f32[2,1024,128]{2,1,0:T(8,128)}, f32[2,1024,128]{2,1,0:T(8,128)}, bf16[...) custom-call(s32[21]{0:T(128)} %pad_add_fusion.scalars, bf16[4,1024,128]{2,1,0:T(8,128)(2,1)} %get-tuple-element.41.q_keep, ...), custom_call_target="tpu_custom_call" | custom-call | flops 4026531840 | bytes 4194304 | tf_op jit(solution)/shard_map/window_grads/pallas_call | solution.py:231
  80.2 6.0 %collective-permute-start.5 = (bf16[2,1024,128]{2,1,0:T(8,128)(2,1)}, bf16[2,1024,128]{2,1,0:T(8,128)(2,1)}, u32[]{:S(2)}, u32[]{:S(2)}) collective-permute-start(bf16[2,1024,128]{2,1,0:T(8,128)(2,1)} %get-tuple-element.49), channel_id=1, source_target_pairs={{8,0},{16,8},{4,12},{24,16},{12,20},{20,28},{9,1},{17,9},{5,13},{2... | collective-permute-start | bytes 1572872 | tf_op jit(solution)/shard_map/ppermute | solution.py:444
  86.2 17.8 %window_grads.5 = (bf16[1024,128]{1,0:T(8,128)(2,1)}, bf16[1024,128]{1,0:T(8,128)(2,1)}, f32[2,1024,128]{2,1,0:T(8,128)}, f32[2,1024,128]{2,1,0:T(8,128)}, bf16[...) custom-call(s32[21]{0:T(128)} %pad_add_fusion.scalars, bf16[4,1024,128]{2,1,0:T(8,128)(2,1)} %get-tuple-element.41.q_keep, ...), custom_call_target="tpu_custom_call" | custom-call | flops 4026531840 | bytes 4194304 | tf_op jit(solution)/shard_map/window_grads/pallas_call | solution.py:231
  104.1 3.7 %merge.4 = bf16[8,4,256,128]{3,2,1,0:T(8,128)(2,1)} custom-call(s32[1]{0:T(128)} %bitcast.scalars, f32[2,1024,128]{2,1,0:T(8,128)} %get-tuple-element.46.own_keep, f32[2,1024,128]{2,1,0:T(8,128)} %get-tuple-element.47.own_recv, bf16[2,1024,128]{2,1,0:T(8,128)(2,1)} %collective-permute-done.4.add_keep, bf16[2,1024,128]{2,1,0:T(8,128)(2,1)} %collective-permute-done.5.add_recv, ...), custom_call_target="tpu_custom_call" | custom-call | tf_op jit(solution)/shard_map/merge/pallas_call | solution.py:377
  107.8 4.5 %all-to-all-start.1 = ((bf16[8,4,256,128]{3,2,1,0:T(8,128)(2,1)}), bf16[8,4,256,128]{3,2,1,0:T(8,128)(2,1)}, u32[]{:S(2)}, u32[]{:S(2)}) async-start(bf16[8,4,256,128]{3,2,1,0:T(8,128)(2,1)} %merge.4), calls=%async_computation.1 | async-start | bytes 4194304 | tf_op jit(solution)/shard_map/all_to_all | solution.py:452
  112.3 2.0 collective-permute-start.17
  115.7 34.1 %collective-permute-done.17.kv_recv = bf16[2,1024,128]{2,1,0:T(8,128)(2,1)} collective-permute-done((bf16[2,1024,128]{2,1,0:T(8,128)(2,1)S(1)}, bf16[2,1024,128]{2,1,0:T(8,128)(2,1)}, u32[]{:S(2)}, u32[]{:S(2)}) %collective-permute-start.17) | collective-permute-done | bytes 524320 | tf_op jit(solution)/shard_map/ppermute | solution.py:444
  151.0 9.3 %collective-permute-done.12.q_recv = bf16[2,1024,128]{2,1,0:T(8,128)(2,1)S(1)} collective-permute-done((bf16[2,1024,128]{2,1,0:T(8,128)(2,1)S(1)}, bf16[2,1024,128]{2,1,0:T(8,128)(2,1)S(1)}, u32[]{:S(2)}, u32[]{:S(2)}) %collective-permute-start.12) | collective-permute-done | bytes 524320 | tf_op jit(solution)/shard_map/ppermute | solution.py:444
  161.1 17.7 %window_grads.6 = (bf16[1024,128]{1,0:T(8,128)(2,1)}, bf16[1024,128]{1,0:T(8,128)(2,1)}, f32[2,1024,128]{2,1,0:T(8,128)}, f32[2,1024,128]{2,1,0:T(8,128)}, bf16[...) custom-call(s32[21]{0:T(128)} %pad_add_fusion.scalars, bf16[4,1024,128]{2,1,0:T(8,128)(2,1)} %get-tuple-element.41.q_keep, ...), custom_call_target="tpu_custom_call" | custom-call | flops 4026531840 | bytes 4194304 | tf_op jit(solution)/shard_map/window_grads/pallas_call | solution.py:231
  180.1 5.4 %collective-permute-start.16 = (bf16[2,1024,128]{2,1,0:T(8,128)(2,1)}, bf16[2,1024,128]{2,1,0:T(8,128)(2,1)}, u32[]{:S(2)}, u32[]{:S(2)}) collective-permute-start(bf16[2,1024,128]{2,1,0:T(8,128)(2,1)} %get-tuple-element.69), channel_id=1, source_target_pairs={{8,0},{16,8},{4,12},{24,16},{12,20},{20,28},{9,1},{17,9},{5,13},{2... | collective-permute-start | bytes 1572872 | tf_op jit(solution)/shard_map/ppermute | solution.py:444
  185.4 17.7 %window_grads.7 = (bf16[1024,128]{1,0:T(8,128)(2,1)}, bf16[1024,128]{1,0:T(8,128)(2,1)}, f32[2,1024,128]{2,1,0:T(8,128)}, f32[2,1024,128]{2,1,0:T(8,128)}, bf16[...) custom-call(s32[21]{0:T(128)} %pad_add_fusion.scalars, bf16[4,1024,128]{2,1,0:T(8,128)(2,1)} %get-tuple-element.41.q_keep, ...), custom_call_target="tpu_custom_call" | custom-call | flops 4026531840 | bytes 4194304 | tf_op jit(solution)/shard_map/window_grads/pallas_call | solution.py:231
  203.2 3.3 %merge.6 = bf16[8,3,256,128]{3,2,1,0:T(8,128)(2,1)} custom-call(s32[1]{0:T(128)} %bitcast.scalars, f32[2,1024,128]{2,1,0:T(8,128)} %get-tuple-element.66.own_keep, f32[2,1024,128]{2,1,0:T(8,128)} %get-tuple-element.67.own_recv, bf16[2,1024,128]{2,1,0:T(8,128)(2,1)} %collective-permute-done.15.add_keep, ...), custom_call_target="tpu_custom_call" | custom-call | tf_op jit(solution)/shard_map/merge/pallas_call | solution.py:377
  206.6 4.5 %all-to-all-start.4 = ((bf16[8,3,256,128]{3,2,1,0:T(8,128)(2,1)}), bf16[8,3,256,128]{3,2,1,0:T(8,128)(2,1)}, u32[]{:S(2)}, u32[]{:S(2)}) async-start(bf16[8,3,256,128]{3,2,1,0:T(8,128)(2,1)} %merge.6), calls=%async_computation.4 | async-start | bytes 3145728 | tf_op jit(solution)/shard_map/all_to_all | solution.py:452
  212.3 5.4 %collective-permute-start.11 = (bf16[2,1024,128]{2,1,0:T(8,128)(2,1)S(1)}, bf16[2,1024,128]{2,1,0:T(8,128)(2,1)}, u32[]{:S(2)}, u32[]{:S(2)}) collective-permute-start(bf16[2,1024,128]{2,1,0:T(8,128)(2,1)S(1)} %copy-done.5), channel_id=1, source_target_pairs={{8,0},{16,8},{4,12},{24,16},{12,20},{20,28},{9,1},{17,9},{5,13},{2... | collective-permute-start | bytes 1572872 | tf_op jit(solution)/shard_map/ppermute | solution.py:444
  217.7 9.5 %collective-permute-done.10.add_keep = bf16[2,1024,128]{2,1,0:T(8,128)(2,1)} collective-permute-done((bf16[2,1024,128]{2,1,0:T(8,128)(2,1)S(1)}, bf16[2,1024,128]{2,1,0:T(8,128)(2,1)}, u32[]{:S(2)}, u32[]{:S(2)}) %collective-permute-start.10) | collective-permute-done | bytes 524320 | tf_op jit(solution)/shard_map/ppermute | solution.py:444
  228.3 3.3 %merge.5 = bf16[8,3,256,128]{3,2,1,0:T(8,128)(2,1)} custom-call(s32[1]{0:T(128)} %bitcast.scalars, f32[2,1024,128]{2,1,0:T(8,128)} %get-tuple-element.57.own_keep, f32[2,1024,128]{2,1,0:T(8,128)} %get-tuple-element.58.own_recv, bf16[2,1024,128]{2,1,0:T(8,128)(2,1)} %collective-permute-done.10.add_keep, ...), custom_call_target="tpu_custom_call" | custom-call | tf_op jit(solution)/shard_map/merge/pallas_call | solution.py:377
  232.0 6.6 %all-to-all-start.3 = ((bf16[8,3,256,128]{3,2,1,0:T(8,128)(2,1)}), bf16[8,3,256,128]{3,2,1,0:T(8,128)(2,1)}, u32[]{:S(2)}, u32[]{:S(2)}) async-start(bf16[8,3,256,128]{3,2,1,0:T(8,128)(2,1)} %merge.5), calls=%async_computation.3 | async-start | bytes 3145728 | tf_op jit(solution)/shard_map/all_to_all | solution.py:452
  239.9 5.4 %collective-permute-start.20 = (bf16[2,1024,128]{2,1,0:T(8,128)(2,1)S(1)}, bf16[2,1024,128]{2,1,0:T(8,128)(2,1)}, u32[]{:S(2)}, u32[]{:S(2)}) collective-permute-start(bf16[2,1024,128]{2,1,0:T(8,128)(2,1)S(1)} %copy-done.9), channel_id=1, source_target_pairs={{8,0},{16,8},{4,12},{24,16},{12,20},{20,28},{9,1},{17,9},{5,13},{2... | collective-permute-start | bytes 1572872 | tf_op jit(solution)/shard_map/ppermute | solution.py:444
  245.3 9.7 %collective-permute-done.19.add_keep = bf16[2,1024,128]{2,1,0:T(8,128)(2,1)} collective-permute-done((bf16[2,1024,128]{2,1,0:T(8,128)(2,1)S(1)}, bf16[2,1024,128]{2,1,0:T(8,128)(2,1)}, u32[]{:S(2)}, u32[]{:S(2)}) %collective-permute-start.19) | collective-permute-done | bytes 524320 | tf_op jit(solution)/shard_map/ppermute | solution.py:444
  256.0 3.0 %merge.7 = bf16[8,2,256,128]{3,2,1,0:T(8,128)(2,1)} custom-call(s32[1]{0:T(128)} %bitcast.scalars, f32[2,1024,128]{2,1,0:T(8,128)} %get-tuple-element.73.own_keep, f32[2,1024,128]{2,1,0:T(8,128)} %get-tuple-element.74.own_recv, bf16[2,1024,128]{2,1,0:T(8,128)(2,1)} %collective-permute-done.19.add_keep, bf16[2,1024,128]{2,1,0:T(8,128)(2,1)} %collective-permute-done.20.add_recv), custom_call_target="tpu_custom_call" | custom-call | tf_op jit(solution)/shard_map/merge/pallas_call | solution.py:377
  259.7 6.2 %all-to-all-start.5 = ((bf16[8,2,256,128]{3,2,1,0:T(8,128)(2,1)}), bf16[8,2,256,128]{3,2,1,0:T(8,128)(2,1)}, u32[]{:S(2)}, u32[]{:S(2)}) async-start(bf16[8,2,256,128]{3,2,1,0:T(8,128)(2,1)} %merge.7), calls=%async_computation.5 | async-start | bytes 2097152 | tf_op jit(solution)/shard_map/all_to_all | solution.py:452
  265.9 4.7 %assemble.2 = bf16[256,32,128]{2,1,0:T(8,128)(2,1)} custom-call(bf16[8,4,256,128]{3,2,1,0:T(8,128)(2,1)} %all-to-all-done.1.refs_0_, bf16[8,3,256,128]{3,2,1,0:T(8,128)(2,1)} %all-to-all-done.3.refs_1_, bf16[8,3,256,128]{3,2,1,0:T(8,128)(2,1)} %all-to-all-done.4.refs_2_), custom_call_target="tpu_custom_call" | custom-call | tf_op jit(solution)/shard_map/assemble/pallas_call | solution.py:410
  270.6 10.8 %all-to-all-done.5.refs_3_ = bf16[8,2,256,128]{3,2,1,0:T(8,128)(2,1)} async-done(((bf16[8,2,256,128]{3,2,1,0:T(8,128)(2,1)}), bf16[8,2,256,128]{3,2,1,0:T(8,128)(2,1)}, u32[]{:S(2)}, u32[]{:S(2)}) %all-to-all-start.5) | async-done | bytes 1048608 | tf_op jit(solution)/shard_map/all_to_all | solution.py:452
  281.4 5.5 %assemble.3 = (bf16[256,32,128]{2,1,0:T(8,128)(2,1)}, bf16[256,32,128]{2,1,0:T(8,128)(2,1)}) custom-call(bf16[8,4,256,128]{3,2,1,0:T(8,128)(2,1)} %all-to-all-done.1.refs_0_, bf16[8,3,256,128]{3,2,1,0:T(8,128)(2,1)} %all-to-all-done.3.refs_1_, bf16[8,3,256,128]{3,2,1,0:T(8,128)(2,1)} %all-to-all-done.4.refs_2_, bf16[8,2,256,128]{3,2,1,0:T(8,128)(2,1)} %all-to-all-done.5.refs_3_), custom_call_target="tpu_custom_call" | custom-call | tf_op jit(solution)/shard_map/assemble/pallas_call | solution.py:410
  (70 shorter events, 20.8 us)
Async XLA Ops:
  5.8 18.5 %collective-permute-start.1 = (bf16[2,1024,128]{2,1,0:T(8,128)(2,1)}, bf16[2,1024,128]{2,1,0:T(8,128)(2,1)}, u32[]{:S(2)}, u32[]{:S(2)}) collective-permute-start(bf16[2,1024,128]{2,1,0:T(8,128)(2,1)} %get-tuple-element.44), channel_id=1, source_target_pairs={{0,4},{4,0},{8,12},{12,8},{16,20},{20,16},{24,28},{28,24},{1,5},{5... | collective-permute-start | bytes 1572872 | tf_op jit(solution)/shard_map/ppermute | solution.py:444
  7.4 78.9 %collective-permute-start.9 = (bf16[3,2,1024,128]{3,2,1,0:T(8,128)(2,1)}, bf16[3,2,1024,128]{3,2,1,0:T(8,128)(2,1)}, u32[]{:S(2)}, u32[]{:S(2)}) collective-permute-start(bf16[3,2,1024,128]{3,2,1,0:T(8,128)(2,1)} %get-tuple-element.54.kv_keep), channel_id=1, source_target_pairs={{4,12},{8,0},{12,20},{16,8},{20,28},{24,16},{5,13},{9,1},{13,21},{... | collective-permute-start | bytes 4718600 | tf_op jit(solution)/shard_map/ppermute | solution.py:444
  16.4 7.7 %copy-start.14 = (bf16[1,1024,128]{2,1,0:T(8,128)(2,1)S(1)}, bf16[1,1024,128]{2,1,0:T(8,128)(2,1)}, u32[]{:S(2)}) copy-start(bf16[1,1024,128]{2,1,0:T(8,128)(2,1)} %get-tuple-element.42) | copy-start | bytes 786436
  16.4 9.3 %copy-start = (s32[8]{0:T(128)S(1)}, s32[8]{0:T(128)}, u32[]{:S(2)}) copy-start(s32[8]{0:T(128)} %param.11) | copy-start | bytes 100
  16.4 10.0 %copy-start.1 = (s32[64]{0:T(128)S(1)}, s32[64]{0:T(128)}, u32[]{:S(2)}) copy-start(s32[64]{0:T(128)} %param.10) | copy-start | bytes 772
  16.4 19.9 %all-to-all-start = ((bf16[8,2,256,128]{3,2,1,0:T(8,128)(2,1)}), bf16[8,2,256,128]{3,2,1,0:T(8,128)(2,1)}, u32[]{:S(2)}, u32[]{:S(2)}) async-start(bf16[8,2,256,128]{3,2,1,0:T(8,128)(2,1)} %get-tuple-element.43), calls=%async_computation | async-start | bytes 2097152 | tf_op jit(solution)/shard_map/all_to_all | solution.py:452
  20.8 37.4 %collective-permute-start.7 = (bf16[2,1024,128]{2,1,0:T(8,128)(2,1)S(1)}, bf16[2,1024,128]{2,1,0:T(8,128)(2,1)}, u32[]{:S(2)}, u32[]{:S(2)}) collective-permute-start(bf16[2,1024,128]{2,1,0:T(8,128)(2,1)S(1)} %copy-done.7), channel_id=1, source_target_pairs={{0,4},{4,0},{8,12},{12,8},{16,20},{20,16},{24,28},{28,24},{1,5},{5... | collective-permute-start | bytes 1572872 | tf_op jit(solution)/shard_map/ppermute | solution.py:444
  22.7 36.8 %collective-permute-start.3 = (bf16[1,2,1024,128]{3,2,1,0:T(8,128)(2,1)S(1)}, bf16[1,2,1024,128]{3,2,1,0:T(8,128)(2,1)S(1)}, u32[]{:S(2)}, u32[]{:S(2)}) collective-permute-start(bf16[1,2,1024,128]{3,2,1,0:T(8,128)(2,1)S(1)} %copy-done.4), channel_id=1, source_target_pairs={{4,12},{8,0},{12,20},{16,8},{20,28},{24,16},{5,13},{9,1},{13,21},{... | collective-permute-start | bytes 1572872 | tf_op jit(solution)/shard_map/ppermute | solution.py:444
  24.0 34.1 %collective-permute-start = (bf16[1,1024,128]{2,1,0:T(8,128)(2,1)S(1)}, bf16[1,1024,128]{2,1,0:T(8,128)(2,1)S(1)}, u32[]{:S(2)}, u32[]{:S(2)}) collective-permute-start(bf16[1,1024,128]{2,1,0:T(8,128)(2,1)S(1)} %copy-done.14), channel_id=1, source_target_pairs={{0,4},{4,0},{8,12},{12,8},{16,20},{20,16},{24,28},{28,24},{1,5},{5... | collective-permute-start | bytes 786440 | tf_op jit(solution)/shard_map/ppermute | solution.py:444
  24.3 36.0 %collective-permute-start.2 = (bf16[2,1024,128]{2,1,0:T(8,128)(2,1)}, bf16[2,1024,128]{2,1,0:T(8,128)(2,1)S(1)}, u32[]{:S(2)}, u32[]{:S(2)}) collective-permute-start(bf16[2,1024,128]{2,1,0:T(8,128)(2,1)} %collective-permute-done.1.kv_recv), channel_id=1, source_target_pairs={{0,8},{8,16},{12,4},{16,24},{20,12},{28,20},{1,9},{9,17},{13,5},{1... | collective-permute-start | bytes 1572872 | tf_op jit(solution)/shard_map/ppermute | solution.py:444
  36.3 71.5 %all-to-all-start.2 = ((bf16[8,2,256,128]{3,2,1,0:T(8,128)(2,1)}), bf16[8,2,256,128]{3,2,1,0:T(8,128)(2,1)}, u32[]{:S(2)}, u32[]{:S(2)}) async-start(bf16[8,2,256,128]{3,2,1,0:T(8,128)(2,1)} %get-tuple-element.62), calls=%async_computation.2 | async-start | bytes 2097152 | tf_op jit(solution)/shard_map/all_to_all | solution.py:452
  58.2 28.0 %collective-permute-start.6 = (bf16[1,1024,128]{2,1,0:T(8,128)(2,1)}, bf16[1,1024,128]{2,1,0:T(8,128)(2,1)}, u32[]{:S(2)}, u32[]{:S(2)}) collective-permute-start(bf16[1,1024,128]{2,1,0:T(8,128)(2,1)} %get-tuple-element.52), channel_id=1, source_target_pairs={{0,4},{4,0},{8,12},{12,8},{16,20},{20,16},{24,28},{28,24},{1,5},{5... | collective-permute-start | bytes 786440 | tf_op jit(solution)/shard_map/ppermute | solution.py:444
  58.2 28.0 %collective-permute-start.8 = (bf16[2,1024,128]{2,1,0:T(8,128)(2,1)}, bf16[2,1024,128]{2,1,0:T(8,128)(2,1)}, u32[]{:S(2)}, u32[]{:S(2)}) collective-permute-start(bf16[2,1024,128]{2,1,0:T(8,128)(2,1)} %collective-permute-done.7.kv_recv), channel_id=1, source_target_pairs={{0,8},{8,16},{12,4},{16,24},{20,12},{28,20},{1,9},{9,17},{13,5},{1... | collective-permute-start | bytes 1572872 | tf_op jit(solution)/shard_map/ppermute | solution.py:444
  78.9 25.2 %collective-permute-start.4 = (bf16[2,1024,128]{2,1,0:T(8,128)(2,1)}, bf16[2,1024,128]{2,1,0:T(8,128)(2,1)}, u32[]{:S(2)}, u32[]{:S(2)}) collective-permute-start(bf16[2,1024,128]{2,1,0:T(8,128)(2,1)} %get-tuple-element.48), channel_id=1, source_target_pairs={{12,4},{0,8},{20,12},{8,16},{28,20},{16,24},{13,5},{1,9},{21,13},{... | collective-permute-start | bytes 1572872 | tf_op jit(solution)/shard_map/ppermute | solution.py:444
  80.2 23.9 %collective-permute-start.5 = (bf16[2,1024,128]{2,1,0:T(8,128)(2,1)}, bf16[2,1024,128]{2,1,0:T(8,128)(2,1)}, u32[]{:S(2)}, u32[]{:S(2)}) collective-permute-start(bf16[2,1024,128]{2,1,0:T(8,128)(2,1)} %get-tuple-element.49), channel_id=1, source_target_pairs={{8,0},{16,8},{4,12},{24,16},{12,20},{20,28},{9,1},{17,9},{5,13},{2... | collective-permute-start | bytes 1572872 | tf_op jit(solution)/shard_map/ppermute | solution.py:444
  86.2 28.2 %collective-permute-start.13 = (bf16[2,1024,128]{2,1,0:T(8,128)(2,1)}, bf16[2,1024,128]{2,1,0:T(8,128)(2,1)}, u32[]{:S(2)}, u32[]{:S(2)}) collective-permute-start(bf16[2,1024,128]{2,1,0:T(8,128)(2,1)} %get-tuple-element.63), channel_id=1, source_target_pairs={{0,4},{4,0},{8,12},{12,8},{16,20},{20,16},{24,28},{28,24},{1,5},{5... | collective-permute-start | bytes 1572872 | tf_op jit(solution)/shard_map/ppermute | solution.py:444
  107.8 98.8 %all-to-all-start.1 = ((bf16[8,4,256,128]{3,2,1,0:T(8,128)(2,1)}), bf16[8,4,256,128]{3,2,1,0:T(8,128)(2,1)}, u32[]{:S(2)}, u32[]{:S(2)}) async-start(bf16[8,4,256,128]{3,2,1,0:T(8,128)(2,1)} %merge.4), calls=%async_computation.1 | async-start | bytes 4194304 | tf_op jit(solution)/shard_map/all_to_all | solution.py:452
  112.3 37.5 %collective-permute-start.17 = (bf16[2,1024,128]{2,1,0:T(8,128)(2,1)S(1)}, bf16[2,1024,128]{2,1,0:T(8,128)(2,1)}, u32[]{:S(2)}, u32[]{:S(2)}) collective-permute-start(bf16[2,1024,128]{2,1,0:T(8,128)(2,1)S(1)} %copy-done.2), channel_id=1, source_target_pairs={{0,4},{4,0},{8,12},{12,8},{16,20},{20,16},{24,28},{28,24},{1,5},{5... | collective-permute-start | bytes 1572872 | tf_op jit(solution)/shard_map/ppermute | solution.py:444
  114.3 46.0 %collective-permute-start.12 = (bf16[2,1024,128]{2,1,0:T(8,128)(2,1)S(1)}, bf16[2,1024,128]{2,1,0:T(8,128)(2,1)S(1)}, u32[]{:S(2)}, u32[]{:S(2)}) collective-permute-start(bf16[2,1024,128]{2,1,0:T(8,128)(2,1)S(1)} %copy-done.3), channel_id=1, source_target_pairs={{0,4},{4,0},{8,12},{12,8},{16,20},{20,16},{24,28},{28,24},{1,5},{5... | collective-permute-start | bytes 1572872 | tf_op jit(solution)/shard_map/ppermute | solution.py:444
  114.4 46.7 %collective-permute-start.14 = (bf16[2,1024,128]{2,1,0:T(8,128)(2,1)}, bf16[2,1024,128]{2,1,0:T(8,128)(2,1)}, u32[]{:S(2)}, u32[]{:S(2)}) collective-permute-start(bf16[2,1024,128]{2,1,0:T(8,128)(2,1)} %collective-permute-done.13.kv_recv), channel_id=1, source_target_pairs={{0,8},{8,16},{12,4},{16,24},{20,12},{28,20},{1,9},{9,17},{13,5},{1... | collective-permute-start | bytes 1572872 | tf_op jit(solution)/shard_map/ppermute | solution.py:444
  149.7 35.7 %collective-permute-start.18 = (bf16[2,1024,128]{2,1,0:T(8,128)(2,1)}, bf16[2,1024,128]{2,1,0:T(8,128)(2,1)}, u32[]{:S(2)}, u32[]{:S(2)}) collective-permute-start(bf16[2,1024,128]{2,1,0:T(8,128)(2,1)} %collective-permute-done.17.kv_recv), channel_id=1, source_target_pairs={{0,8},{8,16},{12,4},{16,24},{20,12},{28,20},{1,9},{9,17},{13,5},{1... | collective-permute-start | bytes 1572872 | tf_op jit(solution)/shard_map/ppermute | solution.py:444
  178.8 24.4 %collective-permute-start.15 = (bf16[2,1024,128]{2,1,0:T(8,128)(2,1)}, bf16[2,1024,128]{2,1,0:T(8,128)(2,1)}, u32[]{:S(2)}, u32[]{:S(2)}) collective-permute-start(bf16[2,1024,128]{2,1,0:T(8,128)(2,1)} %get-tuple-element.68), channel_id=1, source_target_pairs={{12,4},{0,8},{20,12},{8,16},{28,20},{16,24},{13,5},{1,9},{21,13},{... | collective-permute-start | bytes 1572872 | tf_op jit(solution)/shard_map/ppermute | solution.py:444
  180.1 23.1 %collective-permute-start.16 = (bf16[2,1024,128]{2,1,0:T(8,128)(2,1)}, bf16[2,1024,128]{2,1,0:T(8,128)(2,1)}, u32[]{:S(2)}, u32[]{:S(2)}) collective-permute-start(bf16[2,1024,128]{2,1,0:T(8,128)(2,1)} %get-tuple-element.69), channel_id=1, source_target_pairs={{8,0},{16,8},{4,12},{24,16},{12,20},{20,28},{9,1},{17,9},{5,13},{2... | collective-permute-start | bytes 1572872 | tf_op jit(solution)/shard_map/ppermute | solution.py:444
  206.6 25.5 %all-to-all-start.4 = ((bf16[8,3,256,128]{3,2,1,0:T(8,128)(2,1)}), bf16[8,3,256,128]{3,2,1,0:T(8,128)(2,1)}, u32[]{:S(2)}, u32[]{:S(2)}) async-start(bf16[8,3,256,128]{3,2,1,0:T(8,128)(2,1)} %merge.6), calls=%async_computation.4 | async-start | bytes 3145728 | tf_op jit(solution)/shard_map/all_to_all | solution.py:452
  211.0 16.2 %collective-permute-start.10 = (bf16[2,1024,128]{2,1,0:T(8,128)(2,1)S(1)}, bf16[2,1024,128]{2,1,0:T(8,128)(2,1)}, u32[]{:S(2)}, u32[]{:S(2)}) collective-permute-start(bf16[2,1024,128]{2,1,0:T(8,128)(2,1)S(1)} %copy-done.6), channel_id=1, source_target_pairs={{12,4},{0,8},{20,12},{8,16},{28,20},{16,24},{13,5},{1,9},{21,13},{... | collective-permute-start | bytes 1572872 | tf_op jit(solution)/shard_map/ppermute | solution.py:444
  212.3 16.0 %collective-permute-start.11 = (bf16[2,1024,128]{2,1,0:T(8,128)(2,1)S(1)}, bf16[2,1024,128]{2,1,0:T(8,128)(2,1)}, u32[]{:S(2)}, u32[]{:S(2)}) collective-permute-start(bf16[2,1024,128]{2,1,0:T(8,128)(2,1)S(1)} %copy-done.5), channel_id=1, source_target_pairs={{8,0},{16,8},{4,12},{24,16},{12,20},{20,28},{9,1},{17,9},{5,13},{2... | collective-permute-start | bytes 1572872 | tf_op jit(solution)/shard_map/ppermute | solution.py:444
  231.6 7.0 %copy-start.11 = (bf16[2,1024,128]{2,1,0:T(8,128)(2,1)S(1)}, bf16[2,1024,128]{2,1,0:T(8,128)(2,1)}, u32[]{:S(2)}) copy-start(bf16[2,1024,128]{2,1,0:T(8,128)(2,1)} %get-tuple-element.75) | copy-start | bytes 1572868
  231.6 8.3 %copy-start.9 = (bf16[2,1024,128]{2,1,0:T(8,128)(2,1)S(1)}, bf16[2,1024,128]{2,1,0:T(8,128)(2,1)}, u32[]{:S(2)}) copy-start(bf16[2,1024,128]{2,1,0:T(8,128)(2,1)} %get-tuple-element.76) | copy-start | bytes 1572868
  232.0 27.7 %all-to-all-start.3 = ((bf16[8,3,256,128]{3,2,1,0:T(8,128)(2,1)}), bf16[8,3,256,128]{3,2,1,0:T(8,128)(2,1)}, u32[]{:S(2)}, u32[]{:S(2)}) async-start(bf16[8,3,256,128]{3,2,1,0:T(8,128)(2,1)} %merge.5), calls=%async_computation.3 | async-start | bytes 3145728 | tf_op jit(solution)/shard_map/all_to_all | solution.py:452
  238.6 16.3 %collective-permute-start.19 = (bf16[2,1024,128]{2,1,0:T(8,128)(2,1)S(1)}, bf16[2,1024,128]{2,1,0:T(8,128)(2,1)}, u32[]{:S(2)}, u32[]{:S(2)}) collective-permute-start(bf16[2,1024,128]{2,1,0:T(8,128)(2,1)S(1)} %copy-done.11), channel_id=1, source_target_pairs={{12,4},{0,8},{20,12},{8,16},{28,20},{16,24},{13,5},{1,9},{21,13},{... | collective-permute-start | bytes 1572872 | tf_op jit(solution)/shard_map/ppermute | solution.py:444
  239.9 16.1 %collective-permute-start.20 = (bf16[2,1024,128]{2,1,0:T(8,128)(2,1)S(1)}, bf16[2,1024,128]{2,1,0:T(8,128)(2,1)}, u32[]{:S(2)}, u32[]{:S(2)}) collective-permute-start(bf16[2,1024,128]{2,1,0:T(8,128)(2,1)S(1)} %copy-done.9), channel_id=1, source_target_pairs={{8,0},{16,8},{4,12},{24,16},{12,20},{20,28},{9,1},{17,9},{5,13},{2... | collective-permute-start | bytes 1572872 | tf_op jit(solution)/shard_map/ppermute | solution.py:444
  259.7 21.7 %all-to-all-start.5 = ((bf16[8,2,256,128]{3,2,1,0:T(8,128)(2,1)}), bf16[8,2,256,128]{3,2,1,0:T(8,128)(2,1)}, u32[]{:S(2)}, u32[]{:S(2)}) async-start(bf16[8,2,256,128]{3,2,1,0:T(8,128)(2,1)} %merge.7), calls=%async_computation.5 | async-start | bytes 2097152 | tf_op jit(solution)/shard_map/all_to_all | solution.py:452
  (10 other events, 36.7 us)

commit v3 on v2

--- a/solution.py
+++ b/solution.py
@@ -64,6 +64,7 @@
     v_buf,
     low_buf,
     high_buf,
+    own_buf,
     dk_acc,
     dv_acc,
     p_buf,
@@ -213,7 +214,9 @@
     stores += [begin(q_buf.at[pl.ds(tok, tok), :], dq_recv)]
     for slot, ref in ((1, own_keep), (2, own_recv)):
         rows = pl.ds(slot * tok, tok)
-        stores += [begin(dk_acc.at[rows, :], ref.at[0]), begin(dv_acc.at[rows, :], ref.at[1])]
+        own_buf[slot - 1, 0] = (dk_acc[rows, :] * scale).astype(own_buf.dtype)
+        own_buf[slot - 1, 1] = dv_acc[rows, :].astype(own_buf.dtype)
+        stores += [begin(own_buf.at[slot - 1], ref)]
     high_buf[0] = (dk_acc[pl.ds(3 * tok, tok), :] * scale).astype(high_buf.dtype)
     high_buf[1] = dv_acc[pl.ds(3 * tok, tok), :].astype(high_buf.dtype)
     stores += [begin(high_buf, half_high)]
@@ -231,8 +234,7 @@
     return pl.pallas_call(
         functools.partial(attention_kernel, chunk),
         out_shape=(jax.ShapeDtypeStruct((tok, head_dim), jnp.bfloat16),) * 2
-        + (jax.ShapeDtypeStruct((2, tok, head_dim), jnp.float32),) * 2
-        + (jax.ShapeDtypeStruct((2, tok, head_dim), jnp.bfloat16),) * 2,
+        + (jax.ShapeDtypeStruct((2, tok, head_dim), jnp.bfloat16),) * 4,
         in_specs=[pl.BlockSpec(memory_space=pltpu.SMEM)] + [place] * 7,
         out_specs=(place,) * 6,
         scratch_shapes=[
@@ -242,11 +244,12 @@
             pltpu.VMEM((keys_all, head_dim), jnp.bfloat16),
             pltpu.VMEM((2, tok, head_dim), jnp.bfloat16),
             pltpu.VMEM((2, tok, head_dim), jnp.bfloat16),
+            pltpu.VMEM((2, 2, tok, head_dim), jnp.bfloat16),
             pltpu.VMEM((keys_all, head_dim), jnp.float32),
             pltpu.VMEM((keys_all, head_dim), jnp.float32),
             pltpu.VMEM((window, GH * TILE), jnp.float32),
             pltpu.VMEM((window, GH * TILE), jnp.float32),
-            pltpu.SemaphoreType.DMA((18 + senders,)),
+            pltpu.SemaphoreType.DMA((16 + senders,)),
         ],
         cost_estimate=pl.CostEstimate(
             flops=10 * pairs * head_dim, transcendentals=pairs, bytes_accessed=16 * tok * head_dim * 2
@@ -353,17 +356,17 @@
 
 def merge_kernel(scalars, own_keep, own_recv, add_keep, add_recv, *refs):
     query_grads, out = refs[:-1], refs[-1]
-    targets, _, part, head_dim = out.shape
+    targets, _, part, _ = out.shape
     row_count = targets // 2
     side = scalars[0]
-    factors = (head_dim ** (-0.5), 1.0)
     sums = ((own_keep, add_keep, side), (own_recv, add_recv, 1 - side))
     for which, (own, add, place) in enumerate(sums):
         for row in range(row_count):
             rows = pl.ds(row * part, part)
             target = place * row_count + row
-            for plane, factor in enumerate(factors):
-                total = own[plane, rows, :] * factor + add[plane, rows, :].astype(jnp.float32)
+            for plane in range(2):
+                total = own[plane, rows, :].astype(jnp.float32)
+                total += add[plane, rows, :].astype(jnp.float32)
                 out[target, plane] = total.astype(out.dtype)
             for plane, grad in enumerate(query_grads[which::2]):
                 out[target, 2 + plane] = grad[rows, :]

time: 291 us -> 289 us (level)
  transfers between devices with their start and end apart: 27 -> 27, of which waited for: 11 -> 11; matrix products, arithmetic and copies ran while one was open for 1% -> 1% of each run, Pallas kernels for 33% -> 32%
where the time goes in v3:
time: 289 us; the launch traced here: 284 us
  waiting for transfers between devices  104 us (36%)
  Pallas kernels  103 us (36%)
  starting transfers between devices  73 us (25%)
  local copies, waits for them, and re-layouts  3.15 us (1%)
    ppermute x21, waiting for transfers between devices, over_slab(): return lax.ppermute(array, 'slab', pairs)  81.5 us
    pallas_call x4, Pallas kernels, attention_call(): pl.pallas_call(functools.partial(attention_kernel, chunk), out_shape=(jax...  69.5 us
    ppermute x21, starting transfers between devices, over_slab(): return lax.ppermute(array, 'slab', pairs)  43.2 us
    all_to_all x6, starting transfers between devices, to_all(): lax.all_to_all(array, ('slab', 'row'), 0, 0, axis_index_groups=groups, ti...  29.8 us
    all_to_all x6, waiting for transfers between devices, to_all(): lax.all_to_all(array, ('slab', 'row'), 0, 0, axis_index_groups=groups, ti...  22.3 us
    pallas_call x4, Pallas kernels, merge(): pl.pallas_call(merge_kernel, out_shape=jax.ShapeDtypeStruct(shape, jnp.bf...  12.2 us
    pallas_call x2, Pallas kernels, assemble(): pl.pallas_call(functools.partial(assemble_kernel, sources), grid=(steps,)...  10.2 us
  transfers between devices with their start and end apart: 27, of which 11 were waited for; matrix products, arithmetic and copies ran while one was open for 1% of the time, Pallas kernels for 32%

profile of v3, /device:TPU:24, one launch (start us, length us, event | category | flops | bytes accessed | tf_op | source)
XLA Modules:
  0.0 284.2 jit_solution(229417824604530016)
XLA Ops:
  0.6 5.2 %split_pair.1 = (bf16[2,1024,128]{2,1,0:T(8,128)(2,1)}, bf16[2,1024,128]{2,1,0:T(8,128)(2,1)}, bf16[2,1024,128]{2,1,0:T(8,128)(2,1)}, bf16[2,1024,128]{2,1,0:T(8...) custom-call(s32[1]{0:T(128)} %bitcast.scalars, bf16[1024,8,128]{2,1,0:T(8,128)(2,1)} %refs_0_.1, ...), custom_call_target="tpu_custom_call" | custom-call | tf_op jit(solution)/shard_map/split_pair/pallas_call | solution.py:283
  7.4 3.5 %collective-permute-start.9 = (bf16[3,2,1024,128]{3,2,1,0:T(8,128)(2,1)}, bf16[3,2,1024,128]{3,2,1,0:T(8,128)(2,1)}, u32[]{:S(2)}, u32[]{:S(2)}) collective-permute-start(bf16[3,2,1024,128]{3,2,1,0:T(8,128)(2,1)} %get-tuple-element.54.kv_keep), channel_id=1, source_target_pairs={{4,12},{8,0},{12,20},{16,8},{20,28},{24,16},{5,13},{9,1},{13,21},{... | collective-permute-start | bytes 4718600 | tf_op jit(solution)/shard_map/ppermute | solution.py:447
  10.9 5.5 %spread.1 = (bf16[4,1024,128]{2,1,0:T(8,128)(2,1)}, bf16[1,1024,128]{2,1,0:T(8,128)(2,1)}, bf16[1,1024,128]{2,1,0:T(8,128)(2,1)}, bf16[2,1024,128]{2,1,0:T(8,128...) custom-call(s32[1]{0:T(128)} %bitcast.scalars, bf16[1024,8,128]{2,1,0:T(8,128)(2,1)} %queries.1, ...), custom_call_target="tpu_custom_call" | custom-call | tf_op jit(solution)/shard_map/spread/pallas_call | solution.py:325
  16.4 4.4 %all-to-all-start = ((bf16[8,2,256,128]{3,2,1,0:T(8,128)(2,1)}), bf16[8,2,256,128]{3,2,1,0:T(8,128)(2,1)}, u32[]{:S(2)}, u32[]{:S(2)}) async-start(bf16[8,2,256,128]{3,2,1,0:T(8,128)(2,1)} %get-tuple-element.43), calls=%async_computation | async-start | bytes 2097152 | tf_op jit(solution)/shard_map/all_to_all | solution.py:455
  20.8 1.9 collective-permute-start.7
  26.5 9.8 %all-to-all-done.do_ref = bf16[8,2,256,128]{3,2,1,0:T(8,128)(2,1)} async-done(((bf16[8,2,256,128]{3,2,1,0:T(8,128)(2,1)}), bf16[8,2,256,128]{3,2,1,0:T(8,128)(2,1)}, u32[]{:S(2)}, u32[]{:S(2)}) %all-to-all-start) | async-done | bytes 1048608 | tf_op jit(solution)/shard_map/all_to_all | solution.py:455
  36.3 4.2 %all-to-all-start.2 = ((bf16[8,2,256,128]{3,2,1,0:T(8,128)(2,1)}), bf16[8,2,256,128]{3,2,1,0:T(8,128)(2,1)}, u32[]{:S(2)}, u32[]{:S(2)}) async-start(bf16[8,2,256,128]{3,2,1,0:T(8,128)(2,1)} %get-tuple-element.62), calls=%async_computation.2 | async-start | bytes 2097152 | tf_op jit(solution)/shard_map/all_to_all | solution.py:455
  41.1 17.0 %collective-permute-done.q_recv = bf16[1,1024,128]{2,1,0:T(8,128)(2,1)S(1)} collective-permute-done((bf16[1,1024,128]{2,1,0:T(8,128)(2,1)S(1)}, bf16[1,1024,128]{2,1,0:T(8,128)(2,1)S(1)}, u32[]{:S(2)}, u32[]{:S(2)}) %collective-permute-start) | collective-permute-done | bytes 262176 | tf_op jit(solution)/shard_map/ppermute | solution.py:447
  61.1 17.4 %window_grads.4 = (bf16[1024,128]{1,0:T(8,128)(2,1)}, bf16[1024,128]{1,0:T(8,128)(2,1)}, bf16[2,1024,128]{2,1,0:T(8,128)(2,1)}, bf16[2,1024,128]{2,1,0:T(8,128)(...) custom-call(s32[21]{0:T(128)} %pad_add_fusion.scalars, ...), custom_call_target="tpu_custom_call" | custom-call | flops 4026531840 | bytes 4194304 | tf_op jit(solution)/shard_map/window_grads/pallas_call | solution.py:234
  79.8 6.0 %collective-permute-start.5 = (bf16[2,1024,128]{2,1,0:T(8,128)(2,1)}, bf16[2,1024,128]{2,1,0:T(8,128)(2,1)}, u32[]{:S(2)}, u32[]{:S(2)}) collective-permute-start(bf16[2,1024,128]{2,1,0:T(8,128)(2,1)} %get-tuple-element.49), channel_id=1, source_target_pairs={{8,0},{16,8},{4,12},{24,16},{12,20},{20,28},{9,1},{17,9},{5,13},{2... | collective-permute-start | bytes 1572872 | tf_op jit(solution)/shard_map/ppermute | solution.py:447
  85.8 17.4 %window_grads.5 = (bf16[1024,128]{1,0:T(8,128)(2,1)}, bf16[1024,128]{1,0:T(8,128)(2,1)}, bf16[2,1024,128]{2,1,0:T(8,128)(2,1)}, bf16[2,1024,128]{2,1,0:T(8,128)(...) custom-call(s32[21]{0:T(128)} %pad_add_fusion.scalars, ...), custom_call_target="tpu_custom_call" | custom-call | flops 4026531840 | bytes 4194304 | tf_op jit(solution)/shard_map/window_grads/pallas_call | solution.py:234
  103.2 3.4 %merge.4 = bf16[8,4,256,128]{3,2,1,0:T(8,128)(2,1)} custom-call(s32[1]{0:T(128)} %bitcast.scalars, bf16[2,1024,128]{2,1,0:T(8,128)(2,1)} %get-tuple-element.46.own_keep, bf16[2,1024,128]{2,1,0:T(8,128)(2,1)} %get-tuple-element.47.own_recv, bf16[2,1024,128]{2,1,0:T(8,128)(2,1)} %collective-permute-done.4.add_keep, ...), custom_call_target="tpu_custom_call" | custom-call | tf_op jit(solution)/shard_map/merge/pallas_call | solution.py:380
  106.6 4.5 %all-to-all-start.1 = ((bf16[8,4,256,128]{3,2,1,0:T(8,128)(2,1)}), bf16[8,4,256,128]{3,2,1,0:T(8,128)(2,1)}, u32[]{:S(2)}, u32[]{:S(2)}) async-start(bf16[8,4,256,128]{3,2,1,0:T(8,128)(2,1)} %merge.4), calls=%async_computation.1 | async-start | bytes 4194304 | tf_op jit(solution)/shard_map/all_to_all | solution.py:455
  111.1 2.1 collective-permute-start.17
  114.5 34.1 %collective-permute-done.17.kv_recv = bf16[2,1024,128]{2,1,0:T(8,128)(2,1)} collective-permute-done((bf16[2,1024,128]{2,1,0:T(8,128)(2,1)S(1)}, bf16[2,1024,128]{2,1,0:T(8,128)(2,1)}, u32[]{:S(2)}, u32[]{:S(2)}) %collective-permute-start.17) | collective-permute-done | bytes 524320 | tf_op jit(solution)/shard_map/ppermute | solution.py:447
  150.1 9.0 %collective-permute-done.12.q_recv = bf16[2,1024,128]{2,1,0:T(8,128)(2,1)S(1)} collective-permute-done((bf16[2,1024,128]{2,1,0:T(8,128)(2,1)S(1)}, bf16[2,1024,128]{2,1,0:T(8,128)(2,1)S(1)}, u32[]{:S(2)}, u32[]{:S(2)}) %collective-permute-start.12) | collective-permute-done | bytes 524320 | tf_op jit(solution)/shard_map/ppermute | solution.py:447
  159.9 17.4 %window_grads.6 = (bf16[1024,128]{1,0:T(8,128)(2,1)}, bf16[1024,128]{1,0:T(8,128)(2,1)}, bf16[2,1024,128]{2,1,0:T(8,128)(2,1)}, bf16[2,1024,128]{2,1,0:T(8,128)(...) custom-call(s32[21]{0:T(128)} %pad_add_fusion.scalars, ...), custom_call_target="tpu_custom_call" | custom-call | flops 4026531840 | bytes 4194304 | tf_op jit(solution)/shard_map/window_grads/pallas_call | solution.py:234
  178.6 5.4 %collective-permute-start.16 = (bf16[2,1024,128]{2,1,0:T(8,128)(2,1)}, bf16[2,1024,128]{2,1,0:T(8,128)(2,1)}, u32[]{:S(2)}, u32[]{:S(2)}) collective-permute-start(bf16[2,1024,128]{2,1,0:T(8,128)(2,1)} %get-tuple-element.69), channel_id=1, source_target_pairs={{8,0},{16,8},{4,12},{24,16},{12,20},{20,28},{9,1},{17,9},{5,13},{2... | collective-permute-start | bytes 1572872 | tf_op jit(solution)/shard_map/ppermute | solution.py:447
  184.0 17.4 %window_grads.7 = (bf16[1024,128]{1,0:T(8,128)(2,1)}, bf16[1024,128]{1,0:T(8,128)(2,1)}, bf16[2,1024,128]{2,1,0:T(8,128)(2,1)}, bf16[2,1024,128]{2,1,0:T(8,128)(...) custom-call(s32[21]{0:T(128)} %pad_add_fusion.scalars, ...), custom_call_target="tpu_custom_call" | custom-call | flops 4026531840 | bytes 4194304 | tf_op jit(solution)/shard_map/window_grads/pallas_call | solution.py:234
  201.4 3.0 %merge.6 = bf16[8,3,256,128]{3,2,1,0:T(8,128)(2,1)} custom-call(s32[1]{0:T(128)} %bitcast.scalars, bf16[2,1024,128]{2,1,0:T(8,128)(2,1)} %get-tuple-element.66.own_keep, bf16[2,1024,128]{2,1,0:T(8,128)(2,1)} %get-tuple-element.67.own_recv, bf16[2,1024,128]{2,1,0:T(8,128)(2,1)} %collective-permute-done.15.add_keep, ...), custom_call_target="tpu_custom_call" | custom-call | tf_op jit(solution)/shard_map/merge/pallas_call | solution.py:380
  204.5 4.5 %all-to-all-start.4 = ((bf16[8,3,256,128]{3,2,1,0:T(8,128)(2,1)}), bf16[8,3,256,128]{3,2,1,0:T(8,128)(2,1)}, u32[]{:S(2)}, u32[]{:S(2)}) async-start(bf16[8,3,256,128]{3,2,1,0:T(8,128)(2,1)} %merge.6), calls=%async_computation.4 | async-start | bytes 3145728 | tf_op jit(solution)/shard_map/all_to_all | solution.py:455
  210.3 5.3 %collective-permute-start.11 = (bf16[2,1024,128]{2,1,0:T(8,128)(2,1)S(1)}, bf16[2,1024,128]{2,1,0:T(8,128)(2,1)}, u32[]{:S(2)}, u32[]{:S(2)}) collective-permute-start(bf16[2,1024,128]{2,1,0:T(8,128)(2,1)S(1)} %copy-done.5), channel_id=1, source_target_pairs={{8,0},{16,8},{4,12},{24,16},{12,20},{20,28},{9,1},{17,9},{5,13},{2... | collective-permute-start | bytes 1572872 | tf_op jit(solution)/shard_map/ppermute | solution.py:447
  215.6 9.5 %collective-permute-done.10.add_keep = bf16[2,1024,128]{2,1,0:T(8,128)(2,1)} collective-permute-done((bf16[2,1024,128]{2,1,0:T(8,128)(2,1)S(1)}, bf16[2,1024,128]{2,1,0:T(8,128)(2,1)}, u32[]{:S(2)}, u32[]{:S(2)}) %collective-permute-start.10) | collective-permute-done | bytes 524320 | tf_op jit(solution)/shard_map/ppermute | solution.py:447
  226.2 3.0 %merge.5 = bf16[8,3,256,128]{3,2,1,0:T(8,128)(2,1)} custom-call(s32[1]{0:T(128)} %bitcast.scalars, bf16[2,1024,128]{2,1,0:T(8,128)(2,1)} %get-tuple-element.57.own_keep, bf16[2,1024,128]{2,1,0:T(8,128)(2,1)} %get-tuple-element.58.own_recv, bf16[2,1024,128]{2,1,0:T(8,128)(2,1)} %collective-permute-done.10.add_keep, ...), custom_call_target="tpu_custom_call" | custom-call | tf_op jit(solution)/shard_map/merge/pallas_call | solution.py:380
  229.9 6.3 %all-to-all-start.3 = ((bf16[8,3,256,128]{3,2,1,0:T(8,128)(2,1)}), bf16[8,3,256,128]{3,2,1,0:T(8,128)(2,1)}, u32[]{:S(2)}, u32[]{:S(2)}) async-start(bf16[8,3,256,128]{3,2,1,0:T(8,128)(2,1)} %merge.5), calls=%async_computation.3 | async-start | bytes 3145728 | tf_op jit(solution)/shard_map/all_to_all | solution.py:455
  237.6 5.3 %collective-permute-start.20 = (bf16[2,1024,128]{2,1,0:T(8,128)(2,1)S(1)}, bf16[2,1024,128]{2,1,0:T(8,128)(2,1)}, u32[]{:S(2)}, u32[]{:S(2)}) collective-permute-start(bf16[2,1024,128]{2,1,0:T(8,128)(2,1)S(1)} %copy-done.9), channel_id=1, source_target_pairs={{8,0},{16,8},{4,12},{24,16},{12,20},{20,28},{9,1},{17,9},{5,13},{2... | collective-permute-start | bytes 1572872 | tf_op jit(solution)/shard_map/ppermute | solution.py:447
  242.9 9.7 %collective-permute-done.19.add_keep = bf16[2,1024,128]{2,1,0:T(8,128)(2,1)} collective-permute-done((bf16[2,1024,128]{2,1,0:T(8,128)(2,1)S(1)}, bf16[2,1024,128]{2,1,0:T(8,128)(2,1)}, u32[]{:S(2)}, u32[]{:S(2)}) %collective-permute-start.19) | collective-permute-done | bytes 524320 | tf_op jit(solution)/shard_map/ppermute | solution.py:447
  253.7 2.7 merge.7
  257.4 5.9 %all-to-all-start.5 = ((bf16[8,2,256,128]{3,2,1,0:T(8,128)(2,1)}), bf16[8,2,256,128]{3,2,1,0:T(8,128)(2,1)}, u32[]{:S(2)}, u32[]{:S(2)}) async-start(bf16[8,2,256,128]{3,2,1,0:T(8,128)(2,1)} %merge.7), calls=%async_computation.5 | async-start | bytes 2097152 | tf_op jit(solution)/shard_map/all_to_all | solution.py:455
  263.3 4.7 %assemble.2 = bf16[256,32,128]{2,1,0:T(8,128)(2,1)} custom-call(bf16[8,4,256,128]{3,2,1,0:T(8,128)(2,1)} %all-to-all-done.1.refs_0_, bf16[8,3,256,128]{3,2,1,0:T(8,128)(2,1)} %all-to-all-done.3.refs_1_, bf16[8,3,256,128]{3,2,1,0:T(8,128)(2,1)} %all-to-all-done.4.refs_2_), custom_call_target="tpu_custom_call" | custom-call | tf_op jit(solution)/shard_map/assemble/pallas_call | solution.py:413
  268.0 10.8 %all-to-all-done.5.refs_3_ = bf16[8,2,256,128]{3,2,1,0:T(8,128)(2,1)} async-done(((bf16[8,2,256,128]{3,2,1,0:T(8,128)(2,1)}), bf16[8,2,256,128]{3,2,1,0:T(8,128)(2,1)}, u32[]{:S(2)}, u32[]{:S(2)}) %all-to-all-start.5) | async-done | bytes 1048608 | tf_op jit(solution)/shard_map/all_to_all | solution.py:455
  278.8 5.5 %assemble.3 = (bf16[256,32,128]{2,1,0:T(8,128)(2,1)}, bf16[256,32,128]{2,1,0:T(8,128)(2,1)}) custom-call(bf16[8,4,256,128]{3,2,1,0:T(8,128)(2,1)} %all-to-all-done.1.refs_0_, bf16[8,3,256,128]{3,2,1,0:T(8,128)(2,1)} %all-to-all-done.3.refs_1_, bf16[8,3,256,128]{3,2,1,0:T(8,128)(2,1)} %all-to-all-done.4.refs_2_, bf16[8,2,256,128]{3,2,1,0:T(8,128)(2,1)} %all-to-all-done.5.refs_3_), custom_call_target="tpu_custom_call" | custom-call | tf_op jit(solution)/shard_map/assemble/pallas_call | solution.py:413
  (70 shorter events, 21.5 us)
Async XLA Ops:
  5.8 18.5 %collective-permute-start.1 = (bf16[2,1024,128]{2,1,0:T(8,128)(2,1)}, bf16[2,1024,128]{2,1,0:T(8,128)(2,1)}, u32[]{:S(2)}, u32[]{:S(2)}) collective-permute-start(bf16[2,1024,128]{2,1,0:T(8,128)(2,1)} %get-tuple-element.44), channel_id=1, source_target_pairs={{0,4},{4,0},{8,12},{12,8},{16,20},{20,16},{24,28},{28,24},{1,5},{5... | collective-permute-start | bytes 1572872 | tf_op jit(solution)/shard_map/ppermute | solution.py:447
  7.4 78.4 %collective-permute-start.9 = (bf16[3,2,1024,128]{3,2,1,0:T(8,128)(2,1)}, bf16[3,2,1024,128]{3,2,1,0:T(8,128)(2,1)}, u32[]{:S(2)}, u32[]{:S(2)}) collective-permute-start(bf16[3,2,1024,128]{3,2,1,0:T(8,128)(2,1)} %get-tuple-element.54.kv_keep), channel_id=1, source_target_pairs={{4,12},{8,0},{12,20},{16,8},{20,28},{24,16},{5,13},{9,1},{13,21},{... | collective-permute-start | bytes 4718600 | tf_op jit(solution)/shard_map/ppermute | solution.py:447
  16.4 7.7 %copy-start.14 = (bf16[1,1024,128]{2,1,0:T(8,128)(2,1)S(1)}, bf16[1,1024,128]{2,1,0:T(8,128)(2,1)}, u32[]{:S(2)}) copy-start(bf16[1,1024,128]{2,1,0:T(8,128)(2,1)} %get-tuple-element.42) | copy-start | bytes 786436
  16.4 9.3 %copy-start = (s32[8]{0:T(128)S(1)}, s32[8]{0:T(128)}, u32[]{:S(2)}) copy-start(s32[8]{0:T(128)} %param.11) | copy-start | bytes 100
  16.4 10.0 %copy-start.1 = (s32[64]{0:T(128)S(1)}, s32[64]{0:T(128)}, u32[]{:S(2)}) copy-start(s32[64]{0:T(128)} %param.10) | copy-start | bytes 772
  16.4 19.9 %all-to-all-start = ((bf16[8,2,256,128]{3,2,1,0:T(8,128)(2,1)}), bf16[8,2,256,128]{3,2,1,0:T(8,128)(2,1)}, u32[]{:S(2)}, u32[]{:S(2)}) async-start(bf16[8,2,256,128]{3,2,1,0:T(8,128)(2,1)} %get-tuple-element.43), calls=%async_computation | async-start | bytes 2097152 | tf_op jit(solution)/shard_map/all_to_all | solution.py:455
  20.8 37.4 %collective-permute-start.7 = (bf16[2,1024,128]{2,1,0:T(8,128)(2,1)S(1)}, bf16[2,1024,128]{2,1,0:T(8,128)(2,1)}, u32[]{:S(2)}, u32[]{:S(2)}) collective-permute-start(bf16[2,1024,128]{2,1,0:T(8,128)(2,1)S(1)} %copy-done.7), channel_id=1, source_target_pairs={{0,4},{4,0},{8,12},{12,8},{16,20},{20,16},{24,28},{28,24},{1,5},{5... | collective-permute-start | bytes 1572872 | tf_op jit(solution)/shard_map/ppermute | solution.py:447
  22.7 36.8 %collective-permute-start.3 = (bf16[1,2,1024,128]{3,2,1,0:T(8,128)(2,1)S(1)}, bf16[1,2,1024,128]{3,2,1,0:T(8,128)(2,1)S(1)}, u32[]{:S(2)}, u32[]{:S(2)}) collective-permute-start(bf16[1,2,1024,128]{3,2,1,0:T(8,128)(2,1)S(1)} %copy-done.4), channel_id=1, source_target_pairs={{4,12},{8,0},{12,20},{16,8},{20,28},{24,16},{5,13},{9,1},{13,21},{... | collective-permute-start | bytes 1572872 | tf_op jit(solution)/shard_map/ppermute | solution.py:447
  24.0 34.1 %collective-permute-start = (bf16[1,1024,128]{2,1,0:T(8,128)(2,1)S(1)}, bf16[1,1024,128]{2,1,0:T(8,128)(2,1)S(1)}, u32[]{:S(2)}, u32[]{:S(2)}) collective-permute-start(bf16[1,1024,128]{2,1,0:T(8,128)(2,1)S(1)} %copy-done.14), channel_id=1, source_target_pairs={{0,4},{4,0},{8,12},{12,8},{16,20},{20,16},{24,28},{28,24},{1,5},{5... | collective-permute-start | bytes 786440 | tf_op jit(solution)/shard_map/ppermute | solution.py:447
  24.3 36.0 %collective-permute-start.2 = (bf16[2,1024,128]{2,1,0:T(8,128)(2,1)}, bf16[2,1024,128]{2,1,0:T(8,128)(2,1)S(1)}, u32[]{:S(2)}, u32[]{:S(2)}) collective-permute-start(bf16[2,1024,128]{2,1,0:T(8,128)(2,1)} %collective-permute-done.1.kv_recv), channel_id=1, source_target_pairs={{0,8},{8,16},{12,4},{16,24},{20,12},{28,20},{1,9},{9,17},{13,5},{1... | collective-permute-start | bytes 1572872 | tf_op jit(solution)/shard_map/ppermute | solution.py:447
  36.3 70.3 %all-to-all-start.2 = ((bf16[8,2,256,128]{3,2,1,0:T(8,128)(2,1)}), bf16[8,2,256,128]{3,2,1,0:T(8,128)(2,1)}, u32[]{:S(2)}, u32[]{:S(2)}) async-start(bf16[8,2,256,128]{3,2,1,0:T(8,128)(2,1)} %get-tuple-element.62), calls=%async_computation.2 | async-start | bytes 2097152 | tf_op jit(solution)/shard_map/all_to_all | solution.py:455
  58.2 27.6 %collective-permute-start.6 = (bf16[1,1024,128]{2,1,0:T(8,128)(2,1)}, bf16[1,1024,128]{2,1,0:T(8,128)(2,1)}, u32[]{:S(2)}, u32[]{:S(2)}) collective-permute-start(bf16[1,1024,128]{2,1,0:T(8,128)(2,1)} %get-tuple-element.52), channel_id=1, source_target_pairs={{0,4},{4,0},{8,12},{12,8},{16,20},{20,16},{24,28},{28,24},{1,5},{5... | collective-permute-start | bytes 786440 | tf_op jit(solution)/shard_map/ppermute | solution.py:447
  58.2 27.6 %collective-permute-start.8 = (bf16[2,1024,128]{2,1,0:T(8,128)(2,1)}, bf16[2,1024,128]{2,1,0:T(8,128)(2,1)}, u32[]{:S(2)}, u32[]{:S(2)}) collective-permute-start(bf16[2,1024,128]{2,1,0:T(8,128)(2,1)} %collective-permute-done.7.kv_recv), channel_id=1, source_target_pairs={{0,8},{8,16},{12,4},{16,24},{20,12},{28,20},{1,9},{9,17},{13,5},{1... | collective-permute-start | bytes 1572872 | tf_op jit(solution)/shard_map/ppermute | solution.py:447
  78.5 24.7 %collective-permute-start.4 = (bf16[2,1024,128]{2,1,0:T(8,128)(2,1)}, bf16[2,1024,128]{2,1,0:T(8,128)(2,1)}, u32[]{:S(2)}, u32[]{:S(2)}) collective-permute-start(bf16[2,1024,128]{2,1,0:T(8,128)(2,1)} %get-tuple-element.48), channel_id=1, source_target_pairs={{12,4},{0,8},{20,12},{8,16},{28,20},{16,24},{13,5},{1,9},{21,13},{... | collective-permute-start | bytes 1572872 | tf_op jit(solution)/shard_map/ppermute | solution.py:447
  79.8 23.4 %collective-permute-start.5 = (bf16[2,1024,128]{2,1,0:T(8,128)(2,1)}, bf16[2,1024,128]{2,1,0:T(8,128)(2,1)}, u32[]{:S(2)}, u32[]{:S(2)}) collective-permute-start(bf16[2,1024,128]{2,1,0:T(8,128)(2,1)} %get-tuple-element.49), channel_id=1, source_target_pairs={{8,0},{16,8},{4,12},{24,16},{12,20},{20,28},{9,1},{17,9},{5,13},{2... | collective-permute-start | bytes 1572872 | tf_op jit(solution)/shard_map/ppermute | solution.py:447
  85.8 27.5 %collective-permute-start.13 = (bf16[2,1024,128]{2,1,0:T(8,128)(2,1)}, bf16[2,1024,128]{2,1,0:T(8,128)(2,1)}, u32[]{:S(2)}, u32[]{:S(2)}) collective-permute-start(bf16[2,1024,128]{2,1,0:T(8,128)(2,1)} %get-tuple-element.63), channel_id=1, source_target_pairs={{0,4},{4,0},{8,12},{12,8},{16,20},{20,16},{24,28},{28,24},{1,5},{5... | collective-permute-start | bytes 1572872 | tf_op jit(solution)/shard_map/ppermute | solution.py:447
  106.6 97.9 %all-to-all-start.1 = ((bf16[8,4,256,128]{3,2,1,0:T(8,128)(2,1)}), bf16[8,4,256,128]{3,2,1,0:T(8,128)(2,1)}, u32[]{:S(2)}, u32[]{:S(2)}) async-start(bf16[8,4,256,128]{3,2,1,0:T(8,128)(2,1)} %merge.4), calls=%async_computation.1 | async-start | bytes 4194304 | tf_op jit(solution)/shard_map/all_to_all | solution.py:455
  111.1 37.5 %collective-permute-start.17 = (bf16[2,1024,128]{2,1,0:T(8,128)(2,1)S(1)}, bf16[2,1024,128]{2,1,0:T(8,128)(2,1)}, u32[]{:S(2)}, u32[]{:S(2)}) collective-permute-start(bf16[2,1024,128]{2,1,0:T(8,128)(2,1)S(1)} %copy-done.2), channel_id=1, source_target_pairs={{0,4},{4,0},{8,12},{12,8},{16,20},{20,16},{24,28},{28,24},{1,5},{5... | collective-permute-start | bytes 1572872 | tf_op jit(solution)/shard_map/ppermute | solution.py:447
  113.2 46.0 %collective-permute-start.12 = (bf16[2,1024,128]{2,1,0:T(8,128)(2,1)S(1)}, bf16[2,1024,128]{2,1,0:T(8,128)(2,1)S(1)}, u32[]{:S(2)}, u32[]{:S(2)}) collective-permute-start(bf16[2,1024,128]{2,1,0:T(8,128)(2,1)S(1)} %copy-done.3), channel_id=1, source_target_pairs={{0,4},{4,0},{8,12},{12,8},{16,20},{20,16},{24,28},{28,24},{1,5},{5... | collective-permute-start | bytes 1572872 | tf_op jit(solution)/shard_map/ppermute | solution.py:447
  113.3 46.7 %collective-permute-start.14 = (bf16[2,1024,128]{2,1,0:T(8,128)(2,1)}, bf16[2,1024,128]{2,1,0:T(8,128)(2,1)}, u32[]{:S(2)}, u32[]{:S(2)}) collective-permute-start(bf16[2,1024,128]{2,1,0:T(8,128)(2,1)} %collective-permute-done.13.kv_recv), channel_id=1, source_target_pairs={{0,8},{8,16},{12,4},{16,24},{20,12},{28,20},{1,9},{9,17},{13,5},{1... | collective-permute-start | bytes 1572872 | tf_op jit(solution)/shard_map/ppermute | solution.py:447
  148.6 35.4 %collective-permute-start.18 = (bf16[2,1024,128]{2,1,0:T(8,128)(2,1)}, bf16[2,1024,128]{2,1,0:T(8,128)(2,1)}, u32[]{:S(2)}, u32[]{:S(2)}) collective-permute-start(bf16[2,1024,128]{2,1,0:T(8,128)(2,1)} %collective-permute-done.17.kv_recv), channel_id=1, source_target_pairs={{0,8},{8,16},{12,4},{16,24},{20,12},{28,20},{1,9},{9,17},{13,5},{1... | collective-permute-start | bytes 1572872 | tf_op jit(solution)/shard_map/ppermute | solution.py:447
  177.3 24.1 %collective-permute-start.15 = (bf16[2,1024,128]{2,1,0:T(8,128)(2,1)}, bf16[2,1024,128]{2,1,0:T(8,128)(2,1)}, u32[]{:S(2)}, u32[]{:S(2)}) collective-permute-start(bf16[2,1024,128]{2,1,0:T(8,128)(2,1)} %get-tuple-element.68), channel_id=1, source_target_pairs={{12,4},{0,8},{20,12},{8,16},{28,20},{16,24},{13,5},{1,9},{21,13},{... | collective-permute-start | bytes 1572872 | tf_op jit(solution)/shard_map/ppermute | solution.py:447
  178.6 22.8 %collective-permute-start.16 = (bf16[2,1024,128]{2,1,0:T(8,128)(2,1)}, bf16[2,1024,128]{2,1,0:T(8,128)(2,1)}, u32[]{:S(2)}, u32[]{:S(2)}) collective-permute-start(bf16[2,1024,128]{2,1,0:T(8,128)(2,1)} %get-tuple-element.69), channel_id=1, source_target_pairs={{8,0},{16,8},{4,12},{24,16},{12,20},{20,28},{9,1},{17,9},{5,13},{2... | collective-permute-start | bytes 1572872 | tf_op jit(solution)/shard_map/ppermute | solution.py:447
  204.5 25.5 %all-to-all-start.4 = ((bf16[8,3,256,128]{3,2,1,0:T(8,128)(2,1)}), bf16[8,3,256,128]{3,2,1,0:T(8,128)(2,1)}, u32[]{:S(2)}, u32[]{:S(2)}) async-start(bf16[8,3,256,128]{3,2,1,0:T(8,128)(2,1)} %merge.6), calls=%async_computation.4 | async-start | bytes 3145728 | tf_op jit(solution)/shard_map/all_to_all | solution.py:455
  208.9 16.2 %collective-permute-start.10 = (bf16[2,1024,128]{2,1,0:T(8,128)(2,1)S(1)}, bf16[2,1024,128]{2,1,0:T(8,128)(2,1)}, u32[]{:S(2)}, u32[]{:S(2)}) collective-permute-start(bf16[2,1024,128]{2,1,0:T(8,128)(2,1)S(1)} %copy-done.6), channel_id=1, source_target_pairs={{12,4},{0,8},{20,12},{8,16},{28,20},{16,24},{13,5},{1,9},{21,13},{... | collective-permute-start | bytes 1572872 | tf_op jit(solution)/shard_map/ppermute | solution.py:447
  210.3 16.0 %collective-permute-start.11 = (bf16[2,1024,128]{2,1,0:T(8,128)(2,1)S(1)}, bf16[2,1024,128]{2,1,0:T(8,128)(2,1)}, u32[]{:S(2)}, u32[]{:S(2)}) collective-permute-start(bf16[2,1024,128]{2,1,0:T(8,128)(2,1)S(1)} %copy-done.5), channel_id=1, source_target_pairs={{8,0},{16,8},{4,12},{24,16},{12,20},{20,28},{9,1},{17,9},{5,13},{2... | collective-permute-start | bytes 1572872 | tf_op jit(solution)/shard_map/ppermute | solution.py:447
  229.3 7.0 %copy-start.11 = (bf16[2,1024,128]{2,1,0:T(8,128)(2,1)S(1)}, bf16[2,1024,128]{2,1,0:T(8,128)(2,1)}, u32[]{:S(2)}) copy-start(bf16[2,1024,128]{2,1,0:T(8,128)(2,1)} %get-tuple-element.75) | copy-start | bytes 1572868
  229.3 8.3 %copy-start.9 = (bf16[2,1024,128]{2,1,0:T(8,128)(2,1)S(1)}, bf16[2,1024,128]{2,1,0:T(8,128)(2,1)}, u32[]{:S(2)}) copy-start(bf16[2,1024,128]{2,1,0:T(8,128)(2,1)} %get-tuple-element.76) | copy-start | bytes 1572868
  229.9 27.4 %all-to-all-start.3 = ((bf16[8,3,256,128]{3,2,1,0:T(8,128)(2,1)}), bf16[8,3,256,128]{3,2,1,0:T(8,128)(2,1)}, u32[]{:S(2)}, u32[]{:S(2)}) async-start(bf16[8,3,256,128]{3,2,1,0:T(8,128)(2,1)} %merge.5), calls=%async_computation.3 | async-start | bytes 3145728 | tf_op jit(solution)/shard_map/all_to_all | solution.py:455
  236.3 16.3 %collective-permute-start.19 = (bf16[2,1024,128]{2,1,0:T(8,128)(2,1)S(1)}, bf16[2,1024,128]{2,1,0:T(8,128)(2,1)}, u32[]{:S(2)}, u32[]{:S(2)}) collective-permute-start(bf16[2,1024,128]{2,1,0:T(8,128)(2,1)S(1)} %copy-done.11), channel_id=1, source_target_pairs={{12,4},{0,8},{20,12},{8,16},{28,20},{16,24},{13,5},{1,9},{21,13},{... | collective-permute-start | bytes 1572872 | tf_op jit(solution)/shard_map/ppermute | solution.py:447
  237.6 16.1 %collective-permute-start.20 = (bf16[2,1024,128]{2,1,0:T(8,128)(2,1)S(1)}, bf16[2,1024,128]{2,1,0:T(8,128)(2,1)}, u32[]{:S(2)}, u32[]{:S(2)}) collective-permute-start(bf16[2,1024,128]{2,1,0:T(8,128)(2,1)S(1)} %copy-done.9), channel_id=1, source_target_pairs={{8,0},{16,8},{4,12},{24,16},{12,20},{20,28},{9,1},{17,9},{5,13},{2... | collective-permute-start | bytes 1572872 | tf_op jit(solution)/shard_map/ppermute | solution.py:447
  257.4 21.4 %all-to-all-start.5 = ((bf16[8,2,256,128]{3,2,1,0:T(8,128)(2,1)}), bf16[8,2,256,128]{3,2,1,0:T(8,128)(2,1)}, u32[]{:S(2)}, u32[]{:S(2)}) async-start(bf16[8,2,256,128]{3,2,1,0:T(8,128)(2,1)} %merge.7), calls=%async_computation.5 | async-start | bytes 2097152 | tf_op jit(solution)/shard_map/all_to_all | solution.py:455
  (10 other events, 36.7 us)
